TPU v7x, 256 devices: a whole 4x4x8 slice. The times are simulated.
256 devices in a mesh: ctx: 64 (over z, x, core), head: 4 (over y).
Axes of the slice: x: 4, y: 4, z: 8, core: 2. Of those that a mesh axis runs over, the one named last changes fastest.
Arguments:
- queries: bfloat16 [16384, 4096], P('ctx', 'head'), may hold values from -6 to 6
- keys: bfloat16 [16384, 2, 4096], P('ctx', None, 'head'), may hold values from -6 to 6
- values: bfloat16 [16384, 2, 4096], P('ctx', None, 'head'), may hold values from -6 to 6
- betas: float32 [2, 32, 16384], P(None, 'head', 'ctx'), may hold values from 0.02 to 1.9
- log_decay: float32 [32, 16384], P('head', 'ctx'), may hold values from -1 to 0
- segment: int32 [16384], P('ctx'), may hold values from 0 to 127, never falling along the last dimension, each value on 1 to 2048 neighbouring positions
- gain: float32 [4096], P('head'), may hold values from 0.1 to 1.9
- out_weight: bfloat16 [4096, 4096], P('head'), may hold values from -0.125 to 0.125
Outputs:
- mixed: bfloat16 [16384, 4096], P('ctx', 'head')
Inputs may be any that keep to these rules, and one draw needn't show every extreme that they name: `segment`: document numbers never fall along the context; every document has 1 to 2048 tokens and one has exactly 2048.
All inputs are finite; a program needn't handle non-finite values.
Results may differ from a plain program's by a relative error of at most 0.0049.
Values sent between devices are 32-bit elements; how exact they have to be, the bound alone decides.
No kernel may reach another device: no remote copies, remote signals or barrier semaphores. Data moves between devices by JAX's collectives and lax.ppermute only.
A program may use at most 192 MiB of HBM per device.

v0:
```python
import jax
import jax.numpy as jnp
from jax import lax
from jax.sharding import PartitionSpec as P

DK = 128
DV = 128
GROUP = 64


HIGHEST = lax.Precision.HIGHEST


def shifted(value, axis, steps):
    count = lax.axis_size(axis)
    initial, last = (max(0, -steps), min(count, count - steps))
    return lax.ppermute(value, axis, [(source, source + steps) for source in range(initial, last)])


def entering(value, axis, join, neutral):
    count, mine = (lax.axis_size(axis), lax.axis_index(axis))
    pieces = jax.tree.map(lambda part: lax.all_gather(part, axis), value)
    subtotal = jax.tree.map(
        lambda part, zero: jnp.full_like(part, 0) + jnp.asarray(zero, part.dtype), value, neutral
    )

    def turn(position, subtotal):
        longer = join(subtotal, jax.tree.map(lambda part: part[position], pieces))
        return jax.tree.map(lambda new, old: jnp.where(position < mine, new, old), longer, subtotal)

    return lax.fori_loop(0, count - 1, turn, subtotal)


def unit_rows(matrix):
    return matrix / jnp.sqrt(jnp.sum(matrix * matrix, axis=-1, keepdims=True) + 1e-06)


def combine_pairs(earlier, later):
    joined_map = jnp.einsum("hab,hbc->hac", earlier[0], later[0], precision=HIGHEST)
    joined_add = jnp.einsum("hab,hbc->hac", earlier[1], later[0], precision=HIGHEST) + later[1]
    return (joined_map, joined_add)


def shards(queries, keys, values, betas, log_decay, segment, gain, out_weight):
    tok_local = queries.shape[0]
    heads_local = betas.shape[1]
    blocks = tok_local // GROUP
    rows = 2 * GROUP
    query_unit = unit_rows(queries.astype(jnp.float32).reshape(blocks, GROUP, heads_local, DK))
    query_unit = jnp.transpose(query_unit, (2, 0, 1, 3))
    key_unit = unit_rows(keys.astype(jnp.float32).reshape(blocks, rows, heads_local, DK))
    key_unit = jnp.transpose(key_unit, (2, 0, 1, 3))
    value_rows = jnp.transpose(
        values.astype(jnp.float32).reshape(blocks, rows, heads_local, DV), (2, 0, 1, 3)
    )
    strengths = jnp.transpose(betas.reshape(2, heads_local, blocks, GROUP), (1, 2, 3, 0)).reshape(
        heads_local, blocks, rows
    )
    token_log = log_decay.reshape(heads_local, blocks, GROUP)
    step_log = jnp.stack([token_log, jnp.zeros_like(token_log)], axis=-1).reshape(
        heads_local, blocks, rows
    )
    cumulative = jnp.cumsum(step_log, axis=-1)
    penultimate_state = shifted(segment[tok_local - 1 :], "ctx", 1)
    seg_blocks = segment.reshape(blocks, GROUP)
    row_seg = jnp.repeat(seg_blocks, 2, axis=1)
    group_prior = jnp.concatenate([penultimate_state, seg_blocks[:-1, GROUP - 1]])
    position = jnp.arange(rows)
    causal = position[:, None] >= position[None, :]
    strictly = position[:, None] > position[None, :]
    same_doc = row_seg[:, :, None] == row_seg[:, None, :]
    linked = same_doc & causal[None, :, :]
    earlier_link = same_doc & strictly[None, :, :]
    spread_log = cumulative[..., :, None] - cumulative[..., None, :]
    within = jnp.where(linked[None], jnp.exp(jnp.where(linked[None], spread_log, 0.0)), 0.0)
    entry = jnp.where((row_seg == group_prior[:, None])[None], jnp.exp(cumulative), 0.0)
    intersections = jnp.einsum("hnrd,hnsd->hnrs", key_unit, key_unit, precision=HIGHEST)
    lower_part = jnp.where(
        earlier_link[None], strengths[..., :, None] * within * intersections, 0.0
    )
    system = lower_part + jnp.eye(rows, dtype=jnp.float32)
    right_side = jnp.concatenate(
        [strengths[..., None] * value_rows, (strengths * entry)[..., None] * key_unit], axis=-1
    )
    solved = lax.linalg.triangular_solve(
        system, right_side, left_side=True, lower=True, unit_diagonal=True
    )
    pseudo = solved[..., :DV]
    key_mix = solved[..., DV:]
    within_query = within[:, :, 1::2, :]
    entry_query = entry[:, :, 1::2]
    scores = jnp.einsum("hnid,hnsd->hnis", query_unit, key_unit, precision=HIGHEST) * within_query
    local_out = jnp.einsum("hnis,hnsv->hniv", scores, pseudo, precision=HIGHEST)
    reach = entry_query[..., None] * query_unit - jnp.einsum(
        "hnis,hnsd->hnid", scores, key_mix, precision=HIGHEST
    )
    tail = within[:, :, rows - 1, :]
    tail_entry = entry[:, :, rows - 1]
    transition = tail_entry[..., None, None] * jnp.eye(DK, dtype=jnp.float32) - jnp.einsum(
        "hnsa,hnsb->hnab", key_mix * tail[..., None], key_unit, precision=HIGHEST
    )
    addition = jnp.einsum("hnsv,hnsb->hnvb", pseudo * tail[..., None], key_unit, precision=HIGHEST)

    def compose(running, block_pair):
        block_map, block_add = block_pair
        next_map = jnp.einsum("hab,hbc->hac", running[0], block_map, precision=HIGHEST)
        next_add = jnp.einsum("hvb,hbc->hvc", running[1], block_map, precision=HIGHEST) + block_add
        return ((next_map, next_add), running)

    identity_map = jnp.broadcast_to(jnp.eye(DK, dtype=jnp.float32), (heads_local, DK, DK))
    empty_state = jnp.zeros((heads_local, DV, DK), jnp.float32)
    device_pair, prefixes = lax.scan(
        compose,
        (identity_map, empty_state),
        (jnp.moveaxis(transition, 1, 0), jnp.moveaxis(addition, 1, 0)),
    )
    prefix_map = jnp.moveaxis(prefixes[0], 0, 1)
    prefix_add = jnp.moveaxis(prefixes[1], 0, 1)
    mapped = jnp.einsum("hnik,hnak->hnia", reach, prefix_map, precision=HIGHEST)
    local_out = local_out + jnp.einsum("hnik,hnvk->hniv", reach, prefix_add, precision=HIGHEST)
    prior = entering(
        (device_pair[0], device_pair[1]), "ctx", combine_pairs, (identity_map, empty_state)
    )
    incoming = prior[1]
    attended = local_out + jnp.einsum("hnia,hva->hniv", mapped, incoming, precision=HIGHEST)
    attended = jnp.transpose(attended, (1, 2, 0, 3)).reshape(tok_local, heads_local, DV)
    inverse_rms = 1.0 / jnp.sqrt(jnp.mean(attended * attended, axis=-1, keepdims=True) + 1e-06)
    normed = ((attended * inverse_rms).reshape(tok_local, heads_local * DV) * gain[None, :]).astype(
        jnp.bfloat16
    )
    terms = jnp.dot(normed, out_weight, preferred_element_type=jnp.float32)
    return lax.psum_scatter(terms, "head", scatter_dimension=1, tiled=True).astype(jnp.bfloat16)


def solution(mesh):
    return jax.shard_map(
        shards,
        mesh=mesh,
        in_specs=(
            P("ctx", "head"),
            P("ctx", None, "head"),
            P("ctx", None, "head"),
            P(None, "head", "ctx"),
            P("head", "ctx"),
            P("ctx"),
            P("head"),
            P("head", None),
        ),
        out_specs=P("ctx", "head"),
        check_vma=False,
    )
```

profile of v0, /device:TPU:128, one launch (start us, length us, event | category | flops | bytes accessed | tf_op | source)
XLA Modules:
  0.0 956.1 jit_solution(3891058948972943255)
XLA Ops:
  18.6 6.6 add_bitcast_fusion
  25.2 315.8 %custom-call.3 = f32[8,4,1,128,128]{3,4,2,1,0:T(8,128)} custom-call(f32[8,4,1,128,128]{4,3,2,1,0:T(8,128)} %add_bitcast_fusion), custom_call_target="InvertDiagBlocksLowerTriangular" | custom-call | tf_op jit(solution)/shard_map/triangular_solve | solution.py:85
  341.9 2.6 reshape.150
  345.7 3.7 bitcast_multiply_fusion
  349.5 3.8 fusion.20
  353.3 6.1 fusion.47
  359.4 6.2 bitcast_subtract_fusion
  365.6 21.7 %while.31 = (s32[]{:T(128)}, f32[8,128,128]{1,2,0:T(8,128)S(1)}, f32[8,128,128]{1,2,0:T(8,128)S(1)}, f32[4,8,128,128]{2,3,1,0:T(8,128)}, f32[4,8,128,128]{2,3,1,...) while((s32[]{:T(128)}, f32[8,128,128]{1,2,0:T(8,128)S(1)}, ...), condition=%wide.region_4.5_spmd.clone, body=%wide.region_3.4_spmd.clone.sunk | while | flops 403046400 | bytes 18350236 | solution.py:112
  389.5 2.8 slice.28
  394.4 7.0 fusion.62
  401.8 4.9 fusion.59
  406.7 2.1 fusion.26
  408.8 3.1 fusion.24
  411.9 2.3 fusion.56
  414.2 115.5 %all-gather.5.cloned.1.call-done = f32[512,128,128]{2,1,0:T(8,128)} async-done(((f32[8,128,128]{2,1,0:T(8,128)}), f32[512,128,128]{2,1,0:T(8,128)}) %all-gather.5.cloned.1.call-update) | async-done | bytes 33554448 | tf_op jit(solution)/shard_map/all_gather | solution.py:22
  529.7 141.4 %all-gather.7.cloned.1.call-done = f32[512,128,128]{2,1,0:T(8,128)} async-done(((f32[8,128,128]{2,1,0:T(8,128)}), f32[512,128,128]{2,1,0:T(8,128)}) %all-gather.7.cloned.1.call-update) | async-done | bytes 33554448 | tf_op jit(solution)/shard_map/all_gather | solution.py:22
  671.1 215.5 %while.32 = (s32[]{:T(128)}, f32[8,128,128]{1,2,0:T(8,128)S(1)}, s32[]{:T(128)}, f32[64,8,128,128]{3,2,1,0:T(8,128)}, f32[64,8,128,128]{3,2,1,0:T(8,128)}, /*index=5*/s32[]{:T(128)}, s32[]{:T(128)}) while((s32[]{:T(128)}, f32[8,128,128]{1,2,0:T(8,128)S(1)}, s32[]{:T(128)}, f32[64,8,128,128]{3,2,1,0:T(8,128)}, ...), condition=%wide.region_6.7_spmd.clone, body=%wide.region_5.6_spmd.clone.sunk | while | flops 201850880 | bytes 5769323 | solution.py:31
  672.4 2.1 fusion.105
  682.7 2.1 fusion.105
  686.1 2.1 fusion.105
  693.0 2.1 fusion.105
  696.4 2.1 fusion.105
  706.7 2.1 fusion.105
  710.1 2.1 fusion.105
  716.9 2.1 fusion.105
  720.3 2.1 fusion.105
  730.6 2.1 fusion.105
  734.0 2.1 fusion.105
  740.9 2.1 fusion.105
  744.3 2.1 fusion.105
  754.6 2.1 fusion.105
  758.0 2.1 fusion.105
  764.8 2.1 fusion.105
  768.2 2.1 fusion.105
  778.5 2.1 fusion.105
  788.8 2.1 fusion.105
  792.2 2.1 fusion.105
  802.5 2.1 fusion.105
  805.9 2.1 fusion.105
  840.1 2.1 fusion.105
  860.6 2.1 fusion.105
  864.0 2.1 fusion.105
  874.3 2.1 fusion.105
  877.7 2.1 fusion.105
  886.6 2.5 multiply_reduce_fusion.1
  890.2 7.8 fusion.71
  898.1 49.4 %reduce-scatter.2.cloned.1.call-done = f32[256,1024]{1,0:T(8,128)} async-done(((f32[256,4096]{1,0:T(8,128)}), f32[256,1024]{1,0:T(8,128)}) %reduce-scatter.2.cloned.1.call-update) | async-done | bytes 1048592 | tf_op jit(solution)/shard_map/reduce_scatter | solution.py:132
  947.5 2.1 convert_element_type.24
  (346 shorter events, 197.9 us)
Async XLA Ops:
  6.5 523.2 %all-gather.5.cloned.1.call-start = ((), (), s32[]{:S(2)}) async-start(), calls=%async_computation.2 | async-start | bytes 34078720 | tf_op jit(solution)/shard_map/all_gather | solution.py:22
  7.8 336.8 %collective-permute-start = (s32[1]{0:T(128)}, s32[1]{0:T(128)}, u32[]{:S(2)}, u32[]{:S(2)}) collective-permute-start(s32[1]{0:T(128)} %slice.29), channel_id=1, source_target_pairs={{0,4},{4,8},{8,12},{12,16},{16,20},{20,24},{24,28},{28,32},{32,36}... | collective-permute-start | bytes 20 | tf_op jit(solution)/shard_map/ppermute | solution.py:17
  16.0 343.4 %copy-start = (f32[4,128,8,128]{3,2,1,0:T(8,128)}, f32[4,128,8,128]{3,2,1,0:T(8,128)S(1)}, u32[]{:S(2)}) copy-start(f32[4,128,8,128]{3,2,1,0:T(8,128)S(1)} %reshape.149) | copy-start | bytes 6291460
  345.7 3.7 copy-start.8
  353.3 6.2 copy-start.2
  367.0 2.0 copy-start.4
  372.5 2.0 copy-start.4
  377.9 2.0 copy-start.4
  383.3 2.0 copy-start.4
  387.3 2.2 copy-start.6
  388.3 4.0 copy-start.11
  388.4 282.8 %all-gather.7.cloned.1.call-start = ((), (), s32[]{:S(2)}) async-start(), calls=%async_computation.3 | async-start | bytes 34078720 | tf_op jit(solution)/shard_map/all_gather | solution.py:22
  389.5 558.0 %reduce-scatter.2.cloned.1.call-start = ((), (), s32[]{:S(2)}) async-start(), calls=%async_computation.1 | async-start | bytes 5242880 | tf_op jit(solution)/shard_map/reduce_scatter | solution.py:132
  392.5 2.0 copy-start.1
  392.7 1.0 copy-start.5
  401.8 4.9 copy-start.9
  406.7 2.1 copy-start.10
  406.7 5.2 copy-start.7
  408.8 3.1 copy-start.3
  889.2 1.1 copy-start.12
Sparse Core Ops, SparseCore 0:
  388.5 141.2 all-gather.4
  532.5 138.5 all-gather.6
  898.2 49.2 reduce-scatter.1
where the time goes:
time: 965 us; the launch traced here: 956 us
  other arithmetic  331 us (34%)
  waiting for transfers between devices  306 us (32%)
  matrix products  190 us (20%)
  local copies, waits for them, and re-layouts  110 us (11%)
  between operations  13.5 us (1%)
    another operation x4, other arithmetic, shards(): lax.linalg.triangular_solve(system, right_side, left_side=True, lower=Tru...  316 us
    all_gather x2, waiting for transfers between devices, entering(): pieces = jax.tree.map(lambda part: lax.all_gather(part, axis), value)  257 us
    dot_general x63, matrix products, combine_pairs(): jnp.einsum('hab,hbc->hac', earlier[1], later[0], precision=HIGHEST)  130 us
    dynamic_slice x126, local copies, waits for them, and re-layouts, turn(): longer = join(subtotal, jax.tree.map(lambda part: part[position], pieces))  80.6 us
    reduce_scatter x1, waiting for transfers between devices, shards(): lax.psum_scatter(terms, 'head', scatter_dimension=1, tiled=True)  49.4 us
  transfers between devices with their start and end apart: 4, of which 3 were waited for; matrix products, arithmetic and copies ran while one was open for 38% of the time, Pallas kernels for 0%

commit v1 on v0

v1 whole, which is shorter than its diff:
```python
import jax
import jax.numpy as jnp
from jax import lax
from jax.experimental import pallas as pl
from jax.experimental.pallas import tpu as pltpu
from jax.sharding import PartitionSpec as P

DK = 128
DV = 128
GROUP = 64
ROWS = 2 * GROUP
DOCUMENT_LIMIT = 2048
EPS = 1e-06
F32 = jnp.float32
BF16 = jnp.bfloat16


def dotf(a, b, dims=(((1,), (0,)), ((), ()))):
    return lax.dot_general(a, b, dims, preferred_element_type=F32)


def halves(x):
    hi = x.astype(BF16)
    lo = (x - hi.astype(F32)).astype(BF16)
    return hi, lo


def side(x):
    return jnp.concatenate(halves(x), axis=1)


def mm(a, b):
    left = side(a)
    outs = []
    for c in range(0, b.shape[1], 128):
        right = side(b[:, c : c + 128])
        r = dotf(left, jnp.concatenate([right, right], axis=0))
        outs.append(r[:, :128] + r[:, 128:])
    return outs[0] if len(outs) == 1 else jnp.concatenate(outs, axis=1)


def mm_exact_right(a, b16):
    return dotf(side(a), jnp.concatenate([b16, b16], axis=0))


def iota(shape, dim):
    return lax.broadcasted_iota(jnp.int32, shape, dim)


def invert(systems):
    r, c = iota((ROWS, ROWS), 0), iota((ROWS, ROWS), 1)
    eye = (r == c).astype(F32)
    pair = (r >> 1) == (c >> 1)
    xs = [eye - jnp.where(pair, s, 0.0) for s in systems]
    shift = 1
    while (1 << shift) < ROWS:
        band = ((r >> (shift + 1)) == (c >> (shift + 1))) & ((r >> shift) != (c >> shift))
        ys = [mm(jnp.where(band, s, 0.0), x) for s, x in zip(systems, xs)]
        xs = [x - mm(x, y) for x, y in zip(xs, ys)]
        shift += 1
    return xs


def local_kernel(heads_step, blocks, q_ref, k_ref, v_ref, beta_ref, log_ref, seg_ref,
                 pair_ref, out_ref, map_ref, tab_ref):
    step = pl.program_id(0)
    heads = log_ref.shape[0]

    @pl.when(step == 0)
    def _():
        t, s = iota((GROUP, ROWS), 0), iota((GROUP, ROWS), 1)
        even = (s == 2 * t).astype(F32)
        odd = (s == 2 * t + 1).astype(F32)
        upto = (t <= (s >> 1)).astype(F32)
        flat = (t <= s).astype(F32)
        same = (s == t).astype(F32)
        both = even + odd

        def pick(x, sel):
            return lax.dot_general(x, sel, (((1,), (0,)), ((), ())),
                                   precision=lax.Precision.HIGHEST, preferred_element_type=F32)

        seg = jnp.broadcast_to(seg_ref[...].astype(F32), (heads, blocks * GROUP))
        for n in range(blocks):
            cut = slice(n * GROUP, (n + 1) * GROUP)
            lg = log_ref[:, cut]
            tab_ref[:, 8 * n, :] = pick(lg, upto)
            tab_ref[:, 8 * n + 1, :] = pick(beta_ref[0, :, cut], even) + pick(beta_ref[1, :, cut], odd)
            tab_ref[:, 8 * n + 2, :] = pick(seg[:, cut], both)
            tab_ref[:, 8 * n + 3, :] = pick(lg, flat)
            tab_ref[:, 8 * n + 4, :] = pick(seg[:, cut], same)
            for z in range(5, 8):
                tab_ref[:, 8 * n + z, :] = jnp.zeros((heads, ROWS), F32)

    r, c = iota((ROWS, ROWS), 0), iota((ROWS, ROWS), 1)
    diag = r == c
    eye = diag.astype(F32)
    strictly = r > c
    qr, qc = iota((GROUP, ROWS), 0), iota((GROUP, ROWS), 1)
    seen = qc <= 2 * qr + 1

    items = []
    for g in range(heads_step):
        lanes = slice(g * DK, (g + 1) * DK)
        table = tab_ref[step * heads_step + g]
        columns = jnp.concatenate([table[8 * n : 8 * n + 8] for n in range(blocks)]
                                  + [jnp.zeros((ROWS - 8 * blocks, ROWS), F32)], axis=0).T
        prior = table[2:3, 0:1]
        for n in range(blocks):
            key = k_ref[n * ROWS : (n + 1) * ROWS, lanes]
            query = q_ref[n * GROUP : (n + 1) * GROUP, lanes]
            value = v_ref[n * ROWS : (n + 1) * ROWS, lanes]
            cum_row, beta_row, seg_row = (table[8 * n + i : 8 * n + i + 1] for i in range(3))
            cum_col, beta_col, seg_col = (columns[:, 8 * n + i : 8 * n + i + 1] for i in range(3))
            cum_q, seg_q = (columns[:GROUP, 8 * n + i : 8 * n + i + 1] for i in (3, 4))
            cum_last, seg_last = cum_row[:, ROWS - 1 :], seg_row[:, ROWS - 1 :]
            gram = dotf(jnp.concatenate([key, query], axis=0), key, (((1,), (1,)), ((), ())))
            raw, raw_q = gram[:ROWS], gram[ROWS:]
            own = jnp.where(diag, raw, 0.0)
            rk_row = lax.rsqrt(jnp.sum(own, axis=0, keepdims=True) + EPS)
            rk_col = lax.rsqrt(jnp.sum(own, axis=1, keepdims=True) + EPS)
            query32 = query.astype(F32)
            rq = lax.rsqrt(jnp.sum(query32 * query32, axis=1, keepdims=True) + EPS)
            grow_row = rk_row * jnp.exp(-cum_row)
            system = jnp.where(strictly & (seg_col == seg_row), raw, 0.0) * (
                beta_col * rk_col * jnp.exp(cum_col)) * grow_row
            scores = jnp.where(seen & (seg_q == seg_row), raw_q, 0.0) * (rq * jnp.exp(cum_q)) * grow_row
            entry_row = jnp.where(seg_row == prior, jnp.exp(cum_row), 0.0)
            entry_q = jnp.where(seg_q == prior, jnp.exp(cum_q), 0.0)
            tail_col = jnp.where(seg_col == seg_last, jnp.exp(cum_last - cum_col), 0.0) * rk_col
            tail_entry = jnp.where(seg_last == prior, jnp.exp(cum_last), 0.0)
            items.append(dict(
                g=g, n=n, key=key, value=value, system=system, scores=scores,
                reach=query32 * (rq * entry_q), wv=beta_row, wk=beta_row * rk_row * entry_row,
                tail=tail_col, tail_entry=tail_entry))
            prior = seg_last

    for item, x in zip(items, invert([item["system"] for item in items])):
        pseudo = mm_exact_right(x * item["wv"], item["value"])
        key_mix = mm_exact_right(x * item["wk"], item["key"])
        both = jnp.concatenate([key_mix, pseudo], axis=1)
        item["both"] = both
    for item in items:
        hi, lo = halves(item["both"] * item["tail"])
        r2 = dotf(item["key"], jnp.concatenate([hi, lo], axis=1), (((0,), (0,)), ((), ())))
        r2 = r2[:, : 2 * DK] + r2[:, 2 * DK :]
        item["trans"] = item["tail_entry"] * eye - r2[:, :DK]
        item["add"] = r2[:, DK:]
        inner = mm(item["scores"], item["both"])
        item["reach"] = item["reach"] - inner[:, :DK]
        item["local"] = inner[:, DK:]

    for n in range(blocks):
        for g in range(heads_step):
            item = items[g * blocks + n]
            rows = slice(n * GROUP, (n + 1) * GROUP)
            lanes = slice(g * DV, (g + 1) * DV)
            if n == 0:
                map_ref[rows, lanes] = item["reach"]
                out_ref[rows, lanes] = item["local"]
                item["prefix"] = jnp.concatenate([item["trans"], item["add"]], axis=1)
            else:
                prefix = items[g * blocks + n - 1]["prefix"]
                joined = mm(jnp.concatenate([item["reach"], item["trans"]], axis=0), prefix)
                map_ref[rows, lanes] = joined[:GROUP, :DK]
                out_ref[rows, lanes] = item["local"] + joined[:GROUP, DK:]
                item["prefix"] = jnp.concatenate(
                    [joined[GROUP:, :DK], joined[GROUP:, DK:] + item["add"]], axis=1)
            if n == blocks - 1:
                pair_ref[g, :DK, :] = item["prefix"]
    first = seg_ref[:, 0:1].astype(F32)
    last = seg_ref[:, blocks * GROUP - 1 :].astype(F32)
    ends = jnp.where(iota((8, 2 * DK), 0) == 0, first, last)
    for g in range(heads_step):
        pair_ref[g, DK:, :] = ends


def local_stage(queries, keys, values, betas, log_decay, segment):
    tok, heads = queries.shape[0], betas.shape[1]
    blocks = tok // GROUP
    step = 1
    body = lambda *refs: local_kernel(step, blocks, *refs)
    return pl.pallas_call(
        body,
        grid=(heads // step,),
        in_specs=[
            pl.BlockSpec((tok, step * DK), lambda h: (0, h)),
            pl.BlockSpec((2 * tok, step * DK), lambda h: (0, h)),
            pl.BlockSpec((2 * tok, step * DV), lambda h: (0, h)),
            pl.BlockSpec((2, heads, tok), lambda h: (0, 0, 0)),
            pl.BlockSpec((heads, tok), lambda h: (0, 0)),
            pl.BlockSpec((1, tok), lambda h: (0, 0)),
        ],
        out_specs=[
            pl.BlockSpec((step, DK + 8, DK + DV), lambda h: (h, 0, 0)),
            pl.BlockSpec((tok, step * DV), lambda h: (0, h)),
            pl.BlockSpec((tok, step * DK), lambda h: (0, h)),
        ],
        out_shape=[
            jax.ShapeDtypeStruct((heads, DK + 8, DK + DV), F32),
            jax.ShapeDtypeStruct((tok, heads * DV), F32),
            jax.ShapeDtypeStruct((tok, heads * DK), F32),
        ],
        scratch_shapes=[pltpu.VMEM((heads, 8 * blocks, ROWS), F32)],
        compiler_params=pltpu.CompilerParams(dimension_semantics=("arbitrary",)),
        name="local_stage",
    )(queries, keys.reshape(2 * tok, heads * DK), values.reshape(2 * tok, heads * DV),
      betas, log_decay, segment.reshape(1, tok))


def prefix_kernel(in_ref, ex_ref, end_ref):
    count = in_ref.shape[0]
    flags = [jnp.where(in_ref[i, DK : DK + 1, :] == in_ref[i - 1, DK + 1 : DK + 2, :], 1.0, 0.0)
             for i in range(1, count)]
    maps = [in_ref[i, :DK, :DK] * (1.0 if i == 0 else flags[i - 1][:, :DK]) for i in range(count)]
    adds = [in_ref[i, :DK, DK:] for i in range(count)]
    width = 1
    while width < count:
        new_maps, new_adds = list(maps), list(adds)
        for i in range(count):
            if i & width:
                j = (i // width) * width - 1
                joined = mm(maps[i], jnp.concatenate([maps[j], adds[j]], axis=1))
                new_maps[i] = joined[:, :DK]
                new_adds[i] = joined[:, DK:] + adds[i]
        maps, adds = new_maps, new_adds
        width *= 2
    r, c = iota((DK, DK), 0), iota((DK, DK), 1)
    ex_ref[0, :, :DK] = (r == c).astype(F32)
    ex_ref[0, :, DK:] = jnp.zeros((DK, DV), F32)
    for i in range(1, count):
        ex_ref[i, :, :DK] = maps[i - 1] * flags[i - 1][:, :DK]
        ex_ref[i, :, DK:] = adds[i - 1] * flags[i - 1][:, DK:]
    end_ref[:DK, :] = adds[count - 1]
    end_ref[DK:, :] = in_ref[count - 1, DK:, :DV]


def incoming_kernel(in_ref, ex_ref, end_ref, out_ref):
    flag = jnp.where(in_ref[0, DK : DK + 1, :DV] == end_ref[DK + 1 : DK + 2, :], 1.0, 0.0)
    state = end_ref[:DK, :] * flag
    for i in range(ex_ref.shape[0]):
        out_ref[i] = mm(ex_ref[i, :, :DK], state) + ex_ref[i, :, DK:]


def final_kernel(local_ref, map_ref, state_ref, gain_ref, weight_ref, out_ref, normed_ref):
    heads = state_ref.shape[0]

    @pl.when(pl.program_id(0) == 0)
    def _():
        for h in range(heads):
            lanes = slice(h * DV, (h + 1) * DV)
            attended = local_ref[:, lanes] + mm(map_ref[:, lanes], state_ref[h])
            mean = jnp.mean(attended * attended, axis=1, keepdims=True)
            normed_ref[:, lanes] = (attended * lax.rsqrt(mean + EPS) * gain_ref[:, lanes]).astype(BF16)

    out_ref[...] = dotf(normed_ref[...], weight_ref[...])


def final_stage(local, mapped, state, gain, weight):
    tok, feats = local.shape
    heads, width = state.shape[0], weight.shape[1]
    tile = min(width, 512)
    whole = lambda *shape: pl.BlockSpec(shape, lambda j: (0,) * len(shape))
    return pl.pallas_call(
        final_kernel,
        grid=(width // tile,),
        in_specs=[whole(tok, feats), whole(tok, feats), whole(heads, DK, DV), whole(1, feats),
                  pl.BlockSpec((feats, tile), lambda j: (0, j))],
        out_specs=pl.BlockSpec((tok, tile), lambda j: (0, j)),
        out_shape=jax.ShapeDtypeStruct((tok, width), F32),
        scratch_shapes=[pltpu.VMEM((tok, feats), BF16)],
        compiler_params=pltpu.CompilerParams(dimension_semantics=("arbitrary",)),
        name="final_stage",
    )(local, mapped, state, gain.reshape(1, feats), weight)


def shards(queries, keys, values, betas, log_decay, segment, gain, out_weight):
    tok, heads = queries.shape[0], betas.shape[1]
    devices = lax.axis_size("ctx")
    span = DOCUMENT_LIMIT // tok
    assert span == heads and devices % span == 0
    groups = [list(range(i, i + span)) for i in range(0, devices, span)]
    pair, local, mapped = local_stage(queries, keys, values, betas, log_decay, segment)
    mine = lax.all_to_all(pair, "ctx", 0, 0, axis_index_groups=groups)
    exclusive, end = pl.pallas_call(
        prefix_kernel,
        out_shape=[jax.ShapeDtypeStruct((span, DK, DK + DV), F32),
                   jax.ShapeDtypeStruct((DK + 8, DV), F32)],
        name="prefix_stage",
    )(mine)
    end = lax.ppermute(end, "ctx", [(i, i + span) for i in range(devices - span)])
    states = pl.pallas_call(
        incoming_kernel,
        out_shape=jax.ShapeDtypeStruct((span, DK, DV), F32),
        name="incoming_stage",
    )(mine, exclusive, end)
    states = lax.all_to_all(states, "ctx", 0, 0, axis_index_groups=groups)
    terms = final_stage(local, mapped, states, gain, out_weight)
    return lax.psum_scatter(terms, "head", scatter_dimension=1, tiled=True).astype(BF16)


def solution(mesh):
    return jax.shard_map(
        shards,
        mesh=mesh,
        in_specs=(
            P("ctx", "head"),
            P("ctx", None, "head"),
            P("ctx", None, "head"),
            P(None, "head", "ctx"),
            P("head", "ctx"),
            P("ctx"),
            P("head"),
            P("head", None),
        ),
        out_specs=P("ctx", "head"),
        check_vma=False,
    )
```

time: 965 us -> 164 us (0.17)
  other arithmetic: 331 us -> 2.09 us
  waiting for transfers between devices: 306 us -> 53.9 us
  matrix products: 190 us -> 0 us
  local copies, waits for them, and re-layouts: 110 us -> 5.15 us
  Pallas kernels: 0 us -> 48.3 us
  blocking collectives: 0 us -> 35.6 us
    another operation x7 -> x0, other arithmetic: 317 us -> none  [the longest x4 316 us: shards(): lax.linalg.triangular_solve(system, right_side, left_side=True, lower=Tru...]
    all_gather x2 -> x0, waiting for transfers between devices: 257 us -> none  [entering(): pieces = jax.tree.map(lambda part: lax.all_gather(part, axis), value)]
    dot_general x81 -> x0, matrix products: 186 us -> none  [the longest x63 130 us: combine_pairs(): jnp.einsum('hab,hbc->hac', earlier[1], later[0], precision=HIGHEST)]
    dynamic_slice x134 -> x0, local copies, waits for them, and re-layouts: 85.7 us -> none  [the longest x126 80.6 us: turn(): longer = join(subtotal, jax.tree.map(lambda part: part[position], pieces))]
    pallas_call x0 -> x4, Pallas kernels: none -> 48.3 us  [the longest x1 32.3 us: local_stage(): pl.pallas_call(body, grid=(heads // step,), in_specs=[pl.BlockSpec((tok,...]
    all_to_all x0 -> x2, blocking collectives: none -> 35.6 us  [the longest x1 21.1 us: shards(): mine = lax.all_to_all(pair, 'ctx', 0, 0, axis_index_groups=groups)]
  transfers between devices with their start and end apart: 4 -> 2, of which waited for: 3 -> 2; matrix products, arithmetic and copies ran while one was open for 38% -> 0% of each run, Pallas kernels for 0% -> 0%
where the time goes in v1:
time: 164 us; the launch traced here: 161 us
  waiting for transfers between devices  53.9 us (33%)
  Pallas kernels  48.3 us (29%)
  blocking collectives  35.6 us (22%)
  between operations  13.4 us (8%)
  local copies, waits for them, and re-layouts  5.15 us (3%)
  starting transfers between devices  2.9 us (2%)
  other arithmetic  2.09 us (1%)
    reduce_scatter x1, waiting for transfers between devices, shards(): lax.psum_scatter(terms, 'head', scatter_dimension=1, tiled=True)  49.2 us
    pallas_call x1, Pallas kernels, local_stage(): pl.pallas_call(body, grid=(heads // step,), in_specs=[pl.BlockSpec((tok,...  32.3 us
    all_to_all x1, blocking collectives, shards(): mine = lax.all_to_all(pair, 'ctx', 0, 0, axis_index_groups=groups)  21.1 us
    all_to_all x1, blocking collectives, shards(): states = lax.all_to_all(states, 'ctx', 0, 0, axis_index_groups=groups)  14.5 us
    pallas_call x1, Pallas kernels, final_stage(): pl.pallas_call(final_kernel, grid=(width // tile,), in_specs=[whole(tok,...  10.3 us
    ppermute x1, waiting for transfers between devices, shards(): lax.ppermute(end, 'ctx', [(i, i + span) for i in range(devices - span)])  4.7 us
  transfers between devices with their start and end apart: 2, of which 2 were waited for; matrix products, arithmetic and copies ran while one was open for 0% of the time, Pallas kernels for 0%

profile of v1, /device:TPU:128, one launch (start us, length us, event | category | flops | bytes accessed | tf_op | source)
XLA Modules:
  0.0 161.3 jit_solution(2412538114372497904)
XLA Ops:
  6.5 0.0 reduce-scatter.2.cloned.1.call-start
  6.5 2.3 %reshape.12.refs_1_ = bf16[512,1024]{1,0:T(8,128)(2,1)} reshape(bf16[256,2,1024]{2,1,0:T(2,128)(2,1)} %param.9) | data formatting | bytes 2097152 | tf_op jit(solution)/shard_map/reshape | solution.py:207
  8.8 2.3 %reshape.13.refs_2_ = bf16[512,1024]{1,0:T(8,128)(2,1)} reshape(bf16[256,2,1024]{2,1,0:T(2,128)(2,1)} %param.10) | data formatting | bytes 2097152 | tf_op jit(solution)/shard_map/reshape | solution.py:207
  11.1 32.3 %local_stage.1 = (f32[8,136,256]{2,1,0:T(8,128)}, f32[256,1024]{1,0:T(8,128)}, f32[256,1024]{1,0:T(8,128)}) custom-call(bf16[256,1024]{1,0:T(8,128)(2,1)} %refs_0_.1, bf16[512,1024]{1,0:T(8,128)(2,1)} %reshape.12.refs_1_, bf16[512,1024]{1,0:T(8,128)(2,1)} %reshape.13.refs_2_, f32[2,8,256]{2,1,0:T(8,128)} %refs_3_.1, f32[8,256]{1,0:T(8,128)} %refs_4_.1, ...), custom_call_target="tpu_custom_call" | custom-call | tf_op jit(solution)/shard_map/local_stage/pallas_call | solution.py:183
  43.3 21.1 %all_to_all.10.in_ref = f32[8,136,256]{2,1,0:T(8,128)} all-to-all(f32[8,136,256]{2,1,0:T(8,128)} %get-tuple-element.12), channel_id=1, replica_groups={{0,4,8,12,16,20,24,28},{32,36,40,44,48,52,56,60},{64,68,72,76,80,84,88,..., dimensions={0} | all-to-all | bytes 2228224 | tf_op jit(solution)/shard_map/all_to_all | solution.py:284
  64.4 3.0 %prefix_stage.1 = (f32[8,128,256]{2,1,0:T(8,128)}, f32[136,128]{1,0:T(8,128)}) custom-call(f32[8,136,256]{2,1,0:T(8,128)} %all_to_all.10.in_ref), custom_call_target="tpu_custom_call" | custom-call | tf_op jit(solution)/shard_map/prefix_stage/pallas_call | solution.py:285
  67.4 2.9 %collective-permute-start = (f32[136,128]{1,0:T(8,128)}, f32[136,128]{1,0:T(8,128)S(1)}, u32[]{:S(2)}, u32[]{:S(2)}) collective-permute-start(f32[136,128]{1,0:T(8,128)} %get-tuple-element.14), channel_id=1, source_target_pairs={{0,32},{4,36},{8,40},{12,44},{16,48},{20,52},{24,56},{28,60},{32,6... | collective-permute-start | bytes 208904 | tf_op jit(solution)/shard_map/ppermute | solution.py:291
  70.3 4.7 %collective-permute-done.end_ref = f32[136,128]{1,0:T(8,128)S(1)} collective-permute-done((f32[136,128]{1,0:T(8,128)}, f32[136,128]{1,0:T(8,128)S(1)}, u32[]{:S(2)}, u32[]{:S(2)}) %collective-permute-start) | collective-permute-done | bytes 69664 | tf_op jit(solution)/shard_map/ppermute | solution.py:291
  75.0 0.0 copy-start
  75.0 0.6 copy-done
  75.6 2.7 %incoming_stage.1 = f32[8,128,128]{2,1,0:T(8,128)} custom-call(f32[8,136,256]{2,1,0:T(8,128)} %all_to_all.10.in_ref, f32[8,128,256]{2,1,0:T(8,128)} %get-tuple-element.13.ex_ref, f32[136,128]{1,0:T(8,128)} %copy-done), custom_call_target="tpu_custom_call" | custom-call | tf_op jit(solution)/shard_map/incoming_stage/pallas_call | solution.py:292
  78.3 14.5 %all_to_all.11.state_ref = f32[8,128,128]{2,1,0:T(8,128)} all-to-all(f32[8,128,128]{2,1,0:T(8,128)} %incoming_stage.1), channel_id=1, replica_groups={{0,4,8,12,16,20,24,28},{32,36,40,44,48,52,56,60},{64,68,72,76,80,84,88,..., dimensions={0} | all-to-all | bytes 1048576 | tf_op jit(solution)/shard_map/all_to_all | solution.py:297
  92.8 10.3 %final_stage.1 = f32[256,4096]{1,0:T(8,128)} custom-call(f32[256,1024]{1,0:T(8,128)} %get-tuple-element.10.local_ref, f32[256,1024]{1,0:T(8,128)} %get-tuple-element.11.map_ref, f32[8,128,128]{2,1,0:T(8,128)} %all_to_all.11.state_ref, f32[1,1024]{1,0:T(1,128)} %bitcast.2, bf16[1024,4096]{1,0:T(8,128)(2,1)} %weight_ref.1), custom_call_target="tpu_custom_call" | custom-call | tf_op jit(solution)/shard_map/final_stage/pallas_call | solution.py:264
  103.1 0.0 reduce-scatter.2.cloned.1.call-update
  103.2 49.2 %reduce-scatter.2.cloned.1.call-done = f32[256,1024]{1,0:T(8,128)} async-done(((f32[256,4096]{1,0:T(8,128)}), f32[256,1024]{1,0:T(8,128)}) %reduce-scatter.2.cloned.1.call-update) | async-done | bytes 1048592 | tf_op jit(solution)/shard_map/reduce_scatter | solution.py:299
  152.4 2.1 %convert_element_type.3 = bf16[256,1024]{1,0:T(8,128)(2,1)} convert(f32[256,1024]{1,0:T(8,128)} %reduce-scatter.2.cloned.1.call-done) | non-fusion elementwise | flops 262144 | bytes 1572864 | tf_op jit(solution)/shard_map/convert_element_type | solution.py:299
Async XLA Ops:
  6.5 145.8 %reduce-scatter.2.cloned.1.call-start = ((), (), s32[]{:S(2)}) async-start(), calls=%async_computation.3 | async-start | bytes 5242880 | tf_op jit(solution)/shard_map/reduce_scatter | solution.py:299
  67.4 7.6 %collective-permute-start = (f32[136,128]{1,0:T(8,128)}, f32[136,128]{1,0:T(8,128)S(1)}, u32[]{:S(2)}, u32[]{:S(2)}) collective-permute-start(f32[136,128]{1,0:T(8,128)} %get-tuple-element.14), channel_id=1, source_target_pairs={{0,32},{4,36},{8,40},{12,44},{16,48},{20,52},{24,56},{28,60},{32,6... | collective-permute-start | bytes 208904 | tf_op jit(solution)/shard_map/ppermute | solution.py:291
  75.0 0.6 copy-start
Sparse Core Ops, SparseCore 0:
  103.3 49.0 reduce-scatter.1

commit v2 on v1

--- a/solution.py
+++ b/solution.py
@@ -107,9 +107,9 @@
                                   + [jnp.zeros((ROWS - 8 * blocks, ROWS), F32)], axis=0).T
         prior = table[2:3, 0:1]
         for n in range(blocks):
-            key = k_ref[n * ROWS : (n + 1) * ROWS, lanes]
+            key = k_ref[n * GROUP : (n + 1) * GROUP, :, lanes].reshape(ROWS, DK)
             query = q_ref[n * GROUP : (n + 1) * GROUP, lanes]
-            value = v_ref[n * ROWS : (n + 1) * ROWS, lanes]
+            value = v_ref[n * GROUP : (n + 1) * GROUP, :, lanes].reshape(ROWS, DV)
             cum_row, beta_row, seg_row = (table[8 * n + i : 8 * n + i + 1] for i in range(3))
             cum_col, beta_col, seg_col = (columns[:, 8 * n + i : 8 * n + i + 1] for i in range(3))
             cum_q, seg_q = (columns[:GROUP, 8 * n + i : 8 * n + i + 1] for i in (3, 4))
@@ -185,8 +185,8 @@
         grid=(heads // step,),
         in_specs=[
             pl.BlockSpec((tok, step * DK), lambda h: (0, h)),
-            pl.BlockSpec((2 * tok, step * DK), lambda h: (0, h)),
-            pl.BlockSpec((2 * tok, step * DV), lambda h: (0, h)),
+            pl.BlockSpec((tok, 2, step * DK), lambda h: (0, 0, h)),
+            pl.BlockSpec((tok, 2, step * DV), lambda h: (0, 0, h)),
             pl.BlockSpec((2, heads, tok), lambda h: (0, 0, 0)),
             pl.BlockSpec((heads, tok), lambda h: (0, 0)),
             pl.BlockSpec((1, tok), lambda h: (0, 0)),
@@ -204,8 +204,7 @@
         scratch_shapes=[pltpu.VMEM((heads, 8 * blocks, ROWS), F32)],
         compiler_params=pltpu.CompilerParams(dimension_semantics=("arbitrary",)),
         name="local_stage",
-    )(queries, keys.reshape(2 * tok, heads * DK), values.reshape(2 * tok, heads * DV),
-      betas, log_decay, segment.reshape(1, tok))
+    )(queries, keys, values, betas, log_decay, segment.reshape(1, tok))
 
 
 def prefix_kernel(in_ref, ex_ref, end_ref):
@@ -242,36 +241,79 @@
         out_ref[i] = mm(ex_ref[i, :, :DK], state) + ex_ref[i, :, DK:]
 
 
-def final_kernel(local_ref, map_ref, state_ref, gain_ref, weight_ref, out_ref, normed_ref):
+def far_kernel(pick_ref, local_ref, map_ref, state_ref, gain_ref, weight_ref, normed_ref, up_ref, down_ref):
     heads = state_ref.shape[0]
-
-    @pl.when(pl.program_id(0) == 0)
-    def _():
-        for h in range(heads):
-            lanes = slice(h * DV, (h + 1) * DV)
-            attended = local_ref[:, lanes] + mm(map_ref[:, lanes], state_ref[h])
-            mean = jnp.mean(attended * attended, axis=1, keepdims=True)
-            normed_ref[:, lanes] = (attended * lax.rsqrt(mean + EPS) * gain_ref[:, lanes]).astype(BF16)
-
-    out_ref[...] = dotf(normed_ref[...], weight_ref[...])
-
-
-def final_stage(local, mapped, state, gain, weight):
+    for h in range(heads):
+        lanes = slice(h * DV, (h + 1) * DV)
+        attended = local_ref[:, lanes] + mm(map_ref[:, lanes], state_ref[h])
+        mean = jnp.mean(attended * attended, axis=1, keepdims=True)
+        normed_ref[:, lanes] = (attended * lax.rsqrt(mean + EPS) * gain_ref[:, lanes]).astype(BF16)
+    half = up_ref.shape[0]
+    up_ref[...] = dotf(normed_ref[:half, :], weight_ref[...])
+    down_ref[...] = dotf(normed_ref[half:, :], weight_ref[...])
+
+
+def tile_kernel(pick_ref, normed_ref, weight_ref, top_ref, bottom_ref):
+    half = top_ref.shape[0]
+    top_ref[...] = dotf(normed_ref[:half, :], weight_ref[...])
+    bottom_ref[...] = dotf(normed_ref[half:, :], weight_ref[...])
+
+
+def whole(*shape):
+    return pl.BlockSpec(shape, lambda i, *_: (0,) * len(shape))
+
+
+def far_tile(place, local, mapped, state, gain, weight, width):
     tok, feats = local.shape
-    heads, width = state.shape[0], weight.shape[1]
-    tile = min(width, 512)
-    whole = lambda *shape: pl.BlockSpec(shape, lambda j: (0,) * len(shape))
+    heads = state.shape[0]
+    part = jax.ShapeDtypeStruct((tok // 2, width), F32)
     return pl.pallas_call(
-        final_kernel,
-        grid=(width // tile,),
-        in_specs=[whole(tok, feats), whole(tok, feats), whole(heads, DK, DV), whole(1, feats),
-                  pl.BlockSpec((feats, tile), lambda j: (0, j))],
-        out_specs=pl.BlockSpec((tok, tile), lambda j: (0, j)),
-        out_shape=jax.ShapeDtypeStruct((tok, width), F32),
-        scratch_shapes=[pltpu.VMEM((tok, feats), BF16)],
-        compiler_params=pltpu.CompilerParams(dimension_semantics=("arbitrary",)),
-        name="final_stage",
-    )(local, mapped, state, gain.reshape(1, feats), weight)
+        far_kernel,
+        grid_spec=pltpu.PrefetchScalarGridSpec(
+            num_scalar_prefetch=1, grid=(1,),
+            in_specs=[whole(tok, feats), whole(tok, feats), whole(heads, DK, DV), whole(1, feats),
+                      pl.BlockSpec((feats, width), lambda i, at: (0, at[0]))],
+            out_specs=[whole(tok, feats), whole(tok // 2, width), whole(tok // 2, width)]),
+        out_shape=[jax.ShapeDtypeStruct((tok, feats), BF16), part, part],
+        name="far_tile",
+    )(place, local, mapped, state, gain.reshape(1, feats), weight)
+
+
+def one_tile(place, normed, weight, width, name):
+    tok, feats = normed.shape
+    part = jax.ShapeDtypeStruct((tok // 2, width), F32)
+    cols = width // 2
+    out = pl.BlockSpec((tok // 2, cols), lambda i, at: (0, i))
+    return pl.pallas_call(
+        tile_kernel,
+        grid_spec=pltpu.PrefetchScalarGridSpec(
+            num_scalar_prefetch=1, grid=(2,),
+            in_specs=[whole(tok, feats), pl.BlockSpec((feats, cols), lambda i, at: (0, 2 * at[0] + i))],
+            out_specs=[out, out]),
+        out_shape=[part, part],
+        name=name,
+    )(place, normed, weight)
+
+
+def summed_output(local, mapped, states, gain, out_weight):
+    count = lax.axis_size("head")
+    assert count == 4
+    mine = lax.axis_index("head")
+    width = out_weight.shape[1] // count
+    rise = [(i, (i + 1) % count) for i in range(count)]
+    fall = [(i, (i - 1) % count) for i in range(count)]
+    at = lambda step: ((mine + step) % count).astype(jnp.int32).reshape(1)
+    up = lambda x: lax.ppermute(x, "head", rise)
+    down = lambda x: lax.ppermute(x, "head", fall)
+    normed, far_top, far_bottom = far_tile(at(2), local, mapped, states, gain, out_weight, width)
+    got_top, got_bottom = up(far_top), down(far_bottom)
+    next_top, next_bottom = one_tile(at(1), normed, out_weight, width, "next_tile")
+    last_top, last_bottom = one_tile(at(3), normed, out_weight, width, "last_tile")
+    side_bottom, side_top = up(next_bottom), down(last_top)
+    got_top, got_bottom = up(next_top + got_top), down(last_bottom + got_bottom)
+    own_top, own_bottom = one_tile(at(0), normed, out_weight, width, "own_tile")
+    return jnp.concatenate([(own_top + side_top + got_top).astype(BF16),
+                            (own_bottom + side_bottom + got_bottom).astype(BF16)], axis=0)
 
 
 def shards(queries, keys, values, betas, log_decay, segment, gain, out_weight):
@@ -295,8 +337,7 @@
         name="incoming_stage",
     )(mine, exclusive, end)
     states = lax.all_to_all(states, "ctx", 0, 0, axis_index_groups=groups)
-    terms = final_stage(local, mapped, states, gain, out_weight)
-    return lax.psum_scatter(terms, "head", scatter_dimension=1, tiled=True).astype(BF16)
+    return summed_output(local, mapped, states, gain, out_weight)
 
 
 def solution(mesh):

time: 164 us -> 128 us (0.78); the launches traced: 161 us -> 127 us
  waiting for transfers between devices: 53.9 us -> 34.9 us
  blocking collectives: 35.6 us -> 21.1 us
  between operations: 13.4 us -> 0.07 us
  starting transfers between devices: 2.9 us -> 16.1 us
  local copies, waits for them, and re-layouts: 5.15 us -> 1.43 us
  Pallas kernels: 48.3 us -> 51.4 us
    reduce_scatter x1 -> x0, waiting for transfers between devices: 49.2 us -> none  [shards(): lax.psum_scatter(terms, 'head', scatter_dimension=1, tiled=True)]
    ppermute x0 -> x6, waiting for transfers between devices: none -> 20 us  [the longest x3 14.8 us: summed_output(): up = lambda x: lax.ppermute(x, 'head', rise)]
    all_to_all x1 -> x0, blocking collectives: 14.5 us -> none  [shards(): states = lax.all_to_all(states, 'ctx', 0, 0, axis_index_groups=groups)]
    all_to_all x0 -> x1, waiting for transfers between devices: none -> 10.2 us  [shards(): states = lax.all_to_all(states, 'ctx', 0, 0, axis_index_groups=groups)]
    ppermute x0 -> x6, starting transfers between devices: none -> 9.64 us  [the longest x3 6.1 us: summed_output(): down = lambda x: lax.ppermute(x, 'head', fall)]
    reshape x2 -> x0, local copies, waits for them, and re-layouts: 4.52 us -> none  [the longest x1 2.27 us: local_stage(): keys.reshape(2 * tok, heads * DK)]
    all_to_all x0 -> x1, starting transfers between devices: none -> 3.49 us  [shards(): states = lax.all_to_all(states, 'ctx', 0, 0, axis_index_groups=groups)]
    pallas_call x1 -> x4, Pallas kernels: 10.3 us -> 13.5 us  [the longest x3 9.07 us: one_tile(): pl.pallas_call(tile_kernel, grid_spec=pltpu.PrefetchScalarGridSpec(num_sc...]
  transfers between devices with their start and end apart: 2 -> 8, of which waited for: 2 -> 6; matrix products, arithmetic and copies ran while one was open for 0% -> 1% of each run, Pallas kernels for 0% -> 7%
where the time goes in v2:
time: 128 us; the launch traced here: 127 us
  Pallas kernels  51.4 us (40%)
  waiting for transfers between devices  34.9 us (27%)
  blocking collectives  21.1 us (16%)
  starting transfers between devices  16.1 us (13%)
  other arithmetic  2.19 us (2%)
  local copies, waits for them, and re-layouts  1.43 us (1%)
    pallas_call x1, Pallas kernels, local_stage(): pl.pallas_call(body, grid=(heads // step,), in_specs=[pl.BlockSpec((tok,...  32.3 us
    all_to_all x1, blocking collectives, shards(): mine = lax.all_to_all(pair, 'ctx', 0, 0, axis_index_groups=groups)  21.1 us
    ppermute x3, waiting for transfers between devices, summed_output(): up = lambda x: lax.ppermute(x, 'head', rise)  14.8 us
    all_to_all x1, waiting for transfers between devices, shards(): states = lax.all_to_all(states, 'ctx', 0, 0, axis_index_groups=groups)  10.2 us
    pallas_call x3, Pallas kernels, one_tile(): pl.pallas_call(tile_kernel, grid_spec=pltpu.PrefetchScalarGridSpec(num_sc...  9.07 us
    ppermute x3, starting transfers between devices, summed_output(): down = lambda x: lax.ppermute(x, 'head', fall)  6.1 us
    ppermute x3, waiting for transfers between devices, summed_output(): down = lambda x: lax.ppermute(x, 'head', fall)  5.21 us
    ppermute x1, waiting for transfers between devices, shards(): lax.ppermute(end, 'ctx', [(i, i + span) for i in range(devices - span)])  4.69 us
  transfers between devices with their start and end apart: 8, of which 6 were waited for; matrix products, arithmetic and copies ran while one was open for 1% of the time, Pallas kernels for 7%

profile of v2, /device:TPU:128, one launch (start us, length us, event | category | flops | bytes accessed | tf_op | source)
XLA Modules:
  0.0 127.2 jit_solution(514324228048638438)
XLA Ops:
  0.0 32.3 %local_stage.1 = (f32[8,136,256]{2,1,0:T(8,128)}, f32[256,1024]{1,0:T(8,128)}, f32[256,1024]{1,0:T(8,128)}) custom-call(bf16[256,1024]{1,0:T(8,128)(2,1)} %refs_0_.1, bf16[256,2,1024]{2,1,0:T(2,128)(2,1)} %refs_1_.1, bf16[256,2,1024]{2,1,0:T(2,128)(2,1)} %refs_2_.1, f32[2,8,256]{2,1,0:T(8,128)} %refs_3_.1, f32[8,256]{1,0:T(8,128)} %refs_4_.1, s32[1,256]{1,0:T(1,128)} %bitcast.7), custom_call_target="tpu_custom_call" | custom-call | tf_op jit(solution)/shard_map/local_stage/pallas_call | solution.py:183
  32.3 21.1 %all_to_all.10.in_ref = f32[8,136,256]{2,1,0:T(8,128)} all-to-all(f32[8,136,256]{2,1,0:T(8,128)} %get-tuple-element.21), channel_id=1, replica_groups={{0,4,8,12,16,20,24,28},{32,36,40,44,48,52,56,60},{64,68,72,76,80,84,88,..., dimensions={0} | all-to-all | bytes 2228224 | tf_op jit(solution)/shard_map/all_to_all | solution.py:326
  53.4 3.0 %prefix_stage.1 = (f32[8,128,256]{2,1,0:T(8,128)}, f32[136,128]{1,0:T(8,128)}) custom-call(f32[8,136,256]{2,1,0:T(8,128)} %all_to_all.10.in_ref), custom_call_target="tpu_custom_call" | custom-call | tf_op jit(solution)/shard_map/prefix_stage/pallas_call | solution.py:327
  56.4 2.9 %collective-permute-start = (f32[136,128]{1,0:T(8,128)}, f32[136,128]{1,0:T(8,128)S(1)}, u32[]{:S(2)}, u32[]{:S(2)}) collective-permute-start(f32[136,128]{1,0:T(8,128)} %get-tuple-element.23), channel_id=1, source_target_pairs={{0,32},{4,36},{8,40},{12,44},{16,48},{20,52},{24,56},{28,60},{32,6... | collective-permute-start | bytes 208904 | tf_op jit(solution)/shard_map/ppermute | solution.py:333
  59.3 4.7 %collective-permute-done.end_ref = f32[136,128]{1,0:T(8,128)S(1)} collective-permute-done((f32[136,128]{1,0:T(8,128)}, f32[136,128]{1,0:T(8,128)S(1)}, u32[]{:S(2)}, u32[]{:S(2)}) %collective-permute-start) | collective-permute-done | bytes 69664 | tf_op jit(solution)/shard_map/ppermute | solution.py:333
  64.0 0.0 copy-start.4
  64.0 0.6 copy-done.4
  64.6 2.7 %incoming_stage.1 = f32[8,128,128]{2,1,0:T(8,128)} custom-call(f32[8,136,256]{2,1,0:T(8,128)} %all_to_all.10.in_ref, f32[8,128,256]{2,1,0:T(8,128)} %get-tuple-element.22.ex_ref, f32[136,128]{1,0:T(8,128)} %copy-done.4), custom_call_target="tpu_custom_call" | custom-call | tf_op jit(solution)/shard_map/incoming_stage/pallas_call | solution.py:334
  67.3 3.5 %all-to-all-start.1 = ((f32[8,128,128]{2,1,0:T(8,128)}), f32[8,128,128]{2,1,0:T(8,128)S(1)}, u32[]{:S(2)}, u32[]{:S(2)}) async-start(f32[8,128,128]{2,1,0:T(8,128)} %incoming_stage.1), calls=%async_computation.1 | async-start | bytes 1048576 | tf_op jit(solution)/shard_map/all_to_all | solution.py:339
  70.8 10.2 %all-to-all-done.1.state_ref = f32[8,128,128]{2,1,0:T(8,128)S(1)} async-done(((f32[8,128,128]{2,1,0:T(8,128)}), f32[8,128,128]{2,1,0:T(8,128)S(1)}, u32[]{:S(2)}, u32[]{:S(2)}) %all-to-all-start.1) | async-done | bytes 524320 | tf_op jit(solution)/shard_map/all_to_all | solution.py:339
  81.0 0.0 copy-start
  81.0 0.8 copy-done
  81.8 4.4 %far_tile.1 = (bf16[256,1024]{1,0:T(8,128)(2,1)}, f32[128,1024]{1,0:T(8,128)}, f32[128,1024]{1,0:T(8,128)}) custom-call(s32[1]{0:T(128)} %bitcast.1.pick_ref, f32[256,1024]{1,0:T(8,128)} %get-tuple-element.19.local_ref, f32[256,1024]{1,0:T(8,128)} %get-tuple-element.20.map_ref, f32[8,128,128]{2,1,0:T(8,128)} %copy-done, f32[1,1024]{1,0:T(1,128)} %bitcast.6, ...), custom_call_target="tpu_custom_call" | custom-call | tf_op jit(solution)/shard_map/far_tile/pallas_call | solution.py:270
  86.2 1.6 %collective-permute-start.2 = (f32[128,1024]{1,0:T(8,128)}, f32[128,1024]{1,0:T(8,128)S(1)}, u32[]{:S(2)}, u32[]{:S(2)}) collective-permute-start(f32[128,1024]{1,0:T(8,128)} %get-tuple-element.28), channel_id=1, source_target_pairs={{0,1},{1,2},{2,3},{3,0},{4,5},{5,6},{6,7},{7,4},{8,9},{9,10},{10,1... | collective-permute-start | bytes 1572872 | tf_op jit(solution)/shard_map/ppermute | solution.py:306
  87.8 1.7 %collective-permute-start.5 = (f32[128,1024]{1,0:T(8,128)}, f32[128,1024]{1,0:T(8,128)S(1)}, u32[]{:S(2)}, u32[]{:S(2)}) collective-permute-start(f32[128,1024]{1,0:T(8,128)} %get-tuple-element.32), channel_id=1, source_target_pairs={{0,3},{1,0},{2,1},{3,2},{4,7},{5,4},{6,5},{7,6},{8,11},{9,8},{10,9... | collective-permute-start | bytes 1572872 | tf_op jit(solution)/shard_map/ppermute | solution.py:307
  89.4 3.0 %next_tile.1 = (f32[128,1024]{1,0:T(8,128)}, f32[128,1024]{1,0:T(8,128)}) custom-call(s32[1]{0:T(128)} %bitcast.5.pick_ref, bf16[256,1024]{1,0:T(8,128)(2,1)} %get-tuple-element.24.normed_ref, bf16[1024,4096]{1,0:T(8,128)(2,1)} %weight_ref.7), custom_call_target="tpu_custom_call" | custom-call | tf_op jit(solution)/shard_map/next_tile/pallas_call | solution.py:287
  92.4 0.0 copy-start.3
  92.4 3.1 %last_tile.1 = (f32[128,1024]{1,0:T(8,128)}, f32[128,1024]{1,0:T(8,128)}) custom-call(s32[1]{0:T(128)} %bitcast.4.pick_ref, bf16[256,1024]{1,0:T(8,128)(2,1)} %get-tuple-element.24.normed_ref, bf16[1024,4096]{1,0:T(8,128)(2,1)} %weight_ref.7), custom_call_target="tpu_custom_call" | custom-call | tf_op jit(solution)/shard_map/last_tile/pallas_call | solution.py:287
  95.5 0.0 copy-start.1
  95.5 1.8 %collective-permute-start.1 = (f32[128,1024]{1,0:T(8,128)}, f32[128,1024]{1,0:T(8,128)S(1)}, u32[]{:S(2)}, u32[]{:S(2)}) collective-permute-start(f32[128,1024]{1,0:T(8,128)} %get-tuple-element.26), channel_id=1, source_target_pairs={{0,3},{1,0},{2,1},{3,2},{4,7},{5,4},{6,5},{7,6},{8,11},{9,8},{10,9... | collective-permute-start | bytes 1572872 | tf_op jit(solution)/shard_map/ppermute | solution.py:307
  97.3 3.7 %collective-permute-done.2 = f32[128,1024]{1,0:T(8,128)S(1)} collective-permute-done((f32[128,1024]{1,0:T(8,128)}, f32[128,1024]{1,0:T(8,128)S(1)}, u32[]{:S(2)}, u32[]{:S(2)}) %collective-permute-start.2) | collective-permute-done | bytes 524320 | tf_op jit(solution)/shard_map/ppermute | solution.py:306
  101.1 0.0 copy-done.3
  101.1 0.1 add.48
  101.1 0.4 collective-permute-start.3
  101.5 1.6 %collective-permute-start.4 = (f32[128,1024]{1,0:T(8,128)}, f32[128,1024]{1,0:T(8,128)S(1)}, u32[]{:S(2)}, u32[]{:S(2)}) collective-permute-start(f32[128,1024]{1,0:T(8,128)} %get-tuple-element.30), channel_id=1, source_target_pairs={{0,1},{1,2},{2,3},{3,0},{4,5},{5,6},{6,7},{7,4},{8,9},{9,10},{10,1... | collective-permute-start | bytes 1572872 | tf_op jit(solution)/shard_map/ppermute | solution.py:306
  103.1 0.0 collective-permute-done.5
  103.1 0.0 copy-done.1
  103.1 0.1 add.51
  103.2 2.6 %collective-permute-start.6 = (f32[128,1024]{1,0:T(8,128)S(1)}, f32[128,1024]{1,0:T(8,128)S(1)}, u32[]{:S(2)}, u32[]{:S(2)}) collective-permute-start(f32[128,1024]{1,0:T(8,128)S(1)} %add.51), channel_id=1, source_target_pairs={{0,3},{1,0},{2,1},{3,2},{4,7},{5,4},{6,5},{7,6},{8,11},{9,8},{10,9... | collective-permute-start | bytes 1572872 | tf_op jit(solution)/shard_map/ppermute | solution.py:307
  105.8 3.0 %own_tile.1 = (f32[128,1024]{1,0:T(8,128)}, f32[128,1024]{1,0:T(8,128)}) custom-call(s32[1]{0:T(128)} %bitcast.pick_ref, bf16[256,1024]{1,0:T(8,128)(2,1)} %get-tuple-element.24.normed_ref, bf16[1024,4096]{1,0:T(8,128)(2,1)} %weight_ref.7), custom_call_target="tpu_custom_call" | custom-call | tf_op jit(solution)/shard_map/own_tile/pallas_call | solution.py:287
  108.8 0.0 copy-start.2
  108.8 5.2 %collective-permute-done.1 = f32[128,1024]{1,0:T(8,128)S(1)} collective-permute-done((f32[128,1024]{1,0:T(8,128)}, f32[128,1024]{1,0:T(8,128)S(1)}, u32[]{:S(2)}, u32[]{:S(2)}) %collective-permute-start.1) | collective-permute-done | bytes 524320 | tf_op jit(solution)/shard_map/ppermute | solution.py:307
  114.0 3.2 %collective-permute-done.3 = f32[128,1024]{1,0:T(8,128)S(1)} collective-permute-done((f32[128,1024]{1,0:T(8,128)S(1)}, f32[128,1024]{1,0:T(8,128)S(1)}, u32[]{:S(2)}, u32[]{:S(2)}) %collective-permute-start.3) | collective-permute-done | bytes 524320 | tf_op jit(solution)/shard_map/ppermute | solution.py:306
  117.2 1.1 add_convert_fusion.1
  118.3 7.9 %collective-permute-done.4 = f32[128,1024]{1,0:T(8,128)S(1)} collective-permute-done((f32[128,1024]{1,0:T(8,128)}, f32[128,1024]{1,0:T(8,128)S(1)}, u32[]{:S(2)}, u32[]{:S(2)}) %collective-permute-start.4) | collective-permute-done | bytes 524320 | tf_op jit(solution)/shard_map/ppermute | solution.py:306
  126.2 0.0 collective-permute-done.6
  126.2 0.0 copy-done.2
  126.2 0.1 add_convert_fusion
  126.3 0.8 pad_maximum_fusion
Async XLA Ops:
  56.4 7.6 %collective-permute-start = (f32[136,128]{1,0:T(8,128)}, f32[136,128]{1,0:T(8,128)S(1)}, u32[]{:S(2)}, u32[]{:S(2)}) collective-permute-start(f32[136,128]{1,0:T(8,128)} %get-tuple-element.23), channel_id=1, source_target_pairs={{0,32},{4,36},{8,40},{12,44},{16,48},{20,52},{24,56},{28,60},{32,6... | collective-permute-start | bytes 208904 | tf_op jit(solution)/shard_map/ppermute | solution.py:333
  64.0 0.6 copy-start.4
  67.3 13.7 %all-to-all-start.1 = ((f32[8,128,128]{2,1,0:T(8,128)}), f32[8,128,128]{2,1,0:T(8,128)S(1)}, u32[]{:S(2)}, u32[]{:S(2)}) async-start(f32[8,128,128]{2,1,0:T(8,128)} %incoming_stage.1), calls=%async_computation.1 | async-start | bytes 1048576 | tf_op jit(solution)/shard_map/all_to_all | solution.py:339
  81.0 0.8 copy-start
  86.2 14.9 %collective-permute-start.2 = (f32[128,1024]{1,0:T(8,128)}, f32[128,1024]{1,0:T(8,128)S(1)}, u32[]{:S(2)}, u32[]{:S(2)}) collective-permute-start(f32[128,1024]{1,0:T(8,128)} %get-tuple-element.28), channel_id=1, source_target_pairs={{0,1},{1,2},{2,3},{3,0},{4,5},{5,6},{6,7},{7,4},{8,9},{9,10},{10,1... | collective-permute-start | bytes 1572872 | tf_op jit(solution)/shard_map/ppermute | solution.py:306
  87.8 15.3 %collective-permute-start.5 = (f32[128,1024]{1,0:T(8,128)}, f32[128,1024]{1,0:T(8,128)S(1)}, u32[]{:S(2)}, u32[]{:S(2)}) collective-permute-start(f32[128,1024]{1,0:T(8,128)} %get-tuple-element.32), channel_id=1, source_target_pairs={{0,3},{1,0},{2,1},{3,2},{4,7},{5,4},{6,5},{7,6},{8,11},{9,8},{10,9... | collective-permute-start | bytes 1572872 | tf_op jit(solution)/shard_map/ppermute | solution.py:307
  92.4 8.6 %copy-start.3 = (f32[128,1024]{1,0:T(8,128)S(1)}, f32[128,1024]{1,0:T(8,128)}, u32[]{:S(2)}) copy-start(f32[128,1024]{1,0:T(8,128)} %get-tuple-element.27) | copy-start | bytes 1572868
  95.5 7.6 %copy-start.1 = (f32[128,1024]{1,0:T(8,128)S(1)}, f32[128,1024]{1,0:T(8,128)}, u32[]{:S(2)}) copy-start(f32[128,1024]{1,0:T(8,128)} %get-tuple-element.31) | copy-start | bytes 1572868
  95.5 18.5 %collective-permute-start.1 = (f32[128,1024]{1,0:T(8,128)}, f32[128,1024]{1,0:T(8,128)S(1)}, u32[]{:S(2)}, u32[]{:S(2)}) collective-permute-start(f32[128,1024]{1,0:T(8,128)} %get-tuple-element.26), channel_id=1, source_target_pairs={{0,3},{1,0},{2,1},{3,2},{4,7},{5,4},{6,5},{7,6},{8,11},{9,8},{10,9... | collective-permute-start | bytes 1572872 | tf_op jit(solution)/shard_map/ppermute | solution.py:307
  101.1 16.1 %collective-permute-start.3 = (f32[128,1024]{1,0:T(8,128)S(1)}, f32[128,1024]{1,0:T(8,128)S(1)}, u32[]{:S(2)}, u32[]{:S(2)}) collective-permute-start(f32[128,1024]{1,0:T(8,128)S(1)} %add.48), channel_id=1, source_target_pairs={{0,1},{1,2},{2,3},{3,0},{4,5},{5,6},{6,7},{7,4},{8,9},{9,10},{10,1... | collective-permute-start | bytes 1572872 | tf_op jit(solution)/shard_map/ppermute | solution.py:306
  101.5 24.7 %collective-permute-start.4 = (f32[128,1024]{1,0:T(8,128)}, f32[128,1024]{1,0:T(8,128)S(1)}, u32[]{:S(2)}, u32[]{:S(2)}) collective-permute-start(f32[128,1024]{1,0:T(8,128)} %get-tuple-element.30), channel_id=1, source_target_pairs={{0,1},{1,2},{2,3},{3,0},{4,5},{5,6},{6,7},{7,4},{8,9},{9,10},{10,1... | collective-permute-start | bytes 1572872 | tf_op jit(solution)/shard_map/ppermute | solution.py:306
  103.2 23.1 %collective-permute-start.6 = (f32[128,1024]{1,0:T(8,128)S(1)}, f32[128,1024]{1,0:T(8,128)S(1)}, u32[]{:S(2)}, u32[]{:S(2)}) collective-permute-start(f32[128,1024]{1,0:T(8,128)S(1)} %add.51), channel_id=1, source_target_pairs={{0,3},{1,0},{2,1},{3,2},{4,7},{5,4},{6,5},{7,6},{8,11},{9,8},{10,9... | collective-permute-start | bytes 1572872 | tf_op jit(solution)/shard_map/ppermute | solution.py:307
  108.8 17.4 %copy-start.2 = (f32[128,1024]{1,0:T(8,128)S(1)}, f32[128,1024]{1,0:T(8,128)}, u32[]{:S(2)}) copy-start(f32[128,1024]{1,0:T(8,128)} %get-tuple-element.29) | copy-start | bytes 1572868

commit v3 on v2

--- a/solution.py
+++ b/solution.py
@@ -55,14 +55,34 @@
     shift = 1
     while (1 << shift) < ROWS:
         band = ((r >> (shift + 1)) == (c >> (shift + 1))) & ((r >> shift) != (c >> shift))
-        ys = [mm(jnp.where(band, s, 0.0), x) for s, x in zip(systems, xs)]
-        xs = [x - mm(x, y) for x, y in zip(xs, ys)]
+        if shift < 3:
+            ys = [mm(jnp.where(band, s, 0.0), x) for s, x in zip(systems, xs)]
+            xs = [x - mm(x, y) for x, y in zip(xs, ys)]
+        else:
+            size = 1 << shift
+            low = lambda m: jnp.concatenate(
+                [m[i : i + size] for i in range(size, ROWS, 2 * size)], axis=0)
+
+            def spread(m, rest):
+                parts = []
+                for i in range(ROWS // (2 * size)):
+                    parts += [rest(i), m[i * size : (i + 1) * size]]
+                return jnp.concatenate(parts, axis=0)
+
+            empty = jnp.zeros((size, ROWS), F32)
+            low_band = low(band.astype(F32))
+            ys = [mm(low(s) * low_band, x) for s, x in zip(systems, xs)]
+            ys = [spread(y, lambda i: empty) for y in ys]
+            lows = [low(x) for x in xs]
+            lows = [x - mm(x, y) for x, y in zip(lows, ys)]
+            xs = [spread(y, lambda i: x[2 * i * size : (2 * i + 1) * size])
+                  for x, y in zip(xs, lows)]
         shift += 1
     return xs
 
 
-def local_kernel(heads_step, blocks, q_ref, k_ref, v_ref, beta_ref, log_ref, seg_ref,
-                 pair_ref, out_ref, map_ref, tab_ref):
+def key_kernel(heads_step, blocks, k_ref, v_ref, beta_ref, log_ref, seg_ref,
+               pair_ref, solved_ref, prefix_ref, tab_ref):
     step = pl.program_id(0)
     heads = log_ref.shape[0]
 
@@ -96,115 +116,172 @@
     diag = r == c
     eye = diag.astype(F32)
     strictly = r > c
-    qr, qc = iota((GROUP, ROWS), 0), iota((GROUP, ROWS), 1)
-    seen = qc <= 2 * qr + 1
 
     items = []
     for g in range(heads_step):
         lanes = slice(g * DK, (g + 1) * DK)
         table = tab_ref[step * heads_step + g]
-        columns = jnp.concatenate([table[8 * n : 8 * n + 8] for n in range(blocks)]
-                                  + [jnp.zeros((ROWS - 8 * blocks, ROWS), F32)], axis=0).T
+        columns = columns_of(table, blocks)
+        prior = table[2:3, 0:1]
+        for n in range(blocks):
+            key = k_ref[n * GROUP : (n + 1) * GROUP, :, lanes].reshape(ROWS, DK)
+            value = v_ref[n * GROUP : (n + 1) * GROUP, :, lanes].reshape(ROWS, DV)
+            cum_row, beta_row, seg_row = (table[8 * n + i : 8 * n + i + 1] for i in range(3))
+            cum_col, beta_col, seg_col = (columns[:, 8 * n + i : 8 * n + i + 1] for i in range(3))
+            cum_last, seg_last = cum_row[:, ROWS - 1 :], seg_row[:, ROWS - 1 :]
+            raw = dotf(key, key, (((1,), (1,)), ((), ())))
+            own = jnp.where(diag, raw, 0.0)
+            rk_row = lax.rsqrt(jnp.sum(own, axis=0, keepdims=True) + EPS)
+            rk_col = lax.rsqrt(jnp.sum(own, axis=1, keepdims=True) + EPS)
+            tab_ref[step * heads_step + g, 8 * n + 5 : 8 * n + 6, :] = rk_row
+            system = jnp.where(strictly & (seg_col == seg_row), raw, 0.0) * (
+                beta_col * rk_col * jnp.exp(cum_col)) * (rk_row * jnp.exp(-cum_row))
+            entry_row = jnp.where(seg_row == prior, jnp.exp(cum_row), 0.0)
+            tail_col = jnp.where(seg_col == seg_last, jnp.exp(cum_last - cum_col), 0.0) * rk_col
+            tail_entry = jnp.where(seg_last == prior, jnp.exp(cum_last), 0.0)
+            items.append(dict(
+                g=g, n=n, key=key, value=value, system=system, wv=beta_row,
+                wk=beta_row * rk_row * entry_row, tail=tail_col, tail_entry=tail_entry))
+            prior = seg_last
+
+    for item, x in zip(items, invert([item["system"] for item in items])):
+        item["pseudo"] = mm_exact_right(x * item["wv"], item["value"])
+        item["key_mix"] = mm_exact_right(x * item["wk"], item["key"])
+    for item in items:
+        g, n = item["g"], item["n"]
+        both = jnp.concatenate([item["key_mix"], item["pseudo"]], axis=1)
+        solved_ref[g, n] = side(both)
+        r2 = dotf(item["key"], side(both * item["tail"]), (((0,), (0,)), ((), ())))
+        r2 = r2[:, : 2 * DK] + r2[:, 2 * DK :]
+        item["pair"] = (item["tail_entry"] * eye - r2[:, :DK], r2[:, DK:])
+
+    def after(later, earlier):
+        joined = mm(later[0], jnp.concatenate(earlier, axis=1))
+        return joined[:, :DK], joined[:, DK:] + later[1]
+
+    totals = [[items[g * blocks + n]["pair"] for n in range(blocks)] for g in range(heads_step)]
+    first, halfway, third = [t[0] for t in totals], [], []
+    halfway = [after(t[1], t[0]) for t in totals]
+    upper = [after(t[3], t[2]) for t in totals]
+    third = [after(t[2], h) for t, h in zip(totals, halfway)]
+    final = [after(u, h) for u, h in zip(upper, halfway)]
+    begin = seg_ref[:, 0:1].astype(F32)
+    last = seg_ref[:, blocks * GROUP - 1 :].astype(F32)
+    ends = jnp.where(iota((8, 2 * DK), 0) == 0, begin, last)
+    for g in range(heads_step):
+        for n, pair in enumerate((first[g], halfway[g], third[g])):
+            prefix_ref[g, n] = side(jnp.concatenate(pair, axis=1))
+        pair_ref[g, :DK, :DK] = final[g][0]
+        pair_ref[g, :DK, DK:] = final[g][1]
+        pair_ref[g, DK:, :] = ends
+
+
+def columns_of(table, blocks):
+    return jnp.concatenate([table, jnp.zeros((ROWS - 8 * blocks, ROWS), F32)], axis=0).T
+
+
+def mm_sided(a, right):
+    width = right.shape[1] // 2
+    r = dotf(side(a), jnp.concatenate([right, right], axis=0))
+    return r[:, :width] + r[:, width:]
+
+
+def query_kernel(heads_step, blocks, q_ref, k_ref, solved_ref, prefix_ref, tab_ref, out_ref, map_ref):
+    qr, qc = iota((GROUP, ROWS), 0), iota((GROUP, ROWS), 1)
+    seen = qc <= 2 * qr + 1
+    items = []
+    for g in range(heads_step):
+        lanes = slice(g * DK, (g + 1) * DK)
+        table = tab_ref[g]
+        columns = columns_of(table, blocks)
         prior = table[2:3, 0:1]
         for n in range(blocks):
             key = k_ref[n * GROUP : (n + 1) * GROUP, :, lanes].reshape(ROWS, DK)
             query = q_ref[n * GROUP : (n + 1) * GROUP, lanes]
-            value = v_ref[n * GROUP : (n + 1) * GROUP, :, lanes].reshape(ROWS, DV)
-            cum_row, beta_row, seg_row = (table[8 * n + i : 8 * n + i + 1] for i in range(3))
-            cum_col, beta_col, seg_col = (columns[:, 8 * n + i : 8 * n + i + 1] for i in range(3))
+            cum_row, seg_row, rk_row = (table[8 * n + i : 8 * n + i + 1] for i in (0, 2, 5))
             cum_q, seg_q = (columns[:GROUP, 8 * n + i : 8 * n + i + 1] for i in (3, 4))
-            cum_last, seg_last = cum_row[:, ROWS - 1 :], seg_row[:, ROWS - 1 :]
-            gram = dotf(jnp.concatenate([key, query], axis=0), key, (((1,), (1,)), ((), ())))
-            raw, raw_q = gram[:ROWS], gram[ROWS:]
-            own = jnp.where(diag, raw, 0.0)
-            rk_row = lax.rsqrt(jnp.sum(own, axis=0, keepdims=True) + EPS)
-            rk_col = lax.rsqrt(jnp.sum(own, axis=1, keepdims=True) + EPS)
+            raw = dotf(query, key, (((1,), (1,)), ((), ())))
             query32 = query.astype(F32)
             rq = lax.rsqrt(jnp.sum(query32 * query32, axis=1, keepdims=True) + EPS)
-            grow_row = rk_row * jnp.exp(-cum_row)
-            system = jnp.where(strictly & (seg_col == seg_row), raw, 0.0) * (
-                beta_col * rk_col * jnp.exp(cum_col)) * grow_row
-            scores = jnp.where(seen & (seg_q == seg_row), raw_q, 0.0) * (rq * jnp.exp(cum_q)) * grow_row
-            entry_row = jnp.where(seg_row == prior, jnp.exp(cum_row), 0.0)
+            scores = jnp.where(seen & (seg_q == seg_row), raw, 0.0) * (rq * jnp.exp(cum_q)) * (
+                rk_row * jnp.exp(-cum_row))
             entry_q = jnp.where(seg_q == prior, jnp.exp(cum_q), 0.0)
-            tail_col = jnp.where(seg_col == seg_last, jnp.exp(cum_last - cum_col), 0.0) * rk_col
-            tail_entry = jnp.where(seg_last == prior, jnp.exp(cum_last), 0.0)
-            items.append(dict(
-                g=g, n=n, key=key, value=value, system=system, scores=scores,
-                reach=query32 * (rq * entry_q), wv=beta_row, wk=beta_row * rk_row * entry_row,
-                tail=tail_col, tail_entry=tail_entry))
-            prior = seg_last
-
-    for item, x in zip(items, invert([item["system"] for item in items])):
-        pseudo = mm_exact_right(x * item["wv"], item["value"])
-        key_mix = mm_exact_right(x * item["wk"], item["key"])
-        both = jnp.concatenate([key_mix, pseudo], axis=1)
-        item["both"] = both
-    for item in items:
-        hi, lo = halves(item["both"] * item["tail"])
-        r2 = dotf(item["key"], jnp.concatenate([hi, lo], axis=1), (((0,), (0,)), ((), ())))
-        r2 = r2[:, : 2 * DK] + r2[:, 2 * DK :]
-        item["trans"] = item["tail_entry"] * eye - r2[:, :DK]
-        item["add"] = r2[:, DK:]
-        inner = mm(item["scores"], item["both"])
-        item["reach"] = item["reach"] - inner[:, :DK]
-        item["local"] = inner[:, DK:]
-
-    for n in range(blocks):
-        for g in range(heads_step):
-            item = items[g * blocks + n]
-            rows = slice(n * GROUP, (n + 1) * GROUP)
-            lanes = slice(g * DV, (g + 1) * DV)
-            if n == 0:
-                map_ref[rows, lanes] = item["reach"]
-                out_ref[rows, lanes] = item["local"]
-                item["prefix"] = jnp.concatenate([item["trans"], item["add"]], axis=1)
-            else:
-                prefix = items[g * blocks + n - 1]["prefix"]
-                joined = mm(jnp.concatenate([item["reach"], item["trans"]], axis=0), prefix)
-                map_ref[rows, lanes] = joined[:GROUP, :DK]
-                out_ref[rows, lanes] = item["local"] + joined[:GROUP, DK:]
-                item["prefix"] = jnp.concatenate(
-                    [joined[GROUP:, :DK], joined[GROUP:, DK:] + item["add"]], axis=1)
-            if n == blocks - 1:
-                pair_ref[g, :DK, :] = item["prefix"]
-    first = seg_ref[:, 0:1].astype(F32)
-    last = seg_ref[:, blocks * GROUP - 1 :].astype(F32)
-    ends = jnp.where(iota((8, 2 * DK), 0) == 0, first, last)
-    for g in range(heads_step):
-        pair_ref[g, DK:, :] = ends
-
-
-def local_stage(queries, keys, values, betas, log_decay, segment):
-    tok, heads = queries.shape[0], betas.shape[1]
+            items.append((g, n, query32 * (rq * entry_q), mm_sided(scores, solved_ref[g, n])))
+            prior = seg_row[:, ROWS - 1 :]
+    for g, n, entering, inner in items:
+        rows = slice(n * GROUP, (n + 1) * GROUP)
+        lanes = slice(g * DV, (g + 1) * DV)
+        reach, local = entering - inner[:, :DK], inner[:, DK:]
+        if n:
+            joined = mm_sided(reach, prefix_ref[g, n - 1])
+            reach, local = joined[:, :DK], local + joined[:, DK:]
+        map_ref[rows, lanes] = reach
+        out_ref[rows, lanes] = local
+
+
+KEY_STEP = 2
+QUERY_STEP = 2
+
+
+def key_stage(keys, values, betas, log_decay, segment, step=None):
+    tok, heads = keys.shape[0], betas.shape[1]
     blocks = tok // GROUP
-    step = 1
-    body = lambda *refs: local_kernel(step, blocks, *refs)
+    assert blocks == 4
+    step = step or KEY_STEP
+    body = lambda *refs: key_kernel(step, blocks, *refs)
+    return pl.pallas_call(
+        body,
+        grid=(heads // step,),
+        in_specs=[
+            pl.BlockSpec((tok, 2, step * DK), lambda h: (0, 0, h)),
+            pl.BlockSpec((tok, 2, step * DV), lambda h: (0, 0, h)),
+            pl.BlockSpec((2, heads, tok), lambda h: (0, 0, 0)),
+            pl.BlockSpec((heads, tok), lambda h: (0, 0)),
+            pl.BlockSpec((1, tok), lambda h: (0, 0)),
+        ],
+        out_specs=[
+            pl.BlockSpec((step, DK + 8, DK + DV), lambda h: (h, 0, 0)),
+            pl.BlockSpec((step, blocks, ROWS, 2 * (DK + DV)), lambda h: (h, 0, 0, 0)),
+            pl.BlockSpec((step, blocks - 1, DK, 2 * (DK + DV)), lambda h: (h, 0, 0, 0)),
+            pl.BlockSpec((heads, 8 * blocks, ROWS), lambda h: (0, 0, 0)),
+        ],
+        out_shape=[
+            jax.ShapeDtypeStruct((heads, DK + 8, DK + DV), F32),
+            jax.ShapeDtypeStruct((heads, blocks, ROWS, 2 * (DK + DV)), BF16),
+            jax.ShapeDtypeStruct((heads, blocks - 1, DK, 2 * (DK + DV)), BF16),
+            jax.ShapeDtypeStruct((heads, 8 * blocks, ROWS), F32),
+        ],
+        compiler_params=pltpu.CompilerParams(dimension_semantics=("arbitrary",)),
+        name="key_stage",
+    )(keys, values, betas, log_decay, segment.reshape(1, tok))
+
+
+def query_stage(queries, keys, solved, prefix, table, step=None):
+    tok = queries.shape[0]
+    heads, blocks = solved.shape[:2]
+    step = step or QUERY_STEP
+    body = lambda *refs: query_kernel(step, blocks, *refs)
     return pl.pallas_call(
         body,
         grid=(heads // step,),
         in_specs=[
             pl.BlockSpec((tok, step * DK), lambda h: (0, h)),
             pl.BlockSpec((tok, 2, step * DK), lambda h: (0, 0, h)),
-            pl.BlockSpec((tok, 2, step * DV), lambda h: (0, 0, h)),
-            pl.BlockSpec((2, heads, tok), lambda h: (0, 0, 0)),
-            pl.BlockSpec((heads, tok), lambda h: (0, 0)),
-            pl.BlockSpec((1, tok), lambda h: (0, 0)),
+            pl.BlockSpec((step, blocks, ROWS, 2 * (DK + DV)), lambda h: (h, 0, 0, 0)),
+            pl.BlockSpec((step, blocks - 1, DK, 2 * (DK + DV)), lambda h: (h, 0, 0, 0)),
+            pl.BlockSpec((step, 8 * blocks, ROWS), lambda h: (h, 0, 0)),
         ],
         out_specs=[
-            pl.BlockSpec((step, DK + 8, DK + DV), lambda h: (h, 0, 0)),
             pl.BlockSpec((tok, step * DV), lambda h: (0, h)),
             pl.BlockSpec((tok, step * DK), lambda h: (0, h)),
         ],
         out_shape=[
-            jax.ShapeDtypeStruct((heads, DK + 8, DK + DV), F32),
             jax.ShapeDtypeStruct((tok, heads * DV), F32),
             jax.ShapeDtypeStruct((tok, heads * DK), F32),
         ],
-        scratch_shapes=[pltpu.VMEM((heads, 8 * blocks, ROWS), F32)],
         compiler_params=pltpu.CompilerParams(dimension_semantics=("arbitrary",)),
-        name="local_stage",
-    )(queries, keys, values, betas, log_decay, segment.reshape(1, tok))
+        name="query_stage",
+    )(queries, keys, solved, prefix, table)
 
 
 def prefix_kernel(in_ref, ex_ref, end_ref):
@@ -295,6 +372,34 @@
     )(place, normed, weight)
 
 
+def sides_kernel(pick_ref, normed_ref, next_w_ref, last_w_ref, nb_ref, lt_ref, nt_ref, lb_ref):
+    half = nb_ref.shape[0]
+    top, bottom = normed_ref[:half, :], normed_ref[half:, :]
+    nb_ref[...] = dotf(bottom, next_w_ref[...])
+    lt_ref[...] = dotf(top, last_w_ref[...])
+    nt_ref[...] = dotf(top, next_w_ref[...])
+    lb_ref[...] = dotf(bottom, last_w_ref[...])
+
+
+def side_tiles(places, normed, weight, width):
+    tok, feats = normed.shape
+    steps = 4
+    cols = width // steps
+    part = jax.ShapeDtypeStruct((tok // 2, width), F32)
+    out = pl.BlockSpec((tok // 2, cols), lambda i, at: (0, i))
+    return pl.pallas_call(
+        sides_kernel,
+        grid_spec=pltpu.PrefetchScalarGridSpec(
+            num_scalar_prefetch=1, grid=(steps,),
+            in_specs=[whole(tok, feats),
+                      pl.BlockSpec((feats, cols), lambda i, at: (0, steps * at[0] + i)),
+                      pl.BlockSpec((feats, cols), lambda i, at: (0, steps * at[1] + i))],
+            out_specs=[out] * 4),
+        out_shape=[part] * 4,
+        name="side_tiles",
+    )(places, normed, weight, weight)
+
+
 def summed_output(local, mapped, states, gain, out_weight):
     count = lax.axis_size("head")
     assert count == 4
@@ -302,13 +407,13 @@
     width = out_weight.shape[1] // count
     rise = [(i, (i + 1) % count) for i in range(count)]
     fall = [(i, (i - 1) % count) for i in range(count)]
-    at = lambda step: ((mine + step) % count).astype(jnp.int32).reshape(1)
+    at = lambda step: ((mine + step) & (count - 1)).astype(jnp.int32).reshape(1)
     up = lambda x: lax.ppermute(x, "head", rise)
     down = lambda x: lax.ppermute(x, "head", fall)
     normed, far_top, far_bottom = far_tile(at(2), local, mapped, states, gain, out_weight, width)
     got_top, got_bottom = up(far_top), down(far_bottom)
-    next_top, next_bottom = one_tile(at(1), normed, out_weight, width, "next_tile")
-    last_top, last_bottom = one_tile(at(3), normed, out_weight, width, "last_tile")
+    next_bottom, last_top, next_top, last_bottom = side_tiles(
+        jnp.concatenate([at(1), at(3)]), normed, out_weight, width)
     side_bottom, side_top = up(next_bottom), down(last_top)
     got_top, got_bottom = up(next_top + got_top), down(last_bottom + got_bottom)
     own_top, own_bottom = one_tile(at(0), normed, out_weight, width, "own_tile")
@@ -322,10 +427,15 @@
     span = DOCUMENT_LIMIT // tok
     assert span == heads and devices % span == 0
     groups = [list(range(i, i + span)) for i in range(0, devices, span)]
-    pair, local, mapped = local_stage(queries, keys, values, betas, log_decay, segment)
+    vmem = pl.BlockSpec(memory_space=pltpu.VMEM)
+    pair, solved, prefix, table = key_stage(keys, values, betas, log_decay, segment)
+    local, mapped = query_stage(queries, keys, solved, prefix, table)
     mine = lax.all_to_all(pair, "ctx", 0, 0, axis_index_groups=groups)
+    mine, local, mapped = lax.optimization_barrier((mine, local, mapped))
     exclusive, end = pl.pallas_call(
         prefix_kernel,
+        in_specs=[vmem],
+        out_specs=[vmem, vmem],
         out_shape=[jax.ShapeDtypeStruct((span, DK, DK + DV), F32),
                    jax.ShapeDtypeStruct((DK + 8, DV), F32)],
         name="prefix_stage",
@@ -333,6 +443,8 @@
     end = lax.ppermute(end, "ctx", [(i, i + span) for i in range(devices - span)])
     states = pl.pallas_call(
         incoming_kernel,
+        in_specs=[vmem, vmem, vmem],
+        out_specs=vmem,
         out_shape=jax.ShapeDtypeStruct((span, DK, DV), F32),
         name="incoming_stage",
     )(mine, exclusive, end)

time: 128 us -> 118 us (0.922)
  blocking collectives: 21.1 us -> 0 us
  waiting for transfers between devices: 34.9 us -> 42.8 us
  Pallas kernels: 51.4 us -> 46.6 us
  other arithmetic: 2.19 us -> 5.88 us
  starting transfers between devices: 16.1 us -> 19.4 us
    all_to_all x1 -> x0, blocking collectives: 21.1 us -> none  [shards(): mine = lax.all_to_all(pair, 'ctx', 0, 0, axis_index_groups=groups)]
    all_to_all x0 -> x1, waiting for transfers between devices: none -> 8.2 us  [shards(): mine = lax.all_to_all(pair, 'ctx', 0, 0, axis_index_groups=groups)]
    pallas_call x3 -> x1, Pallas kernels: 9.07 us -> 3 us  [one_tile(): pl.pallas_call(tile_kernel, grid_spec=pltpu.PrefetchScalarGridSpec(num_sc...]
    all_to_all x0 -> x1, starting transfers between devices: none -> 4.3 us  [shards(): mine = lax.all_to_all(pair, 'ctx', 0, 0, axis_index_groups=groups)]
    pallas_call x3 -> x5, Pallas kernels: 38 us -> 39.3 us  [the longest x1 19.5 us: key_stage(): pl.pallas_call(body, grid=(heads // step,), in_specs=[pl.BlockSpec((tok,...]
  transfers between devices with their start and end apart: 8 -> 9, of which waited for: 6 -> 7; matrix products, arithmetic and copies ran while one was open for 1% -> 3% of each run, Pallas kernels for 7% -> 15%
where the time goes in v3:
time: 118 us; the launch traced here: 117 us
  Pallas kernels  46.6 us (39%)
  waiting for transfers between devices  42.8 us (36%)
  starting transfers between devices  19.4 us (16%)
  other arithmetic  5.88 us (5%)
  local copies, waits for them, and re-layouts  2.43 us (2%)
    pallas_call x1, Pallas kernels, key_stage(): pl.pallas_call(body, grid=(heads // step,), in_specs=[pl.BlockSpec((tok,...  19.5 us
    ppermute x3, waiting for transfers between devices, summed_output(): up = lambda x: lax.ppermute(x, 'head', rise)  15.7 us
    all_to_all x1, waiting for transfers between devices, shards(): states = lax.all_to_all(states, 'ctx', 0, 0, axis_index_groups=groups)  10.2 us
    pallas_call x1, Pallas kernels, query_stage(): pl.pallas_call(body, grid=(heads // step,), in_specs=[pl.BlockSpec((tok,...  8.43 us
    all_to_all x1, waiting for transfers between devices, shards(): mine = lax.all_to_all(pair, 'ctx', 0, 0, axis_index_groups=groups)  8.2 us
    pallas_call x1, Pallas kernels, side_tiles(): pl.pallas_call(sides_kernel, grid_spec=pltpu.PrefetchScalarGridSpec(num_s...  5.67 us
    ppermute x3, starting transfers between devices, summed_output(): down = lambda x: lax.ppermute(x, 'head', fall)  5.2 us
    ppermute x1, waiting for transfers between devices, shards(): lax.ppermute(end, 'ctx', [(i, i + span) for i in range(devices - span)])  4.69 us
  transfers between devices with their start and end apart: 9, of which 7 were waited for; matrix products, arithmetic and copies ran while one was open for 3% of the time, Pallas kernels for 15%

profile of v3, /device:TPU:128, one launch (start us, length us, event | category | flops | bytes accessed | tf_op | source)
XLA Modules:
  0.0 117.3 jit_solution(1402905363520575055)
XLA Ops:
  0.0 19.5 %key_stage.1 = (f32[8,136,256]{2,1,0:T(8,128)}, bf16[8,4,128,512]{3,2,1,0:T(8,128)(2,1)}, bf16[8,3,128,512]{3,2,1,0:T(8,128)(2,1)}, f32[8,32,128]{2,1,0:T(8,128)}) custom-call(bf16[256,2,1024]{2,1,0:T(2,128)(2,1)} %refs_1_.3, bf16[256,2,1024]{2,1,0:T(2,128)(2,1)} %refs_1_.2, f32[2,8,256]{2,1,0:T(8,128)} %refs_2_.1, f32[8,256]{1,0:T(8,128)} %refs_3_.1, ...), custom_call_target="tpu_custom_call" | custom-call | tf_op jit(solution)/shard_map/key_stage/pallas_call | solution.py:232
  19.5 4.3 %all-to-all-start = ((f32[8,136,256]{2,1,0:T(8,128)}), f32[8,136,256]{2,1,0:T(8,128)S(1)}, u32[]{:S(2)}, u32[]{:S(2)}) async-start(f32[8,136,256]{2,1,0:T(8,128)} %get-tuple-element.25), calls=%async_computation | async-start | bytes 2228224 | tf_op jit(solution)/shard_map/all_to_all | solution.py:433
  23.8 8.4 %query_stage.1 = (f32[256,1024]{1,0:T(8,128)}, f32[256,1024]{1,0:T(8,128)}) custom-call(bf16[256,1024]{1,0:T(8,128)(2,1)} %refs_0_.3, bf16[256,2,1024]{2,1,0:T(2,128)(2,1)} %refs_1_.3, bf16[8,4,128,512]{3,2,1,0:T(8,128)(2,1)} %get-tuple-element.26.refs_2_, bf16[8,3,128,512]{3,2,1,0:T(8,128)(2,1)} %get-tuple-element.27.refs_3_, ...), custom_call_target="tpu_custom_call" | custom-call | tf_op jit(solution)/shard_map/query_stage/pallas_call | solution.py:264
  32.3 8.2 %all-to-all-done.in_ref = f32[8,136,256]{2,1,0:T(8,128)S(1)} async-done(((f32[8,136,256]{2,1,0:T(8,128)}), f32[8,136,256]{2,1,0:T(8,128)S(1)}, u32[]{:S(2)}, u32[]{:S(2)}) %all-to-all-start) | async-done | bytes 1114144 | tf_op jit(solution)/shard_map/all_to_all | solution.py:433
  40.5 0.0 copy-start
  40.5 1.0 copy-done
  41.5 2.9 %prefix_stage.1 = (f32[8,128,256]{2,1,0:T(8,128)}, f32[136,128]{1,0:T(8,128)}) custom-call(f32[8,136,256]{2,1,0:T(8,128)} %copy-done), custom_call_target="tpu_custom_call" | custom-call | tf_op jit(solution)/shard_map/prefix_stage/pallas_call | solution.py:435
  44.4 2.9 %collective-permute-start = (f32[136,128]{1,0:T(8,128)}, f32[136,128]{1,0:T(8,128)S(1)}, u32[]{:S(2)}, u32[]{:S(2)}) collective-permute-start(f32[136,128]{1,0:T(8,128)} %get-tuple-element.35), channel_id=1, source_target_pairs={{0,32},{4,36},{8,40},{12,44},{16,48},{20,52},{24,56},{28,60},{32,6... | collective-permute-start | bytes 208904 | tf_op jit(solution)/shard_map/ppermute | solution.py:443
  47.3 4.7 %collective-permute-done.end_ref = f32[136,128]{1,0:T(8,128)S(1)} collective-permute-done((f32[136,128]{1,0:T(8,128)}, f32[136,128]{1,0:T(8,128)S(1)}, u32[]{:S(2)}, u32[]{:S(2)}) %collective-permute-start) | collective-permute-done | bytes 69664 | tf_op jit(solution)/shard_map/ppermute | solution.py:443
  52.0 0.0 copy-start.2
  52.0 0.6 copy-done.2
  52.7 2.7 %incoming_stage.1 = f32[8,128,128]{2,1,0:T(8,128)} custom-call(f32[8,136,256]{2,1,0:T(8,128)} %copy-done, f32[8,128,256]{2,1,0:T(8,128)} %get-tuple-element.34.ex_ref, f32[136,128]{1,0:T(8,128)} %copy-done.2), custom_call_target="tpu_custom_call" | custom-call | tf_op jit(solution)/shard_map/incoming_stage/pallas_call | solution.py:444
  55.3 3.5 %all-to-all-start.1 = ((f32[8,128,128]{2,1,0:T(8,128)}), f32[8,128,128]{2,1,0:T(8,128)S(1)}, u32[]{:S(2)}, u32[]{:S(2)}) async-start(f32[8,128,128]{2,1,0:T(8,128)} %incoming_stage.1), calls=%async_computation.1 | async-start | bytes 1048576 | tf_op jit(solution)/shard_map/all_to_all | solution.py:451
  58.8 10.2 %all-to-all-done.1.state_ref = f32[8,128,128]{2,1,0:T(8,128)S(1)} async-done(((f32[8,128,128]{2,1,0:T(8,128)}), f32[8,128,128]{2,1,0:T(8,128)S(1)}, u32[]{:S(2)}, u32[]{:S(2)}) %all-to-all-start.1) | async-done | bytes 524320 | tf_op jit(solution)/shard_map/all_to_all | solution.py:451
  69.1 0.0 copy-start.1
  69.1 0.8 copy-done.1
  69.9 4.4 %far_tile.1 = (bf16[256,1024]{1,0:T(8,128)(2,1)}, f32[128,1024]{1,0:T(8,128)}, f32[128,1024]{1,0:T(8,128)}) custom-call(s32[1]{0:T(128)} %bitcast.1.pick_ref, f32[256,1024]{1,0:T(8,128)} %get-tuple-element.31.local_ref, f32[256,1024]{1,0:T(8,128)} %get-tuple-element.32.map_ref, f32[8,128,128]{2,1,0:T(8,128)} %copy-done.1, f32[1,1024]{1,0:T(1,128)} %bitcast.6, ...), custom_call_target="tpu_custom_call" | custom-call | tf_op jit(solution)/shard_map/far_tile/pallas_call | solution.py:347
  74.2 1.6 %collective-permute-start.2 = (f32[128,1024]{1,0:T(8,128)}, f32[128,1024]{1,0:T(8,128)S(1)}, u32[]{:S(2)}, u32[]{:S(2)}) collective-permute-start(f32[128,1024]{1,0:T(8,128)} %get-tuple-element.40), channel_id=1, source_target_pairs={{0,1},{1,2},{2,3},{3,0},{4,5},{5,6},{6,7},{7,4},{8,9},{9,10},{10,1... | collective-permute-start | bytes 1572872 | tf_op jit(solution)/shard_map/ppermute | solution.py:411
  75.8 1.7 %collective-permute-start.5 = (f32[128,1024]{1,0:T(8,128)}, f32[128,1024]{1,0:T(8,128)S(1)}, u32[]{:S(2)}, u32[]{:S(2)}) collective-permute-start(f32[128,1024]{1,0:T(8,128)} %get-tuple-element.44), channel_id=1, source_target_pairs={{0,3},{1,0},{2,1},{3,2},{4,7},{5,4},{6,5},{7,6},{8,11},{9,8},{10,9... | collective-permute-start | bytes 1572872 | tf_op jit(solution)/shard_map/ppermute | solution.py:412
  77.5 0.6 pad_add_fusion.pick_ref
  78.1 5.7 %side_tiles.1 = (f32[128,1024]{1,0:T(8,128)}, f32[128,1024]{1,0:T(8,128)}, f32[128,1024]{1,0:T(8,128)}, f32[128,1024]{1,0:T(8,128)}) custom-call(s32[2]{0:T(128)} %pad_add_fusion.pick_ref, bf16[256,1024]{1,0:T(8,128)(2,1)} %get-tuple-element.36.normed_ref, bf16[1024,4096]{1,0:T(8,128)(2,1)} %last_w_ref.1, bf16[1024,4096]{1,0:T(8,128)(2,1)} %last_w_ref.1), custom_call_target="tpu_custom_call" | custom-call | tf_op jit(solution)/shard_map/side_tiles/pallas_call | solution.py:390
  83.7 1.8 %collective-permute-start.1 = (f32[128,1024]{1,0:T(8,128)}, f32[128,1024]{1,0:T(8,128)S(1)}, u32[]{:S(2)}, u32[]{:S(2)}) collective-permute-start(f32[128,1024]{1,0:T(8,128)} %get-tuple-element.38), channel_id=1, source_target_pairs={{0,3},{1,0},{2,1},{3,2},{4,7},{5,4},{6,5},{7,6},{8,11},{9,8},{10,9... | collective-permute-start | bytes 1572872 | tf_op jit(solution)/shard_map/ppermute | solution.py:412
  85.5 3.6 %collective-permute-done.2 = f32[128,1024]{1,0:T(8,128)S(1)} collective-permute-done((f32[128,1024]{1,0:T(8,128)}, f32[128,1024]{1,0:T(8,128)S(1)}, u32[]{:S(2)}, u32[]{:S(2)}) %collective-permute-start.2) | collective-permute-done | bytes 524320 | tf_op jit(solution)/shard_map/ppermute | solution.py:411
  89.1 1.1 add.31
  90.2 0.4 collective-permute-start.3
  90.6 1.6 %collective-permute-start.4 = (f32[128,1024]{1,0:T(8,128)}, f32[128,1024]{1,0:T(8,128)S(1)}, u32[]{:S(2)}, u32[]{:S(2)}) collective-permute-start(f32[128,1024]{1,0:T(8,128)} %get-tuple-element.42), channel_id=1, source_target_pairs={{0,1},{1,2},{2,3},{3,0},{4,5},{5,6},{6,7},{7,4},{8,9},{9,10},{10,1... | collective-permute-start | bytes 1572872 | tf_op jit(solution)/shard_map/ppermute | solution.py:411
  92.2 0.0 collective-permute-done.5
  92.2 1.1 add.34
  93.3 1.7 %collective-permute-start.6 = (f32[128,1024]{1,0:T(8,128)S(1)}, f32[128,1024]{1,0:T(8,128)S(1)}, u32[]{:S(2)}, u32[]{:S(2)}) collective-permute-start(f32[128,1024]{1,0:T(8,128)S(1)} %add.34), channel_id=1, source_target_pairs={{0,3},{1,0},{2,1},{3,2},{4,7},{5,4},{6,5},{7,6},{8,11},{9,8},{10,9... | collective-permute-start | bytes 1572872 | tf_op jit(solution)/shard_map/ppermute | solution.py:412
  95.0 3.0 %own_tile.1 = (f32[128,1024]{1,0:T(8,128)}, f32[128,1024]{1,0:T(8,128)}) custom-call(s32[1]{0:T(128)} %bitcast.pick_ref, bf16[256,1024]{1,0:T(8,128)(2,1)} %get-tuple-element.36.normed_ref, bf16[1024,4096]{1,0:T(8,128)(2,1)} %last_w_ref.1), custom_call_target="tpu_custom_call" | custom-call | tf_op jit(solution)/shard_map/own_tile/pallas_call | solution.py:364
  98.0 4.1 %collective-permute-done.1 = f32[128,1024]{1,0:T(8,128)S(1)} collective-permute-done((f32[128,1024]{1,0:T(8,128)}, f32[128,1024]{1,0:T(8,128)S(1)}, u32[]{:S(2)}, u32[]{:S(2)}) %collective-permute-start.1) | collective-permute-done | bytes 524320 | tf_op jit(solution)/shard_map/ppermute | solution.py:412
  102.1 4.2 %collective-permute-done.3 = f32[128,1024]{1,0:T(8,128)S(1)} collective-permute-done((f32[128,1024]{1,0:T(8,128)S(1)}, f32[128,1024]{1,0:T(8,128)S(1)}, u32[]{:S(2)}, u32[]{:S(2)}) %collective-permute-start.3) | collective-permute-done | bytes 524320 | tf_op jit(solution)/shard_map/ppermute | solution.py:411
  106.3 1.1 add_convert_fusion.1
  107.4 7.9 %collective-permute-done.4 = f32[128,1024]{1,0:T(8,128)S(1)} collective-permute-done((f32[128,1024]{1,0:T(8,128)}, f32[128,1024]{1,0:T(8,128)S(1)}, u32[]{:S(2)}, u32[]{:S(2)}) %collective-permute-start.4) | collective-permute-done | bytes 524320 | tf_op jit(solution)/shard_map/ppermute | solution.py:411
  115.3 0.0 collective-permute-done.6
  115.3 1.1 add_convert_fusion
  116.4 0.8 pad_maximum_fusion
Async XLA Ops:
  19.5 20.9 %all-to-all-start = ((f32[8,136,256]{2,1,0:T(8,128)}), f32[8,136,256]{2,1,0:T(8,128)S(1)}, u32[]{:S(2)}, u32[]{:S(2)}) async-start(f32[8,136,256]{2,1,0:T(8,128)} %get-tuple-element.25), calls=%async_computation | async-start | bytes 2228224 | tf_op jit(solution)/shard_map/all_to_all | solution.py:433
  40.5 1.0 copy-start
  44.4 7.6 %collective-permute-start = (f32[136,128]{1,0:T(8,128)}, f32[136,128]{1,0:T(8,128)S(1)}, u32[]{:S(2)}, u32[]{:S(2)}) collective-permute-start(f32[136,128]{1,0:T(8,128)} %get-tuple-element.35), channel_id=1, source_target_pairs={{0,32},{4,36},{8,40},{12,44},{16,48},{20,52},{24,56},{28,60},{32,6... | collective-permute-start | bytes 208904 | tf_op jit(solution)/shard_map/ppermute | solution.py:443
  52.0 0.6 copy-start.2
  55.3 13.7 %all-to-all-start.1 = ((f32[8,128,128]{2,1,0:T(8,128)}), f32[8,128,128]{2,1,0:T(8,128)S(1)}, u32[]{:S(2)}, u32[]{:S(2)}) async-start(f32[8,128,128]{2,1,0:T(8,128)} %incoming_stage.1), calls=%async_computation.1 | async-start | bytes 1048576 | tf_op jit(solution)/shard_map/all_to_all | solution.py:451
  69.1 0.8 copy-start.1
  74.2 14.9 %collective-permute-start.2 = (f32[128,1024]{1,0:T(8,128)}, f32[128,1024]{1,0:T(8,128)S(1)}, u32[]{:S(2)}, u32[]{:S(2)}) collective-permute-start(f32[128,1024]{1,0:T(8,128)} %get-tuple-element.40), channel_id=1, source_target_pairs={{0,1},{1,2},{2,3},{3,0},{4,5},{5,6},{6,7},{7,4},{8,9},{9,10},{10,1... | collective-permute-start | bytes 1572872 | tf_op jit(solution)/shard_map/ppermute | solution.py:411
  75.8 16.3 %collective-permute-start.5 = (f32[128,1024]{1,0:T(8,128)}, f32[128,1024]{1,0:T(8,128)S(1)}, u32[]{:S(2)}, u32[]{:S(2)}) collective-permute-start(f32[128,1024]{1,0:T(8,128)} %get-tuple-element.44), channel_id=1, source_target_pairs={{0,3},{1,0},{2,1},{3,2},{4,7},{5,4},{6,5},{7,6},{8,11},{9,8},{10,9... | collective-permute-start | bytes 1572872 | tf_op jit(solution)/shard_map/ppermute | solution.py:412
  83.7 18.3 %collective-permute-start.1 = (f32[128,1024]{1,0:T(8,128)}, f32[128,1024]{1,0:T(8,128)S(1)}, u32[]{:S(2)}, u32[]{:S(2)}) collective-permute-start(f32[128,1024]{1,0:T(8,128)} %get-tuple-element.38), channel_id=1, source_target_pairs={{0,3},{1,0},{2,1},{3,2},{4,7},{5,4},{6,5},{7,6},{8,11},{9,8},{10,9... | collective-permute-start | bytes 1572872 | tf_op jit(solution)/shard_map/ppermute | solution.py:412
  90.2 16.1 %collective-permute-start.3 = (f32[128,1024]{1,0:T(8,128)S(1)}, f32[128,1024]{1,0:T(8,128)S(1)}, u32[]{:S(2)}, u32[]{:S(2)}) collective-permute-start(f32[128,1024]{1,0:T(8,128)S(1)} %add.31), channel_id=1, source_target_pairs={{0,1},{1,2},{2,3},{3,0},{4,5},{5,6},{6,7},{7,4},{8,9},{9,10},{10,1... | collective-permute-start | bytes 1572872 | tf_op jit(solution)/shard_map/ppermute | solution.py:411
  90.6 24.7 %collective-permute-start.4 = (f32[128,1024]{1,0:T(8,128)}, f32[128,1024]{1,0:T(8,128)S(1)}, u32[]{:S(2)}, u32[]{:S(2)}) collective-permute-start(f32[128,1024]{1,0:T(8,128)} %get-tuple-element.42), channel_id=1, source_target_pairs={{0,1},{1,2},{2,3},{3,0},{4,5},{5,6},{6,7},{7,4},{8,9},{9,10},{10,1... | collective-permute-start | bytes 1572872 | tf_op jit(solution)/shard_map/ppermute | solution.py:411
  93.3 22.0 %collective-permute-start.6 = (f32[128,1024]{1,0:T(8,128)S(1)}, f32[128,1024]{1,0:T(8,128)S(1)}, u32[]{:S(2)}, u32[]{:S(2)}) collective-permute-start(f32[128,1024]{1,0:T(8,128)S(1)} %add.34), channel_id=1, source_target_pairs={{0,3},{1,0},{2,1},{3,2},{4,7},{5,4},{6,5},{7,6},{8,11},{9,8},{10,9... | collective-permute-start | bytes 1572872 | tf_op jit(solution)/shard_map/ppermute | solution.py:412

commit v4 on v3

--- a/solution.py
+++ b/solution.py
@@ -4,6 +4,7 @@
 from jax.experimental import pallas as pl
 from jax.experimental.pallas import tpu as pltpu
 from jax.sharding import PartitionSpec as P
+
 
 DK = 128
 DV = 128
@@ -174,6 +175,14 @@
         pair_ref[g, :DK, :DK] = final[g][0]
         pair_ref[g, :DK, DK:] = final[g][1]
         pair_ref[g, DK:, :] = ends
+
+
+def resident():
+    return pl.BlockSpec(memory_space=pltpu.VMEM)
+
+
+def held(x):
+    return pltpu.with_memory_space_constraint(x, pltpu.VMEM)
 
 
 def columns_of(table, blocks):
@@ -284,7 +293,7 @@
     )(queries, keys, solved, prefix, table)
 
 
-def prefix_kernel(in_ref, ex_ref, end_ref):
+def prefix_kernel(in_ref, ex_ref, end_ref, ends_ref):
     count = in_ref.shape[0]
     flags = [jnp.where(in_ref[i, DK : DK + 1, :] == in_ref[i - 1, DK + 1 : DK + 2, :], 1.0, 0.0)
              for i in range(1, count)]
@@ -309,10 +318,11 @@
         ex_ref[i, :, DK:] = adds[i - 1] * flags[i - 1][:, DK:]
     end_ref[:DK, :] = adds[count - 1]
     end_ref[DK:, :] = in_ref[count - 1, DK:, :DV]
-
-
-def incoming_kernel(in_ref, ex_ref, end_ref, out_ref):
-    flag = jnp.where(in_ref[0, DK : DK + 1, :DV] == end_ref[DK + 1 : DK + 2, :], 1.0, 0.0)
+    ends_ref[...] = in_ref[0, DK:, :DV]
+
+
+def incoming_kernel(ends_ref, ex_ref, end_ref, out_ref):
+    flag = jnp.where(ends_ref[0:1, :] == end_ref[DK + 1 : DK + 2, :], 1.0, 0.0)
     state = end_ref[:DK, :] * flag
     for i in range(ex_ref.shape[0]):
         out_ref[i] = mm(ex_ref[i, :, :DK], state) + ex_ref[i, :, DK:]
@@ -320,11 +330,15 @@
 
 def far_kernel(pick_ref, local_ref, map_ref, state_ref, gain_ref, weight_ref, normed_ref, up_ref, down_ref):
     heads = state_ref.shape[0]
-    for h in range(heads):
-        lanes = slice(h * DV, (h + 1) * DV)
-        attended = local_ref[:, lanes] + mm(map_ref[:, lanes], state_ref[h])
-        mean = jnp.mean(attended * attended, axis=1, keepdims=True)
-        normed_ref[:, lanes] = (attended * lax.rsqrt(mean + EPS) * gain_ref[:, lanes]).astype(BF16)
+
+    @pl.when(pl.program_id(0) == 0)
+    def _():
+        for h in range(heads):
+            lanes = slice(h * DV, (h + 1) * DV)
+            attended = local_ref[:, lanes] + mm(map_ref[:, lanes], state_ref[h])
+            mean = jnp.mean(attended * attended, axis=1, keepdims=True)
+            normed_ref[:, lanes] = (attended * lax.rsqrt(mean + EPS) * gain_ref[:, lanes]).astype(BF16)
+
     half = up_ref.shape[0]
     up_ref[...] = dotf(normed_ref[:half, :], weight_ref[...])
     down_ref[...] = dotf(normed_ref[half:, :], weight_ref[...])
@@ -342,23 +356,42 @@
 
 def far_tile(place, local, mapped, state, gain, weight, width):
     tok, feats = local.shape
-    heads = state.shape[0]
-    part = jax.ShapeDtypeStruct((tok // 2, width), F32)
+    part = pltpu.VMEM((tok // 2, width), F32)
+    steps = 2
+    cols = width // steps
+    out = pl.BlockSpec((tok // 2, cols), lambda i, at: (0, i))
     return pl.pallas_call(
         far_kernel,
         grid_spec=pltpu.PrefetchScalarGridSpec(
-            num_scalar_prefetch=1, grid=(1,),
-            in_specs=[whole(tok, feats), whole(tok, feats), whole(heads, DK, DV), whole(1, feats),
-                      pl.BlockSpec((feats, width), lambda i, at: (0, at[0]))],
-            out_specs=[whole(tok, feats), whole(tok // 2, width), whole(tok // 2, width)]),
+            num_scalar_prefetch=1, grid=(steps,),
+            in_specs=[whole(tok, feats), whole(tok, feats), resident(), whole(1, feats),
+                      pl.BlockSpec((feats, cols), lambda i, at: (0, steps * at[0] + i))],
+            out_specs=[whole(tok, feats), out, out]),
         out_shape=[jax.ShapeDtypeStruct((tok, feats), BF16), part, part],
+        compiler_params=pltpu.CompilerParams(vmem_limit_bytes=57 << 20),
         name="far_tile",
-    )(place, local, mapped, state, gain.reshape(1, feats), weight)
-
-
-def one_tile(place, normed, weight, width, name):
+    )(place, local, mapped, held(state), gain.reshape(1, feats), weight)
+
+
+def join_kernel(nt_ref, gt_ref, lb_ref, gb_ref, top_ref, bottom_ref):
+    top_ref[...] = nt_ref[...] + gt_ref[...]
+    bottom_ref[...] = lb_ref[...] + gb_ref[...]
+
+
+def joined(next_top, got_top, last_bottom, got_bottom):
+    return pl.pallas_call(
+        join_kernel,
+        in_specs=[resident()] * 4,
+        out_specs=[resident()] * 2,
+        out_shape=[pltpu.VMEM(next_top.shape, F32)] * 2,
+        compiler_params=pltpu.CompilerParams(vmem_limit_bytes=57 << 20),
+        name="join_tiles",
+    )(held(next_top), held(got_top), held(last_bottom), held(got_bottom))
+
+
+def one_tile(place, normed, weight, width):
     tok, feats = normed.shape
-    part = jax.ShapeDtypeStruct((tok // 2, width), F32)
+    part = pltpu.VMEM((tok // 2, width), F32)
     cols = width // 2
     out = pl.BlockSpec((tok // 2, cols), lambda i, at: (0, i))
     return pl.pallas_call(
@@ -368,7 +401,7 @@
             in_specs=[whole(tok, feats), pl.BlockSpec((feats, cols), lambda i, at: (0, 2 * at[0] + i))],
             out_specs=[out, out]),
         out_shape=[part, part],
-        name=name,
+        compiler_params=pltpu.CompilerParams(vmem_limit_bytes=57 << 20),
     )(place, normed, weight)
 
 
@@ -395,9 +428,16 @@
                       pl.BlockSpec((feats, cols), lambda i, at: (0, steps * at[0] + i)),
                       pl.BlockSpec((feats, cols), lambda i, at: (0, steps * at[1] + i))],
             out_specs=[out] * 4),
-        out_shape=[part] * 4,
+        out_shape=[part] * 2 + [pltpu.VMEM((tok // 2, width), F32)] * 2,
+        compiler_params=pltpu.CompilerParams(vmem_limit_bytes=57 << 20),
         name="side_tiles",
     )(places, normed, weight, weight)
+
+
+def finish_kernel(ot_ref, st_ref, gt_ref, ob_ref, sb_ref, gb_ref, out_ref):
+    half = ot_ref.shape[0]
+    out_ref[:half, :] = (ot_ref[...] + st_ref[...] + gt_ref[...]).astype(BF16)
+    out_ref[half:, :] = (ob_ref[...] + sb_ref[...] + gb_ref[...]).astype(BF16)
 
 
 def summed_output(local, mapped, states, gain, out_weight):
@@ -414,11 +454,18 @@
     got_top, got_bottom = up(far_top), down(far_bottom)
     next_bottom, last_top, next_top, last_bottom = side_tiles(
         jnp.concatenate([at(1), at(3)]), normed, out_weight, width)
-    side_bottom, side_top = up(next_bottom), down(last_top)
-    got_top, got_bottom = up(next_top + got_top), down(last_bottom + got_bottom)
-    own_top, own_bottom = one_tile(at(0), normed, out_weight, width, "own_tile")
-    return jnp.concatenate([(own_top + side_top + got_top).astype(BF16),
-                            (own_bottom + side_bottom + got_bottom).astype(BF16)], axis=0)
+    side_bottom = up(next_bottom)
+    side_top = down(last_top)
+    next_top, last_bottom = joined(next_top, got_top, last_bottom, got_bottom)
+    got_top, got_bottom = up(next_top), down(last_bottom)
+    own_top, own_bottom = one_tile(at(0), normed, out_weight, width)
+    return pl.pallas_call(
+        finish_kernel,
+        in_specs=[resident()] * 6,
+        out_shape=jax.ShapeDtypeStruct((2 * own_top.shape[0], width), BF16),
+        compiler_params=pltpu.CompilerParams(vmem_limit_bytes=57 << 20),
+        name="finish",
+    )(*map(held, (own_top, side_top, got_top, own_bottom, side_bottom, got_bottom)))
 
 
 def shards(queries, keys, values, betas, log_decay, segment, gain, out_weight):
@@ -427,27 +474,28 @@
     span = DOCUMENT_LIMIT // tok
     assert span == heads and devices % span == 0
     groups = [list(range(i, i + span)) for i in range(0, devices, span)]
-    vmem = pl.BlockSpec(memory_space=pltpu.VMEM)
     pair, solved, prefix, table = key_stage(keys, values, betas, log_decay, segment)
     local, mapped = query_stage(queries, keys, solved, prefix, table)
     mine = lax.all_to_all(pair, "ctx", 0, 0, axis_index_groups=groups)
     mine, local, mapped = lax.optimization_barrier((mine, local, mapped))
-    exclusive, end = pl.pallas_call(
+    exclusive, end, ends = pl.pallas_call(
         prefix_kernel,
-        in_specs=[vmem],
-        out_specs=[vmem, vmem],
-        out_shape=[jax.ShapeDtypeStruct((span, DK, DK + DV), F32),
-                   jax.ShapeDtypeStruct((DK + 8, DV), F32)],
+        in_specs=[resident()],
+        out_specs=[resident(), resident(), resident()],
+        out_shape=[pltpu.VMEM((span, DK, DK + DV), F32), pltpu.VMEM((DK + 8, DV), F32),
+                   pltpu.VMEM((8, DV), F32)],
+        compiler_params=pltpu.CompilerParams(vmem_limit_bytes=57 << 20),
         name="prefix_stage",
-    )(mine)
+    )(held(mine))
     end = lax.ppermute(end, "ctx", [(i, i + span) for i in range(devices - span)])
     states = pl.pallas_call(
         incoming_kernel,
-        in_specs=[vmem, vmem, vmem],
-        out_specs=vmem,
-        out_shape=jax.ShapeDtypeStruct((span, DK, DV), F32),
+        in_specs=[resident(), resident(), resident()],
+        out_specs=resident(),
+        out_shape=pltpu.VMEM((span, DK, DV), F32),
+        compiler_params=pltpu.CompilerParams(vmem_limit_bytes=57 << 20),
         name="incoming_stage",
-    )(mine, exclusive, end)
+    )(held(ends), held(exclusive), held(end))
     states = lax.all_to_all(states, "ctx", 0, 0, axis_index_groups=groups)
     return summed_output(local, mapped, states, gain, out_weight)
 

time: 118 us -> 106 us (0.90)
  other arithmetic: 5.88 us -> 0.65 us
  Pallas kernels: 46.6 us -> 42.7 us
  local copies, waits for them, and re-layouts: 2.43 us -> 0 us
    pallas_call x2 -> x4, Pallas kernels: 5.62 us -> 2.9 us  [the longest x1 1.12 us: shards(): pl.pallas_call(incoming_kernel, in_specs=[resident(), resident(), residen...]
    unnamed x6 -> x0, local copies, waits for them, and re-layouts: 2.43 us -> none
    ppermute x3, waiting for transfers between devices: 4.06 us -> 6.43 us  [summed_output(): down = lambda x: lax.ppermute(x, 'head', fall)]
    convert_element_type x2 -> x0, other arithmetic: 2.27 us -> none  [the longest x1 1.14 us: summed_output(): (own_bottom + side_bottom + got_bottom).astype(BF16)]
    add x2 -> x0, other arithmetic: 2.19 us -> none  [the longest x1 1.1 us: summed_output(): last_bottom + got_bottom]
    ppermute x3, waiting for transfers between devices: 15.7 us -> 13.6 us  [summed_output(): up = lambda x: lax.ppermute(x, 'head', rise)]
  transfers between devices with their start and end apart: 9 -> 9, of which waited for: 7 -> 7; matrix products, arithmetic and copies ran while one was open for 3% -> 1% of each run, Pallas kernels for 15% -> 15%
where the time goes in v4:
time: 106 us
  waiting for transfers between devices  42.9 us (40%)
  Pallas kernels  42.7 us (40%)
  starting transfers between devices  19.3 us (18%)
    pallas_call x1, Pallas kernels, key_stage(): pl.pallas_call(body, grid=(heads // step,), in_specs=[pl.BlockSpec((tok,...  19.5 us
    ppermute x3, waiting for transfers between devices, summed_output(): up = lambda x: lax.ppermute(x, 'head', rise)  13.6 us
    all_to_all x1, waiting for transfers between devices, shards(): states = lax.all_to_all(states, 'ctx', 0, 0, axis_index_groups=groups)  10.2 us
    pallas_call x1, Pallas kernels, query_stage(): pl.pallas_call(body, grid=(heads // step,), in_specs=[pl.BlockSpec((tok,...  8.46 us
    all_to_all x1, waiting for transfers between devices, shards(): mine = lax.all_to_all(pair, 'ctx', 0, 0, axis_index_groups=groups)  8.18 us
    ppermute x3, waiting for transfers between devices, summed_output(): down = lambda x: lax.ppermute(x, 'head', fall)  6.43 us
    pallas_call x1, Pallas kernels, side_tiles(): pl.pallas_call(sides_kernel, grid_spec=pltpu.PrefetchScalarGridSpec(num_s...  5.45 us
    ppermute x3, starting transfers between devices, summed_output(): down = lambda x: lax.ppermute(x, 'head', fall)  5.1 us
  transfers between devices with their start and end apart: 9, of which 7 were waited for; matrix products, arithmetic and copies ran while one was open for 1% of the time, Pallas kernels for 15%

profile of v4, /device:TPU:128, one launch (start us, length us, event | category | flops | bytes accessed | tf_op | source)
XLA Modules:
  0.0 105.6 jit_solution(548263410117238358)
XLA Ops:
  0.0 19.5 %key_stage.1 = (f32[8,136,256]{2,1,0:T(8,128)}, bf16[8,4,128,512]{3,2,1,0:T(8,128)(2,1)}, bf16[8,3,128,512]{3,2,1,0:T(8,128)(2,1)}, f32[8,32,128]{2,1,0:T(8,128)}) custom-call(bf16[256,2,1024]{2,1,0:T(2,128)(2,1)} %refs_1_.3, bf16[256,2,1024]{2,1,0:T(2,128)(2,1)} %refs_1_.2, f32[2,8,256]{2,1,0:T(8,128)} %refs_2_.1, f32[8,256]{1,0:T(8,128)} %refs_3_.1, ...), custom_call_target="tpu_custom_call" | custom-call | tf_op jit(solution)/shard_map/key_stage/pallas_call | solution.py:241
  19.5 4.3 %all-to-all-start = ((f32[8,136,256]{2,1,0:T(8,128)}), f32[8,136,256]{2,1,0:T(8,128)S(1)}, u32[]{:S(2)}, u32[]{:S(2)}) async-start(f32[8,136,256]{2,1,0:T(8,128)} %get-tuple-element.28), calls=%async_computation | async-start | bytes 2228224 | tf_op jit(solution)/shard_map/all_to_all | solution.py:479
  23.8 8.5 %query_stage.1 = (f32[256,1024]{1,0:T(8,128)}, f32[256,1024]{1,0:T(8,128)}) custom-call(bf16[256,1024]{1,0:T(8,128)(2,1)} %refs_0_.3, bf16[256,2,1024]{2,1,0:T(2,128)(2,1)} %refs_1_.3, bf16[8,4,128,512]{3,2,1,0:T(8,128)(2,1)} %get-tuple-element.29.refs_2_, bf16[8,3,128,512]{3,2,1,0:T(8,128)(2,1)} %get-tuple-element.30.refs_3_, ...), custom_call_target="tpu_custom_call" | custom-call | tf_op jit(solution)/shard_map/query_stage/pallas_call | solution.py:273
  32.3 8.2 %all-to-all-done.in_ref = f32[8,136,256]{2,1,0:T(8,128)S(1)} async-done(((f32[8,136,256]{2,1,0:T(8,128)}), f32[8,136,256]{2,1,0:T(8,128)S(1)}, u32[]{:S(2)}, u32[]{:S(2)}) %all-to-all-start) | async-done | bytes 1114144 | tf_op jit(solution)/shard_map/all_to_all | solution.py:479
  40.5 0.7 prefix_stage.1
  41.2 2.9 %collective-permute-start = (f32[136,128]{1,0:T(8,128)S(1)}, f32[136,128]{1,0:T(8,128)S(1)}, u32[]{:S(2)}, u32[]{:S(2)}) collective-permute-start(f32[136,128]{1,0:T(8,128)S(1)} %get-tuple-element.39), channel_id=1, source_target_pairs={{0,32},{4,36},{8,40},{12,44},{16,48},{20,52},{24,56},{28,60},{32,6... | collective-permute-start | bytes 208904 | tf_op jit(solution)/shard_map/ppermute | solution.py:490
  44.1 4.5 %collective-permute-done.end_ref = f32[136,128]{1,0:T(8,128)S(1)} collective-permute-done((f32[136,128]{1,0:T(8,128)S(1)}, f32[136,128]{1,0:T(8,128)S(1)}, u32[]{:S(2)}, u32[]{:S(2)}) %collective-permute-start) | collective-permute-done | bytes 69664 | tf_op jit(solution)/shard_map/ppermute | solution.py:490
  48.6 1.1 %incoming_stage.1 = f32[8,128,128]{2,1,0:T(8,128)} custom-call(f32[8,128]{1,0:T(8,128)S(1)} %get-tuple-element.37.ends_ref, f32[8,128,256]{2,1,0:T(8,128)S(1)} %get-tuple-element.38.ex_ref, f32[136,128]{1,0:T(8,128)S(1)} %collective-permute-done.end_ref), custom_call_target="tpu_custom_call" | custom-call | tf_op jit(solution)/shard_map/incoming_stage/pallas_call | solution.py:491
  49.7 3.5 %all-to-all-start.1 = ((f32[8,128,128]{2,1,0:T(8,128)}), f32[8,128,128]{2,1,0:T(8,128)S(1)}, u32[]{:S(2)}, u32[]{:S(2)}) async-start(f32[8,128,128]{2,1,0:T(8,128)} %incoming_stage.1), calls=%async_computation.1 | async-start | bytes 1048576 | tf_op jit(solution)/shard_map/all_to_all | solution.py:499
  53.3 10.2 %all-to-all-done.1.state_ref = f32[8,128,128]{2,1,0:T(8,128)S(1)} async-done(((f32[8,128,128]{2,1,0:T(8,128)}), f32[8,128,128]{2,1,0:T(8,128)S(1)}, u32[]{:S(2)}, u32[]{:S(2)}) %all-to-all-start.1) | async-done | bytes 524320 | tf_op jit(solution)/shard_map/all_to_all | solution.py:499
  63.5 4.0 %far_tile.1 = (bf16[256,1024]{1,0:T(8,128)(2,1)}, f32[128,1024]{1,0:T(8,128)S(1)}, f32[128,1024]{1,0:T(8,128)S(1)}) custom-call(s32[1]{0:T(128)} %bitcast.1.pick_ref, f32[256,1024]{1,0:T(8,128)} %get-tuple-element.34.local_ref, f32[256,1024]{1,0:T(8,128)} %get-tuple-element.35.map_ref, f32[8,128,128]{2,1,0:T(8,128)S(1)} %all-to-all-done.1.state_ref, ...), custom_call_target="tpu_custom_call" | custom-call | tf_op jit(solution)/shard_map/far_tile/pallas_call | solution.py:363
  67.5 1.6 %collective-permute-start.2 = (f32[128,1024]{1,0:T(8,128)S(1)}, f32[128,1024]{1,0:T(8,128)S(1)}, u32[]{:S(2)}, u32[]{:S(2)}) collective-permute-start(f32[128,1024]{1,0:T(8,128)S(1)} %get-tuple-element.44), channel_id=1, source_target_pairs={{0,1},{1,2},{2,3},{3,0},{4,5},{5,6},{6,7},{7,4},{8,9},{9,10},{10,1... | collective-permute-start | bytes 1572872 | tf_op jit(solution)/shard_map/ppermute | solution.py:451
  69.1 1.7 %collective-permute-start.3 = (f32[128,1024]{1,0:T(8,128)S(1)}, f32[128,1024]{1,0:T(8,128)S(1)}, u32[]{:S(2)}, u32[]{:S(2)}) collective-permute-start(f32[128,1024]{1,0:T(8,128)S(1)} %get-tuple-element.46), channel_id=1, source_target_pairs={{0,3},{1,0},{2,1},{3,2},{4,7},{5,4},{6,5},{7,6},{8,11},{9,8},{10,9... | collective-permute-start | bytes 1572872 | tf_op jit(solution)/shard_map/ppermute | solution.py:452
  70.8 0.7 pad_add_fusion.pick_ref
  71.4 5.5 %side_tiles.1 = (f32[128,1024]{1,0:T(8,128)}, f32[128,1024]{1,0:T(8,128)}, f32[128,1024]{1,0:T(8,128)S(1)}, f32[128,1024]{1,0:T(8,128)S(1)}) custom-call(s32[2]{0:T(128)} %pad_add_fusion.pick_ref, bf16[256,1024]{1,0:T(8,128)(2,1)} %get-tuple-element.40.normed_ref, bf16[1024,4096]{1,0:T(8,128)(2,1)} %last_w_ref.1, bf16[1024,4096]{1,0:T(8,128)(2,1)} %last_w_ref.1), custom_call_target="tpu_custom_call" | custom-call | tf_op jit(solution)/shard_map/side_tiles/pallas_call | solution.py:423
  76.9 1.8 %collective-permute-start.1 = (f32[128,1024]{1,0:T(8,128)}, f32[128,1024]{1,0:T(8,128)S(1)}, u32[]{:S(2)}, u32[]{:S(2)}) collective-permute-start(f32[128,1024]{1,0:T(8,128)} %get-tuple-element.42), channel_id=1, source_target_pairs={{0,3},{1,0},{2,1},{3,2},{4,7},{5,4},{6,5},{7,6},{8,11},{9,8},{10,9... | collective-permute-start | bytes 1572872 | tf_op jit(solution)/shard_map/ppermute | solution.py:452
  78.7 0.2 collective-permute-start.5
  78.9 4.1 %collective-permute-done.2.gt_ref = f32[128,1024]{1,0:T(8,128)S(1)} collective-permute-done((f32[128,1024]{1,0:T(8,128)S(1)}, f32[128,1024]{1,0:T(8,128)S(1)}, u32[]{:S(2)}, u32[]{:S(2)}) %collective-permute-start.2) | collective-permute-done | bytes 524320 | tf_op jit(solution)/shard_map/ppermute | solution.py:451
  83.0 1.0 collective-permute-done.3.gb_ref
  83.9 0.1 join_tiles.1
  84.0 1.7 %collective-permute-start.4 = (f32[128,1024]{1,0:T(8,128)S(1)}, f32[128,1024]{1,0:T(8,128)S(1)}, u32[]{:S(2)}, u32[]{:S(2)}) collective-permute-start(f32[128,1024]{1,0:T(8,128)S(1)} %get-tuple-element.47), channel_id=1, source_target_pairs={{0,1},{1,2},{2,3},{3,0},{4,5},{5,6},{6,7},{7,4},{8,9},{9,10},{10,1... | collective-permute-start | bytes 1572872 | tf_op jit(solution)/shard_map/ppermute | solution.py:451
  85.7 1.6 %collective-permute-start.6 = (f32[128,1024]{1,0:T(8,128)S(1)}, f32[128,1024]{1,0:T(8,128)S(1)}, u32[]{:S(2)}, u32[]{:S(2)}) collective-permute-start(f32[128,1024]{1,0:T(8,128)S(1)} %get-tuple-element.50), channel_id=1, source_target_pairs={{0,3},{1,0},{2,1},{3,2},{4,7},{5,4},{6,5},{7,6},{8,11},{9,8},{10,9... | collective-permute-start | bytes 1572872 | tf_op jit(solution)/shard_map/ppermute | solution.py:452
  87.3 2.3 %shard_map.82 = (f32[128,1024]{1,0:T(8,128)S(1)}, f32[128,1024]{1,0:T(8,128)S(1)}) custom-call(s32[1]{0:T(128)} %bitcast.pick_ref, bf16[256,1024]{1,0:T(8,128)(2,1)} %get-tuple-element.40.normed_ref, bf16[1024,4096]{1,0:T(8,128)(2,1)} %last_w_ref.1), custom_call_target="tpu_custom_call" | custom-call | tf_op jit(solution)/shard_map/pallas_call | solution.py:397
  89.7 5.5 %collective-permute-done.1.st_ref = f32[128,1024]{1,0:T(8,128)S(1)} collective-permute-done((f32[128,1024]{1,0:T(8,128)}, f32[128,1024]{1,0:T(8,128)S(1)}, u32[]{:S(2)}, u32[]{:S(2)}) %collective-permute-start.1) | collective-permute-done | bytes 524320 | tf_op jit(solution)/shard_map/ppermute | solution.py:452
  95.1 0.0 collective-permute-done.5.sb_ref
  95.1 9.5 %collective-permute-done.4.gt_ref = f32[128,1024]{1,0:T(8,128)S(1)} collective-permute-done((f32[128,1024]{1,0:T(8,128)S(1)}, f32[128,1024]{1,0:T(8,128)S(1)}, u32[]{:S(2)}, u32[]{:S(2)}) %collective-permute-start.4) | collective-permute-done | bytes 524320 | tf_op jit(solution)/shard_map/ppermute | solution.py:451
  104.7 0.0 collective-permute-done.6.gb_ref
  104.7 0.9 finish.1
Async XLA Ops:
  19.5 20.9 %all-to-all-start = ((f32[8,136,256]{2,1,0:T(8,128)}), f32[8,136,256]{2,1,0:T(8,128)S(1)}, u32[]{:S(2)}, u32[]{:S(2)}) async-start(f32[8,136,256]{2,1,0:T(8,128)} %get-tuple-element.28), calls=%async_computation | async-start | bytes 2228224 | tf_op jit(solution)/shard_map/all_to_all | solution.py:479
  41.2 7.4 %collective-permute-start = (f32[136,128]{1,0:T(8,128)S(1)}, f32[136,128]{1,0:T(8,128)S(1)}, u32[]{:S(2)}, u32[]{:S(2)}) collective-permute-start(f32[136,128]{1,0:T(8,128)S(1)} %get-tuple-element.39), channel_id=1, source_target_pairs={{0,32},{4,36},{8,40},{12,44},{16,48},{20,52},{24,56},{28,60},{32,6... | collective-permute-start | bytes 208904 | tf_op jit(solution)/shard_map/ppermute | solution.py:490
  49.7 13.7 %all-to-all-start.1 = ((f32[8,128,128]{2,1,0:T(8,128)}), f32[8,128,128]{2,1,0:T(8,128)S(1)}, u32[]{:S(2)}, u32[]{:S(2)}) async-start(f32[8,128,128]{2,1,0:T(8,128)} %incoming_stage.1), calls=%async_computation.1 | async-start | bytes 1048576 | tf_op jit(solution)/shard_map/all_to_all | solution.py:499
  67.5 15.4 %collective-permute-start.2 = (f32[128,1024]{1,0:T(8,128)S(1)}, f32[128,1024]{1,0:T(8,128)S(1)}, u32[]{:S(2)}, u32[]{:S(2)}) collective-permute-start(f32[128,1024]{1,0:T(8,128)S(1)} %get-tuple-element.44), channel_id=1, source_target_pairs={{0,1},{1,2},{2,3},{3,0},{4,5},{5,6},{6,7},{7,4},{8,9},{9,10},{10,1... | collective-permute-start | bytes 1572872 | tf_op jit(solution)/shard_map/ppermute | solution.py:451
  69.1 14.8 %collective-permute-start.3 = (f32[128,1024]{1,0:T(8,128)S(1)}, f32[128,1024]{1,0:T(8,128)S(1)}, u32[]{:S(2)}, u32[]{:S(2)}) collective-permute-start(f32[128,1024]{1,0:T(8,128)S(1)} %get-tuple-element.46), channel_id=1, source_target_pairs={{0,3},{1,0},{2,1},{3,2},{4,7},{5,4},{6,5},{7,6},{8,11},{9,8},{10,9... | collective-permute-start | bytes 1572872 | tf_op jit(solution)/shard_map/ppermute | solution.py:452
  76.9 18.3 %collective-permute-start.1 = (f32[128,1024]{1,0:T(8,128)}, f32[128,1024]{1,0:T(8,128)S(1)}, u32[]{:S(2)}, u32[]{:S(2)}) collective-permute-start(f32[128,1024]{1,0:T(8,128)} %get-tuple-element.42), channel_id=1, source_target_pairs={{0,3},{1,0},{2,1},{3,2},{4,7},{5,4},{6,5},{7,6},{8,11},{9,8},{10,9... | collective-permute-start | bytes 1572872 | tf_op jit(solution)/shard_map/ppermute | solution.py:452
  78.7 16.5 %collective-permute-start.5 = (f32[128,1024]{1,0:T(8,128)}, f32[128,1024]{1,0:T(8,128)S(1)}, u32[]{:S(2)}, u32[]{:S(2)}) collective-permute-start(f32[128,1024]{1,0:T(8,128)} %get-tuple-element.49), channel_id=1, source_target_pairs={{0,1},{1,2},{2,3},{3,0},{4,5},{5,6},{6,7},{7,4},{8,9},{9,10},{10,1... | collective-permute-start | bytes 1572872 | tf_op jit(solution)/shard_map/ppermute | solution.py:451
  84.0 20.6 %collective-permute-start.4 = (f32[128,1024]{1,0:T(8,128)S(1)}, f32[128,1024]{1,0:T(8,128)S(1)}, u32[]{:S(2)}, u32[]{:S(2)}) collective-permute-start(f32[128,1024]{1,0:T(8,128)S(1)} %get-tuple-element.47), channel_id=1, source_target_pairs={{0,1},{1,2},{2,3},{3,0},{4,5},{5,6},{6,7},{7,4},{8,9},{9,10},{10,1... | collective-permute-start | bytes 1572872 | tf_op jit(solution)/shard_map/ppermute | solution.py:451
  85.7 19.0 %collective-permute-start.6 = (f32[128,1024]{1,0:T(8,128)S(1)}, f32[128,1024]{1,0:T(8,128)S(1)}, u32[]{:S(2)}, u32[]{:S(2)}) collective-permute-start(f32[128,1024]{1,0:T(8,128)S(1)} %get-tuple-element.50), channel_id=1, source_target_pairs={{0,3},{1,0},{2,1},{3,2},{4,7},{5,4},{6,5},{7,6},{8,11},{9,8},{10,9... | collective-permute-start | bytes 1572872 | tf_op jit(solution)/shard_map/ppermute | solution.py:452

commit v5 on v4

--- a/solution.py
+++ b/solution.py
@@ -38,6 +38,12 @@
         r = dotf(left, jnp.concatenate([right, right], axis=0))
         outs.append(r[:, :128] + r[:, 128:])
     return outs[0] if len(outs) == 1 else jnp.concatenate(outs, axis=1)
+
+
+def mm_tall(a, b):
+    m = a.shape[0]
+    r = dotf(jnp.concatenate(halves(a), axis=0), side(b))
+    return r[:m, :128] + (r[:m, 128:] + r[m:, :128])
 
 
 def mm_exact_right(a, b16):
@@ -72,10 +78,10 @@
 
             empty = jnp.zeros((size, ROWS), F32)
             low_band = low(band.astype(F32))
-            ys = [mm(low(s) * low_band, x) for s, x in zip(systems, xs)]
+            ys = [mm_tall(low(s) * low_band, x) for s, x in zip(systems, xs)]
             ys = [spread(y, lambda i: empty) for y in ys]
             lows = [low(x) for x in xs]
-            lows = [x - mm(x, y) for x, y in zip(lows, ys)]
+            lows = [x - mm_tall(x, y) for x, y in zip(lows, ys)]
             xs = [spread(y, lambda i: x[2 * i * size : (2 * i + 1) * size])
                   for x, y in zip(xs, lows)]
         shift += 1
@@ -101,16 +107,18 @@
             return lax.dot_general(x, sel, (((1,), (0,)), ((), ())),
                                    precision=lax.Precision.HIGHEST, preferred_element_type=F32)
 
-        seg = jnp.broadcast_to(seg_ref[...].astype(F32), (heads, blocks * GROUP))
+        def stacked(x):
+            return jnp.concatenate([x[:, n * GROUP : (n + 1) * GROUP] for n in range(blocks)], axis=0)
+
+        seg = stacked(jnp.broadcast_to(seg_ref[...].astype(F32), (heads, blocks * GROUP)))
+        lg = stacked(log_ref[...])
+        kinds = (pick(lg, upto),
+                 pick(stacked(beta_ref[0]), even) + pick(stacked(beta_ref[1]), odd),
+                 pick(seg, both), pick(lg, flat), pick(seg, same))
         for n in range(blocks):
-            cut = slice(n * GROUP, (n + 1) * GROUP)
-            lg = log_ref[:, cut]
-            tab_ref[:, 8 * n, :] = pick(lg, upto)
-            tab_ref[:, 8 * n + 1, :] = pick(beta_ref[0, :, cut], even) + pick(beta_ref[1, :, cut], odd)
-            tab_ref[:, 8 * n + 2, :] = pick(seg[:, cut], both)
-            tab_ref[:, 8 * n + 3, :] = pick(lg, flat)
-            tab_ref[:, 8 * n + 4, :] = pick(seg[:, cut], same)
-            for z in range(5, 8):
+            for i, kind in enumerate(kinds):
+                tab_ref[:, 8 * n + i, :] = kind[n * heads : (n + 1) * heads]
+            for z in range(len(kinds), 8):
                 tab_ref[:, 8 * n + z, :] = jnp.zeros((heads, ROWS), F32)
 
     r, c = iota((ROWS, ROWS), 0), iota((ROWS, ROWS), 1)
@@ -228,7 +236,7 @@
         out_ref[rows, lanes] = local
 
 
-KEY_STEP = 2
+KEY_STEP = 4
 QUERY_STEP = 2
 
 
@@ -286,7 +294,7 @@
         ],
         out_shape=[
             jax.ShapeDtypeStruct((tok, heads * DV), F32),
-            jax.ShapeDtypeStruct((tok, heads * DK), F32),
+            pltpu.VMEM((tok, heads * DK), F32),
         ],
         compiler_params=pltpu.CompilerParams(dimension_semantics=("arbitrary",)),
         name="query_stage",
@@ -357,20 +365,36 @@
 def far_tile(place, local, mapped, state, gain, weight, width):
     tok, feats = local.shape
     part = pltpu.VMEM((tok // 2, width), F32)
-    steps = 2
+    steps = 4
     cols = width // steps
     out = pl.BlockSpec((tok // 2, cols), lambda i, at: (0, i))
     return pl.pallas_call(
         far_kernel,
         grid_spec=pltpu.PrefetchScalarGridSpec(
             num_scalar_prefetch=1, grid=(steps,),
-            in_specs=[whole(tok, feats), whole(tok, feats), resident(), whole(1, feats),
-                      pl.BlockSpec((feats, cols), lambda i, at: (0, steps * at[0] + i))],
+            in_specs=[whole(tok, feats), resident(), resident(), whole(1, feats),
+                      pl.BlockSpec((feats, cols), lambda i, at: (0, steps * ((at[0] + 2) & 3) + i))],
             out_specs=[whole(tok, feats), out, out]),
         out_shape=[jax.ShapeDtypeStruct((tok, feats), BF16), part, part],
         compiler_params=pltpu.CompilerParams(vmem_limit_bytes=57 << 20),
         name="far_tile",
-    )(place, local, mapped, held(state), gain.reshape(1, feats), weight)
+    )(place, local, held(mapped), held(state), gain.reshape(1, feats), weight)
+
+
+def join_kernel(nt_ref, gt_ref, lb_ref, gb_ref, top_ref, bottom_ref):
+    top_ref[...] = nt_ref[...] + gt_ref[...]
+    bottom_ref[...] = lb_ref[...] + gb_ref[...]
+
+
+def joined(next_top, got_top, last_bottom, got_bottom):
+    return pl.pallas_call(
+        join_kernel,
+        in_specs=[resident()] * 4,
+        out_specs=[resident()] * 2,
+        out_shape=[pltpu.VMEM(next_top.shape, F32)] * 2,
+        compiler_params=pltpu.CompilerParams(vmem_limit_bytes=57 << 20),
+        name="join_tiles",
+    )(held(next_top), held(got_top), held(last_bottom), held(got_bottom))
 
 
 def join_kernel(nt_ref, gt_ref, lb_ref, gb_ref, top_ref, bottom_ref):
@@ -425,8 +449,8 @@
         grid_spec=pltpu.PrefetchScalarGridSpec(
             num_scalar_prefetch=1, grid=(steps,),
             in_specs=[whole(tok, feats),
-                      pl.BlockSpec((feats, cols), lambda i, at: (0, steps * at[0] + i)),
-                      pl.BlockSpec((feats, cols), lambda i, at: (0, steps * at[1] + i))],
+                      pl.BlockSpec((feats, cols), lambda i, at: (0, steps * ((at[0] + 1) & 3) + i)),
+                      pl.BlockSpec((feats, cols), lambda i, at: (0, steps * ((at[0] + 3) & 3) + i))],
             out_specs=[out] * 4),
         out_shape=[part] * 2 + [pltpu.VMEM((tok // 2, width), F32)] * 2,
         compiler_params=pltpu.CompilerParams(vmem_limit_bytes=57 << 20),
@@ -450,10 +474,10 @@
     at = lambda step: ((mine + step) & (count - 1)).astype(jnp.int32).reshape(1)
     up = lambda x: lax.ppermute(x, "head", rise)
     down = lambda x: lax.ppermute(x, "head", fall)
-    normed, far_top, far_bottom = far_tile(at(2), local, mapped, states, gain, out_weight, width)
+    normed, far_top, far_bottom = far_tile(at(0), local, mapped, states, gain, out_weight, width)
     got_top, got_bottom = up(far_top), down(far_bottom)
     next_bottom, last_top, next_top, last_bottom = side_tiles(
-        jnp.concatenate([at(1), at(3)]), normed, out_weight, width)
+        at(0), normed, out_weight, width)
     side_bottom = up(next_bottom)
     side_top = down(last_top)
     next_top, last_bottom = joined(next_top, got_top, last_bottom, got_bottom)

time: 106 us -> 105 us (level)
  Pallas kernels: 42.7 us -> 41.1 us
  waiting for transfers between devices: 42.9 us -> 44.5 us
    ppermute x3, waiting for transfers between devices: 13.6 us -> 15.5 us  [summed_output(): up = lambda x: lax.ppermute(x, 'head', rise)]
    pallas_call x1, Pallas kernels: 19.5 us -> 18.1 us  [key_stage(): pl.pallas_call(body, grid=(heads // step,), in_specs=[pl.BlockSpec((tok,...]
  transfers between devices with their start and end apart: 9 -> 9, of which waited for: 7 -> 7; matrix products, arithmetic and copies ran while one was open for 1% -> 0% of each run, Pallas kernels for 15% -> 15%
where the time goes in v5:
time: 105 us
  waiting for transfers between devices  44.5 us (42%)
  Pallas kernels  41.1 us (39%)
  starting transfers between devices  19.3 us (18%)
    pallas_call x1, Pallas kernels, key_stage(): pl.pallas_call(body, grid=(heads // step,), in_specs=[pl.BlockSpec((tok,...  18.1 us
    ppermute x3, waiting for transfers between devices, summed_output(): up = lambda x: lax.ppermute(x, 'head', rise)  15.5 us
    all_to_all x1, waiting for transfers between devices, shards(): states = lax.all_to_all(states, 'ctx', 0, 0, axis_index_groups=groups)  10.2 us
    all_to_all x1, waiting for transfers between devices, shards(): mine = lax.all_to_all(pair, 'ctx', 0, 0, axis_index_groups=groups)  8.43 us
    pallas_call x1, Pallas kernels, query_stage(): pl.pallas_call(body, grid=(heads // step,), in_specs=[pl.BlockSpec((tok,...  8.2 us
    ppermute x3, waiting for transfers between devices, summed_output(): down = lambda x: lax.ppermute(x, 'head', fall)  5.85 us
    ppermute x3, starting transfers between devices, summed_output(): down = lambda x: lax.ppermute(x, 'head', fall)  5.12 us
    pallas_call x1, Pallas kernels, side_tiles(): pl.pallas_call(sides_kernel, grid_spec=pltpu.PrefetchScalarGridSpec(num_s...  4.77 us
  transfers between devices with their start and end apart: 9, of which 7 were waited for; matrix products, arithmetic and copies ran while one was open for 0% of the time, Pallas kernels for 15%

profile of v5, /device:TPU:128, one launch (start us, length us, event | category | flops | bytes accessed | tf_op | source)
XLA Modules:
  0.0 104.9 jit_solution(8785017146408589285)
XLA Ops:
  0.0 18.1 %key_stage.1 = (f32[8,136,256]{2,1,0:T(8,128)}, bf16[8,4,128,512]{3,2,1,0:T(8,128)(2,1)}, bf16[8,3,128,512]{3,2,1,0:T(8,128)(2,1)}, f32[8,32,128]{2,1,0:T(8,128)}) custom-call(bf16[256,2,1024]{2,1,0:T(2,128)(2,1)} %refs_1_.3, bf16[256,2,1024]{2,1,0:T(2,128)(2,1)} %refs_1_.2, f32[2,8,256]{2,1,0:T(8,128)} %refs_2_.1, f32[8,256]{1,0:T(8,128)} %refs_3_.1, ...), custom_call_target="tpu_custom_call" | custom-call | tf_op jit(solution)/shard_map/key_stage/pallas_call | solution.py:249
  18.1 4.3 %all-to-all-start = ((f32[8,136,256]{2,1,0:T(8,128)}), f32[8,136,256]{2,1,0:T(8,128)S(1)}, u32[]{:S(2)}, u32[]{:S(2)}) async-start(f32[8,136,256]{2,1,0:T(8,128)} %get-tuple-element.28), calls=%async_computation | async-start | bytes 2228224 | tf_op jit(solution)/shard_map/all_to_all | solution.py:503
  22.4 8.2 %query_stage.1 = (f32[256,1024]{1,0:T(8,128)}, f32[256,1024]{1,0:T(8,128)S(1)}) custom-call(bf16[256,1024]{1,0:T(8,128)(2,1)} %refs_0_.3, bf16[256,2,1024]{2,1,0:T(2,128)(2,1)} %refs_1_.3, bf16[8,4,128,512]{3,2,1,0:T(8,128)(2,1)} %get-tuple-element.29.refs_2_, bf16[8,3,128,512]{3,2,1,0:T(8,128)(2,1)} %get-tuple-element.30.refs_3_, ...), custom_call_target="tpu_custom_call" | custom-call | tf_op jit(solution)/shard_map/query_stage/pallas_call | solution.py:281
  30.6 8.4 %all-to-all-done.in_ref = f32[8,136,256]{2,1,0:T(8,128)S(1)} async-done(((f32[8,136,256]{2,1,0:T(8,128)}), f32[8,136,256]{2,1,0:T(8,128)S(1)}, u32[]{:S(2)}, u32[]{:S(2)}) %all-to-all-start) | async-done | bytes 1114144 | tf_op jit(solution)/shard_map/all_to_all | solution.py:503
  39.1 0.7 prefix_stage.1
  39.8 2.9 %collective-permute-start = (f32[136,128]{1,0:T(8,128)S(1)}, f32[136,128]{1,0:T(8,128)S(1)}, u32[]{:S(2)}, u32[]{:S(2)}) collective-permute-start(f32[136,128]{1,0:T(8,128)S(1)} %get-tuple-element.39), channel_id=1, source_target_pairs={{0,32},{4,36},{8,40},{12,44},{16,48},{20,52},{24,56},{28,60},{32,6... | collective-permute-start | bytes 208904 | tf_op jit(solution)/shard_map/ppermute | solution.py:514
  42.8 4.5 %collective-permute-done.end_ref = f32[136,128]{1,0:T(8,128)S(1)} collective-permute-done((f32[136,128]{1,0:T(8,128)S(1)}, f32[136,128]{1,0:T(8,128)S(1)}, u32[]{:S(2)}, u32[]{:S(2)}) %collective-permute-start) | collective-permute-done | bytes 69664 | tf_op jit(solution)/shard_map/ppermute | solution.py:514
  47.2 1.1 %incoming_stage.1 = f32[8,128,128]{2,1,0:T(8,128)} custom-call(f32[8,128]{1,0:T(8,128)S(1)} %get-tuple-element.37.ends_ref, f32[8,128,256]{2,1,0:T(8,128)S(1)} %get-tuple-element.38.ex_ref, f32[136,128]{1,0:T(8,128)S(1)} %collective-permute-done.end_ref), custom_call_target="tpu_custom_call" | custom-call | tf_op jit(solution)/shard_map/incoming_stage/pallas_call | solution.py:515
  48.4 3.5 %all-to-all-start.1 = ((f32[8,128,128]{2,1,0:T(8,128)}), f32[8,128,128]{2,1,0:T(8,128)S(1)}, u32[]{:S(2)}, u32[]{:S(2)}) async-start(f32[8,128,128]{2,1,0:T(8,128)} %incoming_stage.1), calls=%async_computation.1 | async-start | bytes 1048576 | tf_op jit(solution)/shard_map/all_to_all | solution.py:523
  51.9 10.2 %all-to-all-done.1.state_ref = f32[8,128,128]{2,1,0:T(8,128)S(1)} async-done(((f32[8,128,128]{2,1,0:T(8,128)}), f32[8,128,128]{2,1,0:T(8,128)S(1)}, u32[]{:S(2)}, u32[]{:S(2)}) %all-to-all-start.1) | async-done | bytes 524320 | tf_op jit(solution)/shard_map/all_to_all | solution.py:523
  62.1 4.7 %far_tile.1 = (bf16[256,1024]{1,0:T(8,128)(2,1)}, f32[128,1024]{1,0:T(8,128)S(1)}, f32[128,1024]{1,0:T(8,128)S(1)}) custom-call(s32[1]{0:T(128)} %bitcast.pick_ref, f32[256,1024]{1,0:T(8,128)} %get-tuple-element.34.local_ref, f32[256,1024]{1,0:T(8,128)S(1)} %get-tuple-element.35.map_ref, f32[8,128,128]{2,1,0:T(8,128)S(1)} %all-to-all-done.1.state_ref, ...), custom_call_target="tpu_custom_call" | custom-call | tf_op jit(solution)/shard_map/far_tile/pallas_call | solution.py:371
  66.8 1.6 %collective-permute-start.2 = (f32[128,1024]{1,0:T(8,128)S(1)}, f32[128,1024]{1,0:T(8,128)S(1)}, u32[]{:S(2)}, u32[]{:S(2)}) collective-permute-start(f32[128,1024]{1,0:T(8,128)S(1)} %get-tuple-element.44), channel_id=1, source_target_pairs={{0,1},{1,2},{2,3},{3,0},{4,5},{5,6},{6,7},{7,4},{8,9},{9,10},{10,1... | collective-permute-start | bytes 1572872 | tf_op jit(solution)/shard_map/ppermute | solution.py:475
  68.4 1.7 %collective-permute-start.3 = (f32[128,1024]{1,0:T(8,128)S(1)}, f32[128,1024]{1,0:T(8,128)S(1)}, u32[]{:S(2)}, u32[]{:S(2)}) collective-permute-start(f32[128,1024]{1,0:T(8,128)S(1)} %get-tuple-element.46), channel_id=1, source_target_pairs={{0,3},{1,0},{2,1},{3,2},{4,7},{5,4},{6,5},{7,6},{8,11},{9,8},{10,9... | collective-permute-start | bytes 1572872 | tf_op jit(solution)/shard_map/ppermute | solution.py:476
  70.1 4.8 %side_tiles.1 = (f32[128,1024]{1,0:T(8,128)}, f32[128,1024]{1,0:T(8,128)}, f32[128,1024]{1,0:T(8,128)S(1)}, f32[128,1024]{1,0:T(8,128)S(1)}) custom-call(s32[1]{0:T(128)} %bitcast.pick_ref, bf16[256,1024]{1,0:T(8,128)(2,1)} %get-tuple-element.40.normed_ref, bf16[1024,4096]{1,0:T(8,128)(2,1)} %last_w_ref.1, bf16[1024,4096]{1,0:T(8,128)(2,1)} %last_w_ref.1), custom_call_target="tpu_custom_call" | custom-call | tf_op jit(solution)/shard_map/side_tiles/pallas_call | solution.py:447
  74.8 1.8 %collective-permute-start.1 = (f32[128,1024]{1,0:T(8,128)}, f32[128,1024]{1,0:T(8,128)S(1)}, u32[]{:S(2)}, u32[]{:S(2)}) collective-permute-start(f32[128,1024]{1,0:T(8,128)} %get-tuple-element.42), channel_id=1, source_target_pairs={{0,3},{1,0},{2,1},{3,2},{4,7},{5,4},{6,5},{7,6},{8,11},{9,8},{10,9... | collective-permute-start | bytes 1572872 | tf_op jit(solution)/shard_map/ppermute | solution.py:476
  76.6 0.2 collective-permute-start.5
  76.9 6.0 %collective-permute-done.2.gt_ref = f32[128,1024]{1,0:T(8,128)S(1)} collective-permute-done((f32[128,1024]{1,0:T(8,128)S(1)}, f32[128,1024]{1,0:T(8,128)S(1)}, u32[]{:S(2)}, u32[]{:S(2)}) %collective-permute-start.2) | collective-permute-done | bytes 524320 | tf_op jit(solution)/shard_map/ppermute | solution.py:475
  82.8 0.4 collective-permute-done.3.gb_ref
  83.2 0.1 join_tiles.1
  83.3 1.7 %collective-permute-start.4 = (f32[128,1024]{1,0:T(8,128)S(1)}, f32[128,1024]{1,0:T(8,128)S(1)}, u32[]{:S(2)}, u32[]{:S(2)}) collective-permute-start(f32[128,1024]{1,0:T(8,128)S(1)} %get-tuple-element.47), channel_id=1, source_target_pairs={{0,1},{1,2},{2,3},{3,0},{4,5},{5,6},{6,7},{7,4},{8,9},{9,10},{10,1... | collective-permute-start | bytes 1572872 | tf_op jit(solution)/shard_map/ppermute | solution.py:475
  85.0 1.7 %collective-permute-start.6 = (f32[128,1024]{1,0:T(8,128)S(1)}, f32[128,1024]{1,0:T(8,128)S(1)}, u32[]{:S(2)}, u32[]{:S(2)}) collective-permute-start(f32[128,1024]{1,0:T(8,128)S(1)} %get-tuple-element.50), channel_id=1, source_target_pairs={{0,3},{1,0},{2,1},{3,2},{4,7},{5,4},{6,5},{7,6},{8,11},{9,8},{10,9... | collective-permute-start | bytes 1572872 | tf_op jit(solution)/shard_map/ppermute | solution.py:476
  86.6 2.4 %shard_map.82 = (f32[128,1024]{1,0:T(8,128)S(1)}, f32[128,1024]{1,0:T(8,128)S(1)}) custom-call(s32[1]{0:T(128)} %bitcast.pick_ref, bf16[256,1024]{1,0:T(8,128)(2,1)} %get-tuple-element.40.normed_ref, bf16[1024,4096]{1,0:T(8,128)(2,1)} %last_w_ref.1), custom_call_target="tpu_custom_call" | custom-call | tf_op jit(solution)/shard_map/pallas_call | solution.py:421
  89.0 5.5 %collective-permute-done.1.st_ref = f32[128,1024]{1,0:T(8,128)S(1)} collective-permute-done((f32[128,1024]{1,0:T(8,128)}, f32[128,1024]{1,0:T(8,128)S(1)}, u32[]{:S(2)}, u32[]{:S(2)}) %collective-permute-start.1) | collective-permute-done | bytes 524320 | tf_op jit(solution)/shard_map/ppermute | solution.py:476
  94.5 0.0 collective-permute-done.5.sb_ref
  94.5 9.5 %collective-permute-done.4.gt_ref = f32[128,1024]{1,0:T(8,128)S(1)} collective-permute-done((f32[128,1024]{1,0:T(8,128)S(1)}, f32[128,1024]{1,0:T(8,128)S(1)}, u32[]{:S(2)}, u32[]{:S(2)}) %collective-permute-start.4) | collective-permute-done | bytes 524320 | tf_op jit(solution)/shard_map/ppermute | solution.py:475
  104.0 0.0 collective-permute-done.6.gb_ref
  104.0 0.9 finish.1
Async XLA Ops:
  18.1 20.9 %all-to-all-start = ((f32[8,136,256]{2,1,0:T(8,128)}), f32[8,136,256]{2,1,0:T(8,128)S(1)}, u32[]{:S(2)}, u32[]{:S(2)}) async-start(f32[8,136,256]{2,1,0:T(8,128)} %get-tuple-element.28), calls=%async_computation | async-start | bytes 2228224 | tf_op jit(solution)/shard_map/all_to_all | solution.py:503
  39.8 7.4 %collective-permute-start = (f32[136,128]{1,0:T(8,128)S(1)}, f32[136,128]{1,0:T(8,128)S(1)}, u32[]{:S(2)}, u32[]{:S(2)}) collective-permute-start(f32[136,128]{1,0:T(8,128)S(1)} %get-tuple-element.39), channel_id=1, source_target_pairs={{0,32},{4,36},{8,40},{12,44},{16,48},{20,52},{24,56},{28,60},{32,6... | collective-permute-start | bytes 208904 | tf_op jit(solution)/shard_map/ppermute | solution.py:514
  48.4 13.7 %all-to-all-start.1 = ((f32[8,128,128]{2,1,0:T(8,128)}), f32[8,128,128]{2,1,0:T(8,128)S(1)}, u32[]{:S(2)}, u32[]{:S(2)}) async-start(f32[8,128,128]{2,1,0:T(8,128)} %incoming_stage.1), calls=%async_computation.1 | async-start | bytes 1048576 | tf_op jit(solution)/shard_map/all_to_all | solution.py:523
  66.8 16.0 %collective-permute-start.2 = (f32[128,1024]{1,0:T(8,128)S(1)}, f32[128,1024]{1,0:T(8,128)S(1)}, u32[]{:S(2)}, u32[]{:S(2)}) collective-permute-start(f32[128,1024]{1,0:T(8,128)S(1)} %get-tuple-element.44), channel_id=1, source_target_pairs={{0,1},{1,2},{2,3},{3,0},{4,5},{5,6},{6,7},{7,4},{8,9},{9,10},{10,1... | collective-permute-start | bytes 1572872 | tf_op jit(solution)/shard_map/ppermute | solution.py:475
  68.4 14.8 %collective-permute-start.3 = (f32[128,1024]{1,0:T(8,128)S(1)}, f32[128,1024]{1,0:T(8,128)S(1)}, u32[]{:S(2)}, u32[]{:S(2)}) collective-permute-start(f32[128,1024]{1,0:T(8,128)S(1)} %get-tuple-element.46), channel_id=1, source_target_pairs={{0,3},{1,0},{2,1},{3,2},{4,7},{5,4},{6,5},{7,6},{8,11},{9,8},{10,9... | collective-permute-start | bytes 1572872 | tf_op jit(solution)/shard_map/ppermute | solution.py:476
  74.8 19.6 %collective-permute-start.1 = (f32[128,1024]{1,0:T(8,128)}, f32[128,1024]{1,0:T(8,128)S(1)}, u32[]{:S(2)}, u32[]{:S(2)}) collective-permute-start(f32[128,1024]{1,0:T(8,128)} %get-tuple-element.42), channel_id=1, source_target_pairs={{0,3},{1,0},{2,1},{3,2},{4,7},{5,4},{6,5},{7,6},{8,11},{9,8},{10,9... | collective-permute-start | bytes 1572872 | tf_op jit(solution)/shard_map/ppermute | solution.py:476
  76.6 17.8 %collective-permute-start.5 = (f32[128,1024]{1,0:T(8,128)}, f32[128,1024]{1,0:T(8,128)S(1)}, u32[]{:S(2)}, u32[]{:S(2)}) collective-permute-start(f32[128,1024]{1,0:T(8,128)} %get-tuple-element.49), channel_id=1, source_target_pairs={{0,1},{1,2},{2,3},{3,0},{4,5},{5,6},{6,7},{7,4},{8,9},{9,10},{10,1... | collective-permute-start | bytes 1572872 | tf_op jit(solution)/shard_map/ppermute | solution.py:475
  83.3 20.6 %collective-permute-start.4 = (f32[128,1024]{1,0:T(8,128)S(1)}, f32[128,1024]{1,0:T(8,128)S(1)}, u32[]{:S(2)}, u32[]{:S(2)}) collective-permute-start(f32[128,1024]{1,0:T(8,128)S(1)} %get-tuple-element.47), channel_id=1, source_target_pairs={{0,1},{1,2},{2,3},{3,0},{4,5},{5,6},{6,7},{7,4},{8,9},{9,10},{10,1... | collective-permute-start | bytes 1572872 | tf_op jit(solution)/shard_map/ppermute | solution.py:475
  85.0 19.0 %collective-permute-start.6 = (f32[128,1024]{1,0:T(8,128)S(1)}, f32[128,1024]{1,0:T(8,128)S(1)}, u32[]{:S(2)}, u32[]{:S(2)}) collective-permute-start(f32[128,1024]{1,0:T(8,128)S(1)} %get-tuple-element.50), channel_id=1, source_target_pairs={{0,3},{1,0},{2,1},{3,2},{4,7},{5,4},{6,5},{7,6},{8,11},{9,8},{10,9... | collective-permute-start | bytes 1572872 | tf_op jit(solution)/shard_map/ppermute | solution.py:476

commit v6 on v5

--- a/solution.py
+++ b/solution.py
@@ -329,27 +329,34 @@
     ends_ref[...] = in_ref[0, DK:, :DV]
 
 
-def incoming_kernel(ends_ref, ex_ref, end_ref, out_ref):
+def incoming_kernel(spot_ref, ends_ref, ex_ref, end_ref, *out_refs):
     flag = jnp.where(ends_ref[0:1, :] == end_ref[DK + 1 : DK + 2, :], 1.0, 0.0)
     state = end_ref[:DK, :] * flag
-    for i in range(ex_ref.shape[0]):
-        out_ref[i] = mm(ex_ref[i, :, :DK], state) + ex_ref[i, :, DK:]
-
-
-def far_kernel(pick_ref, local_ref, map_ref, state_ref, gain_ref, weight_ref, normed_ref, up_ref, down_ref):
-    heads = state_ref.shape[0]
-
-    @pl.when(pl.program_id(0) == 0)
-    def _():
-        for h in range(heads):
-            lanes = slice(h * DV, (h + 1) * DV)
-            attended = local_ref[:, lanes] + mm(map_ref[:, lanes], state_ref[h])
-            mean = jnp.mean(attended * attended, axis=1, keepdims=True)
-            normed_ref[:, lanes] = (attended * lax.rsqrt(mean + EPS) * gain_ref[:, lanes]).astype(BF16)
-
+    for step, out_ref in enumerate(out_refs):
+        i = spot_ref[0] ^ step
+        out_ref[...] = mm(ex_ref[i, :, :DK], state) + ex_ref[i, :, DK:]
+
+
+def far_kernel(heads, place_ref, spot_ref, local_ref, map_ref, gain_ref, weight_ref, *refs):
+    state_refs = refs[:heads]
+    normed_ref, up_ref, down_ref, columns_ref, own_ref, copied, read = refs[heads:]
+    width = up_ref.shape[1]
+    start = pl.multiple_of(((place_ref[0] + 2) & 3) * width, width)
+    bring = pltpu.make_async_copy(local_ref, own_ref, read)
+    bring.start()
+    load = pltpu.make_async_copy(weight_ref.at[:, pl.ds(start, width)], columns_ref, copied)
+    load.start()
+    spots = [pl.ds(pl.multiple_of((spot_ref[0] ^ step) * DV, DV), DV) for step in range(heads)]
+    read_out = [mm(map_ref[:, lanes], ref[...]) for lanes, ref in zip(spots, state_refs)]
+    bring.wait()
+    for lanes, part in zip(spots, read_out):
+        attended = own_ref[:, lanes] + part
+        mean = jnp.mean(attended * attended, axis=1, keepdims=True)
+        normed_ref[:, lanes] = (attended * lax.rsqrt(mean + EPS) * gain_ref[:, lanes]).astype(BF16)
+    load.wait()
     half = up_ref.shape[0]
-    up_ref[...] = dotf(normed_ref[:half, :], weight_ref[...])
-    down_ref[...] = dotf(normed_ref[half:, :], weight_ref[...])
+    up_ref[...] = dotf(normed_ref[:half, :], columns_ref[...])
+    down_ref[...] = dotf(normed_ref[half:, :], columns_ref[...])
 
 
 def tile_kernel(pick_ref, normed_ref, weight_ref, top_ref, bottom_ref):
@@ -362,23 +369,22 @@
     return pl.BlockSpec(shape, lambda i, *_: (0,) * len(shape))
 
 
-def far_tile(place, local, mapped, state, gain, weight, width):
+def far_tile(place, spot, local, mapped, states, gain, weight, width):
     tok, feats = local.shape
     part = pltpu.VMEM((tok // 2, width), F32)
-    steps = 4
-    cols = width // steps
-    out = pl.BlockSpec((tok // 2, cols), lambda i, at: (0, i))
-    return pl.pallas_call(
-        far_kernel,
-        grid_spec=pltpu.PrefetchScalarGridSpec(
-            num_scalar_prefetch=1, grid=(steps,),
-            in_specs=[whole(tok, feats), resident(), resident(), whole(1, feats),
-                      pl.BlockSpec((feats, cols), lambda i, at: (0, steps * ((at[0] + 2) & 3) + i))],
-            out_specs=[whole(tok, feats), out, out]),
+    anywhere = pl.BlockSpec(memory_space=pl.ANY)
+    scalar = pl.BlockSpec(memory_space=pltpu.SMEM)
+    body = lambda *refs: far_kernel(len(states), *refs)
+    return pl.pallas_call(
+        body,
+        in_specs=[scalar, scalar, anywhere, resident(), resident(), anywhere] + [resident()] * len(states),
+        out_specs=[resident()] * 3,
         out_shape=[jax.ShapeDtypeStruct((tok, feats), BF16), part, part],
+        scratch_shapes=[pltpu.VMEM((feats, width), BF16), pltpu.VMEM((tok, feats), F32),
+                        pltpu.SemaphoreType.DMA(()), pltpu.SemaphoreType.DMA(())],
         compiler_params=pltpu.CompilerParams(vmem_limit_bytes=57 << 20),
         name="far_tile",
-    )(place, local, held(mapped), held(state), gain.reshape(1, feats), weight)
+    )(place, spot, local, held(mapped), gain.reshape(1, feats), weight, *map(held, states))
 
 
 def join_kernel(nt_ref, gt_ref, lb_ref, gb_ref, top_ref, bottom_ref):
@@ -464,7 +470,7 @@
     out_ref[half:, :] = (ob_ref[...] + sb_ref[...] + gb_ref[...]).astype(BF16)
 
 
-def summed_output(local, mapped, states, gain, out_weight):
+def summed_output(spot, local, mapped, states, gain, out_weight):
     count = lax.axis_size("head")
     assert count == 4
     mine = lax.axis_index("head")
@@ -474,7 +480,7 @@
     at = lambda step: ((mine + step) & (count - 1)).astype(jnp.int32).reshape(1)
     up = lambda x: lax.ppermute(x, "head", rise)
     down = lambda x: lax.ppermute(x, "head", fall)
-    normed, far_top, far_bottom = far_tile(at(0), local, mapped, states, gain, out_weight, width)
+    normed, far_top, far_bottom = far_tile(at(0), spot, local, mapped, states, gain, out_weight, width)
     got_top, got_bottom = up(far_top), down(far_bottom)
     next_bottom, last_top, next_top, last_bottom = side_tiles(
         at(0), normed, out_weight, width)
@@ -512,16 +518,20 @@
         name="prefix_stage",
     )(held(mine))
     end = lax.ppermute(end, "ctx", [(i, i + span) for i in range(devices - span)])
+    assert span & (span - 1) == 0
+    spot = (lax.axis_index("ctx") & (span - 1)).astype(jnp.int32).reshape(1)
     states = pl.pallas_call(
         incoming_kernel,
-        in_specs=[resident(), resident(), resident()],
-        out_specs=resident(),
-        out_shape=pltpu.VMEM((span, DK, DV), F32),
+        in_specs=[pl.BlockSpec(memory_space=pltpu.SMEM)] + [resident()] * 3,
+        out_specs=[resident()] * span,
+        out_shape=[pltpu.VMEM((DK, DV), F32)] * span,
         compiler_params=pltpu.CompilerParams(vmem_limit_bytes=57 << 20),
         name="incoming_stage",
-    )(held(ends), held(exclusive), held(end))
-    states = lax.all_to_all(states, "ctx", 0, 0, axis_index_groups=groups)
-    return summed_output(local, mapped, states, gain, out_weight)
+    )(spot, held(ends), held(exclusive), held(end))
+    moved = {step: lax.ppermute(states[step], "ctx", [(i, i ^ step) for i in range(devices)])
+             for step in (4, 5, 2, 6, 3, 7, 1)}
+    states = [states[0]] + [moved[step] for step in range(1, span)]
+    return summed_output(spot, local, mapped, states, gain, out_weight)
 
 
 def solution(mesh):

time: 105 us -> 105 us (level)
  starting transfers between devices: 19.3 us -> 25.1 us
  waiting for transfers between devices: 44.5 us -> 40.2 us
  Pallas kernels: 41.1 us -> 39.2 us
    all_to_all x1 -> x0, waiting for transfers between devices: 10.2 us -> none  [shards(): states = lax.all_to_all(states, 'ctx', 0, 0, axis_index_groups=groups)]
    ppermute x0 -> x7, starting transfers between devices: none -> 8.15 us  [shards(): lax.ppermute(states[step], 'ctx', [(i, i ^ step) for i in range(devices)])]
    ppermute x3, starting transfers between devices: 5.12 us -> 9.03 us  [summed_output(): down = lambda x: lax.ppermute(x, 'head', fall)]
    ppermute x0 -> x7, waiting for transfers between devices: none -> 3.81 us  [shards(): lax.ppermute(states[step], 'ctx', [(i, i ^ step) for i in range(devices)])]
    ppermute x3, waiting for transfers between devices: 15.5 us -> 19.2 us  [summed_output(): up = lambda x: lax.ppermute(x, 'head', rise)]
    all_to_all x1 -> x0, starting transfers between devices: 3.49 us -> none  [shards(): states = lax.all_to_all(states, 'ctx', 0, 0, axis_index_groups=groups)]
    ppermute x3, starting transfers between devices: 3.45 us -> 0.65 us  [summed_output(): up = lambda x: lax.ppermute(x, 'head', rise)]
    pallas_call x2, Pallas kernels: 5.85 us -> 3.95 us  [the longest x1 3.63 us: far_tile(): pl.pallas_call(body, in_specs=[scalar, scalar, anywhere, resident(), resi...]
  transfers between devices with their start and end apart: 9 -> 15, of which waited for: 7 -> 10; matrix products, arithmetic and copies ran while one was open for 0% -> 0% of each run, Pallas kernels for 15% -> 15%
where the time goes in v6:
time: 105 us
  waiting for transfers between devices  40.2 us (38%)
  Pallas kernels  39.2 us (37%)
  starting transfers between devices  25.1 us (24%)
    ppermute x3, waiting for transfers between devices, summed_output(): up = lambda x: lax.ppermute(x, 'head', rise)  19.2 us
    pallas_call x1, Pallas kernels, key_stage(): pl.pallas_call(body, grid=(heads // step,), in_specs=[pl.BlockSpec((tok,...  18.2 us
    ppermute x3, starting transfers between devices, summed_output(): down = lambda x: lax.ppermute(x, 'head', fall)  9.03 us
    all_to_all x1, waiting for transfers between devices, shards(): mine = lax.all_to_all(pair, 'ctx', 0, 0, axis_index_groups=groups)  8.44 us
    pallas_call x1, Pallas kernels, query_stage(): pl.pallas_call(body, grid=(heads // step,), in_specs=[pl.BlockSpec((tok,...  8.19 us
    ppermute x7, starting transfers between devices, shards(): lax.ppermute(states[step], 'ctx', [(i, i ^ step) for i in range(devices)])  8.15 us
    pallas_call x1, Pallas kernels, side_tiles(): pl.pallas_call(sides_kernel, grid_spec=pltpu.PrefetchScalarGridSpec(num_s...  4.77 us
    ppermute x1, waiting for transfers between devices, shards(): lax.ppermute(end, 'ctx', [(i, i + span) for i in range(devices - span)])  4.48 us
  transfers between devices with their start and end apart: 15, of which 10 were waited for; matrix products, arithmetic and copies ran while one was open for 0% of the time, Pallas kernels for 15%

profile of v6, /device:TPU:128, one launch (start us, length us, event | category | flops | bytes accessed | tf_op | source)
XLA Modules:
  0.0 104.6 jit_solution(9575211530553560746)
XLA Ops:
  0.0 18.2 %key_stage.1 = (f32[8,136,256]{2,1,0:T(8,128)}, bf16[8,4,128,512]{3,2,1,0:T(8,128)(2,1)}, bf16[8,3,128,512]{3,2,1,0:T(8,128)(2,1)}, f32[8,32,128]{2,1,0:T(8,128)}) custom-call(bf16[256,2,1024]{2,1,0:T(2,128)(2,1)} %refs_1_.3, bf16[256,2,1024]{2,1,0:T(2,128)(2,1)} %refs_1_.2, f32[2,8,256]{2,1,0:T(8,128)} %refs_2_.1, f32[8,256]{1,0:T(8,128)} %refs_3_.1, ...), custom_call_target="tpu_custom_call" | custom-call | tf_op jit(solution)/shard_map/key_stage/pallas_call | solution.py:249
  18.2 4.3 %all-to-all-start = ((f32[8,136,256]{2,1,0:T(8,128)}), f32[8,136,256]{2,1,0:T(8,128)S(1)}, u32[]{:S(2)}, u32[]{:S(2)}) async-start(f32[8,136,256]{2,1,0:T(8,128)} %get-tuple-element.36), calls=%async_computation | async-start | bytes 2228224 | tf_op jit(solution)/shard_map/all_to_all | solution.py:509
  22.5 8.2 %query_stage.1 = (f32[256,1024]{1,0:T(8,128)}, f32[256,1024]{1,0:T(8,128)S(1)}) custom-call(bf16[256,1024]{1,0:T(8,128)(2,1)} %refs_0_.3, bf16[256,2,1024]{2,1,0:T(2,128)(2,1)} %refs_1_.3, bf16[8,4,128,512]{3,2,1,0:T(8,128)(2,1)} %get-tuple-element.37.refs_2_, bf16[8,3,128,512]{3,2,1,0:T(8,128)(2,1)} %get-tuple-element.38.refs_3_, ...), custom_call_target="tpu_custom_call" | custom-call | tf_op jit(solution)/shard_map/query_stage/pallas_call | solution.py:281
  30.7 8.4 %all-to-all-done.in_ref = f32[8,136,256]{2,1,0:T(8,128)S(1)} async-done(((f32[8,136,256]{2,1,0:T(8,128)}), f32[8,136,256]{2,1,0:T(8,128)S(1)}, u32[]{:S(2)}, u32[]{:S(2)}) %all-to-all-start) | async-done | bytes 1114144 | tf_op jit(solution)/shard_map/all_to_all | solution.py:509
  39.1 0.7 prefix_stage.1
  39.9 2.9 %collective-permute-start = (f32[136,128]{1,0:T(8,128)S(1)}, f32[136,128]{1,0:T(8,128)S(1)}, u32[]{:S(2)}, u32[]{:S(2)}) collective-permute-start(f32[136,128]{1,0:T(8,128)S(1)} %get-tuple-element.47), channel_id=1, source_target_pairs={{0,32},{4,36},{8,40},{12,44},{16,48},{20,52},{24,56},{28,60},{32,6... | collective-permute-start | bytes 208904 | tf_op jit(solution)/shard_map/ppermute | solution.py:520
  42.8 4.5 %collective-permute-done.end_ref = f32[136,128]{1,0:T(8,128)S(1)} collective-permute-done((f32[136,128]{1,0:T(8,128)S(1)}, f32[136,128]{1,0:T(8,128)S(1)}, u32[]{:S(2)}, u32[]{:S(2)}) %collective-permute-start) | collective-permute-done | bytes 69664 | tf_op jit(solution)/shard_map/ppermute | solution.py:520
  47.3 0.3 incoming_stage.1
  47.6 0.1 collective-permute-start.1
  47.7 0.6 collective-permute-start.2
  48.3 1.2 %collective-permute-start.3 = (f32[128,128]{1,0:T(8,128)S(1)}, f32[128,128]{1,0:T(8,128)S(1)}, u32[]{:S(2)}, u32[]{:S(2)}) collective-permute-start(f32[128,128]{1,0:T(8,128)S(1)} %get-tuple-element.51), channel_id=1, source_target_pairs={{0,12},{4,8},{8,4},{12,0},{16,28},{20,24},{24,20},{28,16},{32,44},... | collective-permute-start | bytes 196616 | tf_op jit(solution)/shard_map/ppermute | solution.py:531
  49.5 0.9 collective-permute-start.4
  50.4 2.3 %collective-permute-start.5 = (f32[128,128]{1,0:T(8,128)S(1)}, f32[128,128]{1,0:T(8,128)S(1)}, u32[]{:S(2)}, u32[]{:S(2)}) collective-permute-start(f32[128,128]{1,0:T(8,128)S(1)} %get-tuple-element.53), channel_id=1, source_target_pairs={{0,20},{4,16},{8,28},{12,24},{16,4},{20,0},{24,12},{28,8},{32,52},... | collective-permute-start | bytes 196616 | tf_op jit(solution)/shard_map/ppermute | solution.py:531
  52.8 0.0 collective-permute-done.1.refs_7_
  52.8 1.2 %collective-permute-start.6 = (f32[128,128]{1,0:T(8,128)S(1)}, f32[128,128]{1,0:T(8,128)S(1)}, u32[]{:S(2)}, u32[]{:S(2)}) collective-permute-start(f32[128,128]{1,0:T(8,128)S(1)} %get-tuple-element.54), channel_id=1, source_target_pairs={{0,24},{4,28},{8,16},{12,20},{16,8},{20,12},{24,0},{28,4},{32,56},... | collective-permute-start | bytes 196616 | tf_op jit(solution)/shard_map/ppermute | solution.py:531
  54.0 0.0 collective-permute-done.2.refs_8_
  54.0 1.8 %collective-permute-start.7 = (f32[128,128]{1,0:T(8,128)S(1)}, f32[128,128]{1,0:T(8,128)S(1)}, u32[]{:S(2)}, u32[]{:S(2)}) collective-permute-start(f32[128,128]{1,0:T(8,128)S(1)} %get-tuple-element.55), channel_id=1, source_target_pairs={{0,28},{4,24},{8,20},{12,16},{16,12},{20,8},{24,4},{28,0},{32,60},... | collective-permute-start | bytes 196616 | tf_op jit(solution)/shard_map/ppermute | solution.py:531
  55.8 0.0 collective-permute-done.3.refs_9_
  55.8 0.2 collective-permute-done.4.refs_10_
  56.0 0.6 collective-permute-done.5.refs_11_
  56.6 2.1 %collective-permute-done.6.refs_12_ = f32[128,128]{1,0:T(8,128)S(1)} collective-permute-done((f32[128,128]{1,0:T(8,128)S(1)}, f32[128,128]{1,0:T(8,128)S(1)}, u32[]{:S(2)}, u32[]{:S(2)}) %collective-permute-start.6) | collective-permute-done | bytes 65568 | tf_op jit(solution)/shard_map/ppermute | solution.py:531
  58.7 0.9 collective-permute-done.7.refs_13_
  59.6 3.6 %far_tile.1 = (bf16[256,1024]{1,0:T(8,128)(2,1)}, f32[128,1024]{1,0:T(8,128)S(1)}, f32[128,1024]{1,0:T(8,128)S(1)}) custom-call(s32[1]{0:T(128)} %bitcast.refs_0_.pick_ref, s32[1]{0:T(128)} %bitcast.1.spot_ref.refs_1_, f32[256,1024]{1,0:T(8,128)} %get-tuple-element.42.refs_2_, f32[256,1024]{1,0:T(8,128)S(1)} %get-tuple-element.43.refs_3_, ...), custom_call_target="tpu_custom_call" | custom-call | tf_op jit(solution)/shard_map/far_tile/pallas_call | solution.py:378
  63.2 3.1 %collective-permute-start.10 = (f32[128,1024]{1,0:T(8,128)S(1)}, f32[128,1024]{1,0:T(8,128)S(1)}, u32[]{:S(2)}, u32[]{:S(2)}) collective-permute-start(f32[128,1024]{1,0:T(8,128)S(1)} %get-tuple-element.62), channel_id=1, source_target_pairs={{0,3},{1,0},{2,1},{3,2},{4,7},{5,4},{6,5},{7,6},{8,11},{9,8},{10,9... | collective-permute-start | bytes 1572872 | tf_op jit(solution)/shard_map/ppermute | solution.py:482
  66.3 0.0 collective-permute-start.9
  66.3 4.8 %side_tiles.1 = (f32[128,1024]{1,0:T(8,128)}, f32[128,1024]{1,0:T(8,128)}, f32[128,1024]{1,0:T(8,128)S(1)}, f32[128,1024]{1,0:T(8,128)S(1)}) custom-call(s32[1]{0:T(128)} %bitcast.refs_0_.pick_ref, bf16[256,1024]{1,0:T(8,128)(2,1)} %get-tuple-element.56.normed_ref, bf16[1024,4096]{1,0:T(8,128)(2,1)} %last_w_ref.1, bf16[1024,4096]{1,0:T(8,128)(2,1)} %last_w_ref.1), custom_call_target="tpu_custom_call" | custom-call | tf_op jit(solution)/shard_map/side_tiles/pallas_call | solution.py:453
  71.1 0.6 collective-permute-start.12
  71.6 2.7 %collective-permute-start.8 = (f32[128,1024]{1,0:T(8,128)}, f32[128,1024]{1,0:T(8,128)S(1)}, u32[]{:S(2)}, u32[]{:S(2)}) collective-permute-start(f32[128,1024]{1,0:T(8,128)} %get-tuple-element.58), channel_id=1, source_target_pairs={{0,3},{1,0},{2,1},{3,2},{4,7},{5,4},{6,5},{7,6},{8,11},{9,8},{10,9... | collective-permute-start | bytes 1572872 | tf_op jit(solution)/shard_map/ppermute | solution.py:482
  74.3 4.3 %collective-permute-done.10.gb_ref = f32[128,1024]{1,0:T(8,128)S(1)} collective-permute-done((f32[128,1024]{1,0:T(8,128)S(1)}, f32[128,1024]{1,0:T(8,128)S(1)}, u32[]{:S(2)}, u32[]{:S(2)}) %collective-permute-start.10) | collective-permute-done | bytes 524320 | tf_op jit(solution)/shard_map/ppermute | solution.py:482
  78.6 3.7 %collective-permute-done.9.gt_ref = f32[128,1024]{1,0:T(8,128)S(1)} collective-permute-done((f32[128,1024]{1,0:T(8,128)S(1)}, f32[128,1024]{1,0:T(8,128)S(1)}, u32[]{:S(2)}, u32[]{:S(2)}) %collective-permute-start.9) | collective-permute-done | bytes 524320 | tf_op jit(solution)/shard_map/ppermute | solution.py:481
  82.3 0.1 join_tiles.1
  82.4 0.1 collective-permute-start.11
  82.5 3.2 %collective-permute-start.13 = (f32[128,1024]{1,0:T(8,128)S(1)}, f32[128,1024]{1,0:T(8,128)S(1)}, u32[]{:S(2)}, u32[]{:S(2)}) collective-permute-start(f32[128,1024]{1,0:T(8,128)S(1)} %get-tuple-element.66), channel_id=1, source_target_pairs={{0,3},{1,0},{2,1},{3,2},{4,7},{5,4},{6,5},{7,6},{8,11},{9,8},{10,9... | collective-permute-start | bytes 1572872 | tf_op jit(solution)/shard_map/ppermute | solution.py:482
  85.7 2.3 %shard_map.82 = (f32[128,1024]{1,0:T(8,128)S(1)}, f32[128,1024]{1,0:T(8,128)S(1)}) custom-call(s32[1]{0:T(128)} %bitcast.refs_0_.pick_ref, bf16[256,1024]{1,0:T(8,128)(2,1)} %get-tuple-element.56.normed_ref, bf16[1024,4096]{1,0:T(8,128)(2,1)} %last_w_ref.1), custom_call_target="tpu_custom_call" | custom-call | tf_op jit(solution)/shard_map/pallas_call | solution.py:427
  88.1 5.5 %collective-permute-done.12.sb_ref = f32[128,1024]{1,0:T(8,128)S(1)} collective-permute-done((f32[128,1024]{1,0:T(8,128)}, f32[128,1024]{1,0:T(8,128)S(1)}, u32[]{:S(2)}, u32[]{:S(2)}) %collective-permute-start.12) | collective-permute-done | bytes 524320 | tf_op jit(solution)/shard_map/ppermute | solution.py:481
  93.5 0.0 collective-permute-done.8.st_ref
  93.5 10.1 %collective-permute-done.11.gt_ref = f32[128,1024]{1,0:T(8,128)S(1)} collective-permute-done((f32[128,1024]{1,0:T(8,128)S(1)}, f32[128,1024]{1,0:T(8,128)S(1)}, u32[]{:S(2)}, u32[]{:S(2)}) %collective-permute-start.11) | collective-permute-done | bytes 524320 | tf_op jit(solution)/shard_map/ppermute | solution.py:481
  103.6 0.0 collective-permute-done.13.gb_ref
  103.6 0.9 finish.1
Async XLA Ops:
  18.2 20.9 %all-to-all-start = ((f32[8,136,256]{2,1,0:T(8,128)}), f32[8,136,256]{2,1,0:T(8,128)S(1)}, u32[]{:S(2)}, u32[]{:S(2)}) async-start(f32[8,136,256]{2,1,0:T(8,128)} %get-tuple-element.36), calls=%async_computation | async-start | bytes 2228224 | tf_op jit(solution)/shard_map/all_to_all | solution.py:509
  39.9 7.4 %collective-permute-start = (f32[136,128]{1,0:T(8,128)S(1)}, f32[136,128]{1,0:T(8,128)S(1)}, u32[]{:S(2)}, u32[]{:S(2)}) collective-permute-start(f32[136,128]{1,0:T(8,128)S(1)} %get-tuple-element.47), channel_id=1, source_target_pairs={{0,32},{4,36},{8,40},{12,44},{16,48},{20,52},{24,56},{28,60},{32,6... | collective-permute-start | bytes 208904 | tf_op jit(solution)/shard_map/ppermute | solution.py:520
  47.6 5.2 %collective-permute-start.1 = (f32[128,128]{1,0:T(8,128)S(1)}, f32[128,128]{1,0:T(8,128)S(1)}, u32[]{:S(2)}, u32[]{:S(2)}) collective-permute-start(f32[128,128]{1,0:T(8,128)S(1)} %get-tuple-element.49), channel_id=1, source_target_pairs={{0,4},{4,0},{8,12},{12,8},{16,20},{20,16},{24,28},{28,24},{32,36},... | collective-permute-start | bytes 196616 | tf_op jit(solution)/shard_map/ppermute | solution.py:531
  47.7 6.3 %collective-permute-start.2 = (f32[128,128]{1,0:T(8,128)S(1)}, f32[128,128]{1,0:T(8,128)S(1)}, u32[]{:S(2)}, u32[]{:S(2)}) collective-permute-start(f32[128,128]{1,0:T(8,128)S(1)} %get-tuple-element.50), channel_id=1, source_target_pairs={{0,8},{4,12},{8,0},{12,4},{16,24},{20,28},{24,16},{28,20},{32,40},... | collective-permute-start | bytes 196616 | tf_op jit(solution)/shard_map/ppermute | solution.py:531
  48.3 7.4 %collective-permute-start.3 = (f32[128,128]{1,0:T(8,128)S(1)}, f32[128,128]{1,0:T(8,128)S(1)}, u32[]{:S(2)}, u32[]{:S(2)}) collective-permute-start(f32[128,128]{1,0:T(8,128)S(1)} %get-tuple-element.51), channel_id=1, source_target_pairs={{0,12},{4,8},{8,4},{12,0},{16,28},{20,24},{24,20},{28,16},{32,44},... | collective-permute-start | bytes 196616 | tf_op jit(solution)/shard_map/ppermute | solution.py:531
  49.5 6.5 %collective-permute-start.4 = (f32[128,128]{1,0:T(8,128)S(1)}, f32[128,128]{1,0:T(8,128)S(1)}, u32[]{:S(2)}, u32[]{:S(2)}) collective-permute-start(f32[128,128]{1,0:T(8,128)S(1)} %get-tuple-element.52), channel_id=1, source_target_pairs={{0,16},{4,20},{8,24},{12,28},{16,0},{20,4},{24,8},{28,12},{32,48},... | collective-permute-start | bytes 196616 | tf_op jit(solution)/shard_map/ppermute | solution.py:531
  50.4 6.2 %collective-permute-start.5 = (f32[128,128]{1,0:T(8,128)S(1)}, f32[128,128]{1,0:T(8,128)S(1)}, u32[]{:S(2)}, u32[]{:S(2)}) collective-permute-start(f32[128,128]{1,0:T(8,128)S(1)} %get-tuple-element.53), channel_id=1, source_target_pairs={{0,20},{4,16},{8,28},{12,24},{16,4},{20,0},{24,12},{28,8},{32,52},... | collective-permute-start | bytes 196616 | tf_op jit(solution)/shard_map/ppermute | solution.py:531
  52.8 5.9 %collective-permute-start.6 = (f32[128,128]{1,0:T(8,128)S(1)}, f32[128,128]{1,0:T(8,128)S(1)}, u32[]{:S(2)}, u32[]{:S(2)}) collective-permute-start(f32[128,128]{1,0:T(8,128)S(1)} %get-tuple-element.54), channel_id=1, source_target_pairs={{0,24},{4,28},{8,16},{12,20},{16,8},{20,12},{24,0},{28,4},{32,56},... | collective-permute-start | bytes 196616 | tf_op jit(solution)/shard_map/ppermute | solution.py:531
  54.0 5.6 %collective-permute-start.7 = (f32[128,128]{1,0:T(8,128)S(1)}, f32[128,128]{1,0:T(8,128)S(1)}, u32[]{:S(2)}, u32[]{:S(2)}) collective-permute-start(f32[128,128]{1,0:T(8,128)S(1)} %get-tuple-element.55), channel_id=1, source_target_pairs={{0,28},{4,24},{8,20},{12,16},{16,12},{20,8},{24,4},{28,0},{32,60},... | collective-permute-start | bytes 196616 | tf_op jit(solution)/shard_map/ppermute | solution.py:531
  63.2 15.4 %collective-permute-start.10 = (f32[128,1024]{1,0:T(8,128)S(1)}, f32[128,1024]{1,0:T(8,128)S(1)}, u32[]{:S(2)}, u32[]{:S(2)}) collective-permute-start(f32[128,1024]{1,0:T(8,128)S(1)} %get-tuple-element.62), channel_id=1, source_target_pairs={{0,3},{1,0},{2,1},{3,2},{4,7},{5,4},{6,5},{7,6},{8,11},{9,8},{10,9... | collective-permute-start | bytes 1572872 | tf_op jit(solution)/shard_map/ppermute | solution.py:482
  66.3 16.0 %collective-permute-start.9 = (f32[128,1024]{1,0:T(8,128)S(1)}, f32[128,1024]{1,0:T(8,128)S(1)}, u32[]{:S(2)}, u32[]{:S(2)}) collective-permute-start(f32[128,1024]{1,0:T(8,128)S(1)} %get-tuple-element.60), channel_id=1, source_target_pairs={{0,1},{1,2},{2,3},{3,0},{4,5},{5,6},{6,7},{7,4},{8,9},{9,10},{10,1... | collective-permute-start | bytes 1572872 | tf_op jit(solution)/shard_map/ppermute | solution.py:481
  71.1 22.5 %collective-permute-start.12 = (f32[128,1024]{1,0:T(8,128)}, f32[128,1024]{1,0:T(8,128)S(1)}, u32[]{:S(2)}, u32[]{:S(2)}) collective-permute-start(f32[128,1024]{1,0:T(8,128)} %get-tuple-element.65), channel_id=1, source_target_pairs={{0,1},{1,2},{2,3},{3,0},{4,5},{5,6},{6,7},{7,4},{8,9},{9,10},{10,1... | collective-permute-start | bytes 1572872 | tf_op jit(solution)/shard_map/ppermute | solution.py:481
  71.6 21.9 %collective-permute-start.8 = (f32[128,1024]{1,0:T(8,128)}, f32[128,1024]{1,0:T(8,128)S(1)}, u32[]{:S(2)}, u32[]{:S(2)}) collective-permute-start(f32[128,1024]{1,0:T(8,128)} %get-tuple-element.58), channel_id=1, source_target_pairs={{0,3},{1,0},{2,1},{3,2},{4,7},{5,4},{6,5},{7,6},{8,11},{9,8},{10,9... | collective-permute-start | bytes 1572872 | tf_op jit(solution)/shard_map/ppermute | solution.py:482
  82.4 21.2 %collective-permute-start.11 = (f32[128,1024]{1,0:T(8,128)S(1)}, f32[128,1024]{1,0:T(8,128)S(1)}, u32[]{:S(2)}, u32[]{:S(2)}) collective-permute-start(f32[128,1024]{1,0:T(8,128)S(1)} %get-tuple-element.63), channel_id=1, source_target_pairs={{0,1},{1,2},{2,3},{3,0},{4,5},{5,6},{6,7},{7,4},{8,9},{9,10},{10,1... | collective-permute-start | bytes 1572872 | tf_op jit(solution)/shard_map/ppermute | solution.py:481
  82.5 21.1 %collective-permute-start.13 = (f32[128,1024]{1,0:T(8,128)S(1)}, f32[128,1024]{1,0:T(8,128)S(1)}, u32[]{:S(2)}, u32[]{:S(2)}) collective-permute-start(f32[128,1024]{1,0:T(8,128)S(1)} %get-tuple-element.66), channel_id=1, source_target_pairs={{0,3},{1,0},{2,1},{3,2},{4,7},{5,4},{6,5},{7,6},{8,11},{9,8},{10,9... | collective-permute-start | bytes 1572872 | tf_op jit(solution)/shard_map/ppermute | solution.py:482

commit v7 on v5

--- a/solution.py
+++ b/solution.py
@@ -336,26 +336,33 @@
         out_ref[i] = mm(ex_ref[i, :, :DK], state) + ex_ref[i, :, DK:]
 
 
-def far_kernel(pick_ref, local_ref, map_ref, state_ref, gain_ref, weight_ref, normed_ref, up_ref, down_ref):
-    heads = state_ref.shape[0]
-
-    @pl.when(pl.program_id(0) == 0)
-    def _():
-        for h in range(heads):
-            lanes = slice(h * DV, (h + 1) * DV)
-            attended = local_ref[:, lanes] + mm(map_ref[:, lanes], state_ref[h])
-            mean = jnp.mean(attended * attended, axis=1, keepdims=True)
-            normed_ref[:, lanes] = (attended * lax.rsqrt(mean + EPS) * gain_ref[:, lanes]).astype(BF16)
-
+def far_kernel(place_ref, local_ref, map_ref, state_ref, gain_ref, weight_ref, normed_ref, up_ref, down_ref,
+               columns_ref, own_ref, copied, read):
+    heads, width = state_ref.shape[0], up_ref.shape[1]
+    start = pl.multiple_of(((place_ref[0] + 2) & 3) * width, width)
+    bring = pltpu.make_async_copy(local_ref, own_ref, read)
+    bring.start()
+    load = pltpu.make_async_copy(weight_ref.at[:, pl.ds(start, width)], columns_ref, copied)
+    load.start()
+    read_out = [mm(map_ref[:, h * DV : (h + 1) * DV], state_ref[h]) for h in range(heads)]
+    bring.wait()
+    for h in range(heads):
+        lanes = slice(h * DV, (h + 1) * DV)
+        attended = own_ref[:, lanes] + read_out[h]
+        mean = jnp.mean(attended * attended, axis=1, keepdims=True)
+        normed_ref[:, lanes] = (attended * lax.rsqrt(mean + EPS) * gain_ref[:, lanes]).astype(BF16)
+    load.wait()
     half = up_ref.shape[0]
-    up_ref[...] = dotf(normed_ref[:half, :], weight_ref[...])
-    down_ref[...] = dotf(normed_ref[half:, :], weight_ref[...])
+    terms = dotf(normed_ref[...], columns_ref[...])
+    up_ref[...] = terms[:half]
+    down_ref[...] = terms[half:]
 
 
 def tile_kernel(pick_ref, normed_ref, weight_ref, top_ref, bottom_ref):
     half = top_ref.shape[0]
-    top_ref[...] = dotf(normed_ref[:half, :], weight_ref[...])
-    bottom_ref[...] = dotf(normed_ref[half:, :], weight_ref[...])
+    terms = dotf(normed_ref[...], weight_ref[...])
+    top_ref[...] = terms[:half]
+    bottom_ref[...] = terms[half:]
 
 
 def whole(*shape):
@@ -365,17 +372,14 @@
 def far_tile(place, local, mapped, state, gain, weight, width):
     tok, feats = local.shape
     part = pltpu.VMEM((tok // 2, width), F32)
-    steps = 4
-    cols = width // steps
-    out = pl.BlockSpec((tok // 2, cols), lambda i, at: (0, i))
+    anywhere = pl.BlockSpec(memory_space=pl.ANY)
     return pl.pallas_call(
         far_kernel,
-        grid_spec=pltpu.PrefetchScalarGridSpec(
-            num_scalar_prefetch=1, grid=(steps,),
-            in_specs=[whole(tok, feats), resident(), resident(), whole(1, feats),
-                      pl.BlockSpec((feats, cols), lambda i, at: (0, steps * ((at[0] + 2) & 3) + i))],
-            out_specs=[whole(tok, feats), out, out]),
+        in_specs=[pl.BlockSpec(memory_space=pltpu.SMEM), anywhere, resident(), resident(), resident(), anywhere],
+        out_specs=[resident()] * 3,
         out_shape=[jax.ShapeDtypeStruct((tok, feats), BF16), part, part],
+        scratch_shapes=[pltpu.VMEM((feats, width), BF16), pltpu.VMEM((tok, feats), F32),
+                        pltpu.SemaphoreType.DMA(()), pltpu.SemaphoreType.DMA(())],
         compiler_params=pltpu.CompilerParams(vmem_limit_bytes=57 << 20),
         name="far_tile",
     )(place, local, held(mapped), held(state), gain.reshape(1, feats), weight)
@@ -431,11 +435,12 @@
 
 def sides_kernel(pick_ref, normed_ref, next_w_ref, last_w_ref, nb_ref, lt_ref, nt_ref, lb_ref):
     half = nb_ref.shape[0]
-    top, bottom = normed_ref[:half, :], normed_ref[half:, :]
-    nb_ref[...] = dotf(bottom, next_w_ref[...])
-    lt_ref[...] = dotf(top, last_w_ref[...])
-    nt_ref[...] = dotf(top, next_w_ref[...])
-    lb_ref[...] = dotf(bottom, last_w_ref[...])
+    terms = dotf(normed_ref[...], next_w_ref[...])
+    nt_ref[...] = terms[:half]
+    nb_ref[...] = terms[half:]
+    terms = dotf(normed_ref[...], last_w_ref[...])
+    lt_ref[...] = terms[:half]
+    lb_ref[...] = terms[half:]
 
 
 def side_tiles(places, normed, weight, width):

time: 105 us -> 104 us (level)
  Pallas kernels: 41.1 us -> 40 us
    pallas_call x1, Pallas kernels: 4.73 us -> 3.42 us  [far_tile(): pl.pallas_call(far_kernel, in_specs=[pl.BlockSpec(memory_space=pltpu.SMEM...]
where the time goes in v7:
time: 104 us
  waiting for transfers between devices  44.3 us (43%)
  Pallas kernels  40 us (38%)
  starting transfers between devices  19.6 us (19%)
    pallas_call x1, Pallas kernels, key_stage(): pl.pallas_call(body, grid=(heads // step,), in_specs=[pl.BlockSpec((tok,...  18.1 us
    ppermute x3, waiting for transfers between devices, summed_output(): up = lambda x: lax.ppermute(x, 'head', rise)  15.3 us
    all_to_all x1, waiting for transfers between devices, shards(): states = lax.all_to_all(states, 'ctx', 0, 0, axis_index_groups=groups)  10.2 us
    all_to_all x1, waiting for transfers between devices, shards(): mine = lax.all_to_all(pair, 'ctx', 0, 0, axis_index_groups=groups)  8.43 us
    pallas_call x1, Pallas kernels, query_stage(): pl.pallas_call(body, grid=(heads // step,), in_specs=[pl.BlockSpec((tok,...  8.2 us
    ppermute x3, waiting for transfers between devices, summed_output(): down = lambda x: lax.ppermute(x, 'head', fall)  5.87 us
    ppermute x3, starting transfers between devices, summed_output(): down = lambda x: lax.ppermute(x, 'head', fall)  5.12 us
    pallas_call x1, Pallas kernels, side_tiles(): pl.pallas_call(sides_kernel, grid_spec=pltpu.PrefetchScalarGridSpec(num_s...  4.99 us
  transfers between devices with their start and end apart: 9, of which 7 were waited for; matrix products, arithmetic and copies ran while one was open for 0% of the time, Pallas kernels for 15%

profile of v7, /device:TPU:128, one launch (start us, length us, event | category | flops | bytes accessed | tf_op | source)
XLA Modules:
  0.0 103.9 jit_solution(12849522533797625703)
XLA Ops:
  0.0 18.1 %key_stage.1 = (f32[8,136,256]{2,1,0:T(8,128)}, bf16[8,4,128,512]{3,2,1,0:T(8,128)(2,1)}, bf16[8,3,128,512]{3,2,1,0:T(8,128)(2,1)}, f32[8,32,128]{2,1,0:T(8,128)}) custom-call(bf16[256,2,1024]{2,1,0:T(2,128)(2,1)} %refs_1_.3, bf16[256,2,1024]{2,1,0:T(2,128)(2,1)} %refs_1_.2, f32[2,8,256]{2,1,0:T(8,128)} %refs_2_.1, f32[8,256]{1,0:T(8,128)} %refs_3_.1, ...), custom_call_target="tpu_custom_call" | custom-call | tf_op jit(solution)/shard_map/key_stage/pallas_call | solution.py:249
  18.1 4.3 %all-to-all-start = ((f32[8,136,256]{2,1,0:T(8,128)}), f32[8,136,256]{2,1,0:T(8,128)S(1)}, u32[]{:S(2)}, u32[]{:S(2)}) async-start(f32[8,136,256]{2,1,0:T(8,128)} %get-tuple-element.28), calls=%async_computation | async-start | bytes 2228224 | tf_op jit(solution)/shard_map/all_to_all | solution.py:508
  22.4 8.2 %query_stage.1 = (f32[256,1024]{1,0:T(8,128)}, f32[256,1024]{1,0:T(8,128)S(1)}) custom-call(bf16[256,1024]{1,0:T(8,128)(2,1)} %refs_0_.3, bf16[256,2,1024]{2,1,0:T(2,128)(2,1)} %refs_1_.3, bf16[8,4,128,512]{3,2,1,0:T(8,128)(2,1)} %get-tuple-element.29.refs_2_, bf16[8,3,128,512]{3,2,1,0:T(8,128)(2,1)} %get-tuple-element.30.refs_3_, ...), custom_call_target="tpu_custom_call" | custom-call | tf_op jit(solution)/shard_map/query_stage/pallas_call | solution.py:281
  30.6 8.4 %all-to-all-done.in_ref = f32[8,136,256]{2,1,0:T(8,128)S(1)} async-done(((f32[8,136,256]{2,1,0:T(8,128)}), f32[8,136,256]{2,1,0:T(8,128)S(1)}, u32[]{:S(2)}, u32[]{:S(2)}) %all-to-all-start) | async-done | bytes 1114144 | tf_op jit(solution)/shard_map/all_to_all | solution.py:508
  39.1 0.7 prefix_stage.1
  39.8 2.9 %collective-permute-start = (f32[136,128]{1,0:T(8,128)S(1)}, f32[136,128]{1,0:T(8,128)S(1)}, u32[]{:S(2)}, u32[]{:S(2)}) collective-permute-start(f32[136,128]{1,0:T(8,128)S(1)} %get-tuple-element.39), channel_id=1, source_target_pairs={{0,32},{4,36},{8,40},{12,44},{16,48},{20,52},{24,56},{28,60},{32,6... | collective-permute-start | bytes 208904 | tf_op jit(solution)/shard_map/ppermute | solution.py:519
  42.8 4.5 %collective-permute-done.end_ref = f32[136,128]{1,0:T(8,128)S(1)} collective-permute-done((f32[136,128]{1,0:T(8,128)S(1)}, f32[136,128]{1,0:T(8,128)S(1)}, u32[]{:S(2)}, u32[]{:S(2)}) %collective-permute-start) | collective-permute-done | bytes 69664 | tf_op jit(solution)/shard_map/ppermute | solution.py:519
  47.2 1.1 %incoming_stage.1 = f32[8,128,128]{2,1,0:T(8,128)} custom-call(f32[8,128]{1,0:T(8,128)S(1)} %get-tuple-element.37.ends_ref, f32[8,128,256]{2,1,0:T(8,128)S(1)} %get-tuple-element.38.ex_ref, f32[136,128]{1,0:T(8,128)S(1)} %collective-permute-done.end_ref), custom_call_target="tpu_custom_call" | custom-call | tf_op jit(solution)/shard_map/incoming_stage/pallas_call | solution.py:520
  48.4 3.5 %all-to-all-start.1 = ((f32[8,128,128]{2,1,0:T(8,128)}), f32[8,128,128]{2,1,0:T(8,128)S(1)}, u32[]{:S(2)}, u32[]{:S(2)}) async-start(f32[8,128,128]{2,1,0:T(8,128)} %incoming_stage.1), calls=%async_computation.1 | async-start | bytes 1048576 | tf_op jit(solution)/shard_map/all_to_all | solution.py:528
  51.9 10.2 %all-to-all-done.1.state_ref = f32[8,128,128]{2,1,0:T(8,128)S(1)} async-done(((f32[8,128,128]{2,1,0:T(8,128)}), f32[8,128,128]{2,1,0:T(8,128)S(1)}, u32[]{:S(2)}, u32[]{:S(2)}) %all-to-all-start.1) | async-done | bytes 524320 | tf_op jit(solution)/shard_map/all_to_all | solution.py:528
  62.1 3.4 %far_tile.1 = (bf16[256,1024]{1,0:T(8,128)(2,1)}, f32[128,1024]{1,0:T(8,128)S(1)}, f32[128,1024]{1,0:T(8,128)S(1)}) custom-call(s32[1]{0:T(128)} %bitcast.place_ref.pick_ref, f32[256,1024]{1,0:T(8,128)} %get-tuple-element.34.local_ref, f32[256,1024]{1,0:T(8,128)S(1)} %get-tuple-element.35.map_ref, f32[8,128,128]{2,1,0:T(8,128)S(1)} %all-to-all-done.1.state_ref, ...), custom_call_target="tpu_custom_call" | custom-call | tf_op jit(solution)/shard_map/far_tile/pallas_call | solution.py:376
  65.5 1.8 %collective-permute-start.2 = (f32[128,1024]{1,0:T(8,128)S(1)}, f32[128,1024]{1,0:T(8,128)S(1)}, u32[]{:S(2)}, u32[]{:S(2)}) collective-permute-start(f32[128,1024]{1,0:T(8,128)S(1)} %get-tuple-element.44), channel_id=1, source_target_pairs={{0,1},{1,2},{2,3},{3,0},{4,5},{5,6},{6,7},{7,4},{8,9},{9,10},{10,1... | collective-permute-start | bytes 1572872 | tf_op jit(solution)/shard_map/ppermute | solution.py:480
  67.4 1.7 %collective-permute-start.3 = (f32[128,1024]{1,0:T(8,128)S(1)}, f32[128,1024]{1,0:T(8,128)S(1)}, u32[]{:S(2)}, u32[]{:S(2)}) collective-permute-start(f32[128,1024]{1,0:T(8,128)S(1)} %get-tuple-element.46), channel_id=1, source_target_pairs={{0,3},{1,0},{2,1},{3,2},{4,7},{5,4},{6,5},{7,6},{8,11},{9,8},{10,9... | collective-permute-start | bytes 1572872 | tf_op jit(solution)/shard_map/ppermute | solution.py:481
  69.0 5.0 %side_tiles.1 = (f32[128,1024]{1,0:T(8,128)}, f32[128,1024]{1,0:T(8,128)}, f32[128,1024]{1,0:T(8,128)S(1)}, f32[128,1024]{1,0:T(8,128)S(1)}) custom-call(s32[1]{0:T(128)} %bitcast.place_ref.pick_ref, bf16[256,1024]{1,0:T(8,128)(2,1)} %get-tuple-element.40.normed_ref, bf16[1024,4096]{1,0:T(8,128)(2,1)} %last_w_ref.1, bf16[1024,4096]{1,0:T(8,128)(2,1)} %last_w_ref.1), custom_call_target="tpu_custom_call" | custom-call | tf_op jit(solution)/shard_map/side_tiles/pallas_call | solution.py:452
  74.0 1.8 %collective-permute-start.1 = (f32[128,1024]{1,0:T(8,128)}, f32[128,1024]{1,0:T(8,128)S(1)}, u32[]{:S(2)}, u32[]{:S(2)}) collective-permute-start(f32[128,1024]{1,0:T(8,128)} %get-tuple-element.42), channel_id=1, source_target_pairs={{0,3},{1,0},{2,1},{3,2},{4,7},{5,4},{6,5},{7,6},{8,11},{9,8},{10,9... | collective-permute-start | bytes 1572872 | tf_op jit(solution)/shard_map/ppermute | solution.py:481
  75.8 0.2 collective-permute-start.5
  76.0 5.7 %collective-permute-done.2.gt_ref = f32[128,1024]{1,0:T(8,128)S(1)} collective-permute-done((f32[128,1024]{1,0:T(8,128)S(1)}, f32[128,1024]{1,0:T(8,128)S(1)}, u32[]{:S(2)}, u32[]{:S(2)}) %collective-permute-start.2) | collective-permute-done | bytes 524320 | tf_op jit(solution)/shard_map/ppermute | solution.py:480
  81.8 0.4 collective-permute-done.3.gb_ref
  82.2 0.1 join_tiles.1
  82.3 1.7 %collective-permute-start.4 = (f32[128,1024]{1,0:T(8,128)S(1)}, f32[128,1024]{1,0:T(8,128)S(1)}, u32[]{:S(2)}, u32[]{:S(2)}) collective-permute-start(f32[128,1024]{1,0:T(8,128)S(1)} %get-tuple-element.47), channel_id=1, source_target_pairs={{0,1},{1,2},{2,3},{3,0},{4,5},{5,6},{6,7},{7,4},{8,9},{9,10},{10,1... | collective-permute-start | bytes 1572872 | tf_op jit(solution)/shard_map/ppermute | solution.py:480
  83.9 1.7 %collective-permute-start.6 = (f32[128,1024]{1,0:T(8,128)S(1)}, f32[128,1024]{1,0:T(8,128)S(1)}, u32[]{:S(2)}, u32[]{:S(2)}) collective-permute-start(f32[128,1024]{1,0:T(8,128)S(1)} %get-tuple-element.50), channel_id=1, source_target_pairs={{0,3},{1,0},{2,1},{3,2},{4,7},{5,4},{6,5},{7,6},{8,11},{9,8},{10,9... | collective-permute-start | bytes 1572872 | tf_op jit(solution)/shard_map/ppermute | solution.py:481
  85.6 2.3 %shard_map.82 = (f32[128,1024]{1,0:T(8,128)S(1)}, f32[128,1024]{1,0:T(8,128)S(1)}) custom-call(s32[1]{0:T(128)} %bitcast.place_ref.pick_ref, bf16[256,1024]{1,0:T(8,128)(2,1)} %get-tuple-element.40.normed_ref, bf16[1024,4096]{1,0:T(8,128)(2,1)} %last_w_ref.1), custom_call_target="tpu_custom_call" | custom-call | tf_op jit(solution)/shard_map/pallas_call | solution.py:425
  87.9 5.5 %collective-permute-done.1.st_ref = f32[128,1024]{1,0:T(8,128)S(1)} collective-permute-done((f32[128,1024]{1,0:T(8,128)}, f32[128,1024]{1,0:T(8,128)S(1)}, u32[]{:S(2)}, u32[]{:S(2)}) %collective-permute-start.1) | collective-permute-done | bytes 524320 | tf_op jit(solution)/shard_map/ppermute | solution.py:481
  93.4 0.0 collective-permute-done.5.sb_ref
  93.4 9.5 %collective-permute-done.4.gt_ref = f32[128,1024]{1,0:T(8,128)S(1)} collective-permute-done((f32[128,1024]{1,0:T(8,128)S(1)}, f32[128,1024]{1,0:T(8,128)S(1)}, u32[]{:S(2)}, u32[]{:S(2)}) %collective-permute-start.4) | collective-permute-done | bytes 524320 | tf_op jit(solution)/shard_map/ppermute | solution.py:480
  102.9 0.0 collective-permute-done.6.gb_ref
  102.9 0.9 finish.1
Async XLA Ops:
  18.1 20.9 %all-to-all-start = ((f32[8,136,256]{2,1,0:T(8,128)}), f32[8,136,256]{2,1,0:T(8,128)S(1)}, u32[]{:S(2)}, u32[]{:S(2)}) async-start(f32[8,136,256]{2,1,0:T(8,128)} %get-tuple-element.28), calls=%async_computation | async-start | bytes 2228224 | tf_op jit(solution)/shard_map/all_to_all | solution.py:508
  39.8 7.4 %collective-permute-start = (f32[136,128]{1,0:T(8,128)S(1)}, f32[136,128]{1,0:T(8,128)S(1)}, u32[]{:S(2)}, u32[]{:S(2)}) collective-permute-start(f32[136,128]{1,0:T(8,128)S(1)} %get-tuple-element.39), channel_id=1, source_target_pairs={{0,32},{4,36},{8,40},{12,44},{16,48},{20,52},{24,56},{28,60},{32,6... | collective-permute-start | bytes 208904 | tf_op jit(solution)/shard_map/ppermute | solution.py:519
  48.4 13.7 %all-to-all-start.1 = ((f32[8,128,128]{2,1,0:T(8,128)}), f32[8,128,128]{2,1,0:T(8,128)S(1)}, u32[]{:S(2)}, u32[]{:S(2)}) async-start(f32[8,128,128]{2,1,0:T(8,128)} %incoming_stage.1), calls=%async_computation.1 | async-start | bytes 1048576 | tf_op jit(solution)/shard_map/all_to_all | solution.py:528
  65.5 16.3 %collective-permute-start.2 = (f32[128,1024]{1,0:T(8,128)S(1)}, f32[128,1024]{1,0:T(8,128)S(1)}, u32[]{:S(2)}, u32[]{:S(2)}) collective-permute-start(f32[128,1024]{1,0:T(8,128)S(1)} %get-tuple-element.44), channel_id=1, source_target_pairs={{0,1},{1,2},{2,3},{3,0},{4,5},{5,6},{6,7},{7,4},{8,9},{9,10},{10,1... | collective-permute-start | bytes 1572872 | tf_op jit(solution)/shard_map/ppermute | solution.py:480
  67.4 14.8 %collective-permute-start.3 = (f32[128,1024]{1,0:T(8,128)S(1)}, f32[128,1024]{1,0:T(8,128)S(1)}, u32[]{:S(2)}, u32[]{:S(2)}) collective-permute-start(f32[128,1024]{1,0:T(8,128)S(1)} %get-tuple-element.46), channel_id=1, source_target_pairs={{0,3},{1,0},{2,1},{3,2},{4,7},{5,4},{6,5},{7,6},{8,11},{9,8},{10,9... | collective-permute-start | bytes 1572872 | tf_op jit(solution)/shard_map/ppermute | solution.py:481
  74.0 19.4 %collective-permute-start.1 = (f32[128,1024]{1,0:T(8,128)}, f32[128,1024]{1,0:T(8,128)S(1)}, u32[]{:S(2)}, u32[]{:S(2)}) collective-permute-start(f32[128,1024]{1,0:T(8,128)} %get-tuple-element.42), channel_id=1, source_target_pairs={{0,3},{1,0},{2,1},{3,2},{4,7},{5,4},{6,5},{7,6},{8,11},{9,8},{10,9... | collective-permute-start | bytes 1572872 | tf_op jit(solution)/shard_map/ppermute | solution.py:481
  75.8 17.6 %collective-permute-start.5 = (f32[128,1024]{1,0:T(8,128)}, f32[128,1024]{1,0:T(8,128)S(1)}, u32[]{:S(2)}, u32[]{:S(2)}) collective-permute-start(f32[128,1024]{1,0:T(8,128)} %get-tuple-element.49), channel_id=1, source_target_pairs={{0,1},{1,2},{2,3},{3,0},{4,5},{5,6},{6,7},{7,4},{8,9},{9,10},{10,1... | collective-permute-start | bytes 1572872 | tf_op jit(solution)/shard_map/ppermute | solution.py:480
  82.3 20.6 %collective-permute-start.4 = (f32[128,1024]{1,0:T(8,128)S(1)}, f32[128,1024]{1,0:T(8,128)S(1)}, u32[]{:S(2)}, u32[]{:S(2)}) collective-permute-start(f32[128,1024]{1,0:T(8,128)S(1)} %get-tuple-element.47), channel_id=1, source_target_pairs={{0,1},{1,2},{2,3},{3,0},{4,5},{5,6},{6,7},{7,4},{8,9},{9,10},{10,1... | collective-permute-start | bytes 1572872 | tf_op jit(solution)/shard_map/ppermute | solution.py:480
  83.9 19.0 %collective-permute-start.6 = (f32[128,1024]{1,0:T(8,128)S(1)}, f32[128,1024]{1,0:T(8,128)S(1)}, u32[]{:S(2)}, u32[]{:S(2)}) collective-permute-start(f32[128,1024]{1,0:T(8,128)S(1)} %get-tuple-element.50), channel_id=1, source_target_pairs={{0,3},{1,0},{2,1},{3,2},{4,7},{5,4},{6,5},{7,6},{8,11},{9,8},{10,9... | collective-permute-start | bytes 1572872 | tf_op jit(solution)/shard_map/ppermute | solution.py:481

commit v8 on v7

--- a/solution.py
+++ b/solution.py
@@ -464,9 +464,13 @@
 
 
 def finish_kernel(ot_ref, st_ref, gt_ref, ob_ref, sb_ref, gb_ref, out_ref):
-    half = ot_ref.shape[0]
-    out_ref[:half, :] = (ot_ref[...] + st_ref[...] + gt_ref[...]).astype(BF16)
-    out_ref[half:, :] = (ob_ref[...] + sb_ref[...] + gb_ref[...]).astype(BF16)
+    @pl.when(pl.program_id(0) == 0)
+    def _():
+        out_ref[...] = (ot_ref[...] + st_ref[...] + gt_ref[...]).astype(BF16)
+
+    @pl.when(pl.program_id(0) == 1)
+    def _():
+        out_ref[...] = (ob_ref[...] + sb_ref[...] + gb_ref[...]).astype(BF16)
 
 
 def summed_output(local, mapped, states, gain, out_weight):
@@ -490,7 +494,9 @@
     own_top, own_bottom = one_tile(at(0), normed, out_weight, width)
     return pl.pallas_call(
         finish_kernel,
+        grid=(2,),
         in_specs=[resident()] * 6,
+        out_specs=pl.BlockSpec(own_top.shape, lambda i: (i, 0)),
         out_shape=jax.ShapeDtypeStruct((2 * own_top.shape[0], width), BF16),
         compiler_params=pltpu.CompilerParams(vmem_limit_bytes=57 << 20),
         name="finish",

time: 104 us -> 104 us (level)
  no operation moved by 1% of the time
where the time goes in v8:
time: 104 us
  waiting for transfers between devices  44.3 us (43%)
  Pallas kernels  39.9 us (38%)
  starting transfers between devices  19.6 us (19%)
    pallas_call x1, Pallas kernels, key_stage(): pl.pallas_call(body, grid=(heads // step,), in_specs=[pl.BlockSpec((tok,...  18.1 us
    ppermute x3, waiting for transfers between devices, summed_output(): up = lambda x: lax.ppermute(x, 'head', rise)  15.3 us
    all_to_all x1, waiting for transfers between devices, shards(): states = lax.all_to_all(states, 'ctx', 0, 0, axis_index_groups=groups)  10.2 us
    all_to_all x1, waiting for transfers between devices, shards(): mine = lax.all_to_all(pair, 'ctx', 0, 0, axis_index_groups=groups)  8.43 us
    pallas_call x1, Pallas kernels, query_stage(): pl.pallas_call(body, grid=(heads // step,), in_specs=[pl.BlockSpec((tok,...  8.2 us
    ppermute x3, waiting for transfers between devices, summed_output(): down = lambda x: lax.ppermute(x, 'head', fall)  5.87 us
    ppermute x3, starting transfers between devices, summed_output(): down = lambda x: lax.ppermute(x, 'head', fall)  5.12 us
    pallas_call x1, Pallas kernels, side_tiles(): pl.pallas_call(sides_kernel, grid_spec=pltpu.PrefetchScalarGridSpec(num_s...  4.99 us
  transfers between devices with their start and end apart: 9, of which 7 were waited for; matrix products, arithmetic and copies ran while one was open for 0% of the time, Pallas kernels for 15%

profile of v8, /device:TPU:128, one launch (start us, length us, event | category | flops | bytes accessed | tf_op | source)
XLA Modules:
  0.0 103.8 jit_solution(6809747557426694047)
XLA Ops:
  0.0 18.1 %key_stage.1 = (f32[8,136,256]{2,1,0:T(8,128)}, bf16[8,4,128,512]{3,2,1,0:T(8,128)(2,1)}, bf16[8,3,128,512]{3,2,1,0:T(8,128)(2,1)}, f32[8,32,128]{2,1,0:T(8,128)}) custom-call(bf16[256,2,1024]{2,1,0:T(2,128)(2,1)} %refs_1_.3, bf16[256,2,1024]{2,1,0:T(2,128)(2,1)} %refs_1_.2, f32[2,8,256]{2,1,0:T(8,128)} %refs_2_.1, f32[8,256]{1,0:T(8,128)} %refs_3_.1, ...), custom_call_target="tpu_custom_call" | custom-call | tf_op jit(solution)/shard_map/key_stage/pallas_call | solution.py:249
  18.1 4.3 %all-to-all-start = ((f32[8,136,256]{2,1,0:T(8,128)}), f32[8,136,256]{2,1,0:T(8,128)S(1)}, u32[]{:S(2)}, u32[]{:S(2)}) async-start(f32[8,136,256]{2,1,0:T(8,128)} %get-tuple-element.28), calls=%async_computation | async-start | bytes 2228224 | tf_op jit(solution)/shard_map/all_to_all | solution.py:514
  22.4 8.2 %query_stage.1 = (f32[256,1024]{1,0:T(8,128)}, f32[256,1024]{1,0:T(8,128)S(1)}) custom-call(bf16[256,1024]{1,0:T(8,128)(2,1)} %refs_0_.3, bf16[256,2,1024]{2,1,0:T(2,128)(2,1)} %refs_1_.3, bf16[8,4,128,512]{3,2,1,0:T(8,128)(2,1)} %get-tuple-element.29.refs_2_, bf16[8,3,128,512]{3,2,1,0:T(8,128)(2,1)} %get-tuple-element.30.refs_3_, ...), custom_call_target="tpu_custom_call" | custom-call | tf_op jit(solution)/shard_map/query_stage/pallas_call | solution.py:281
  30.6 8.4 %all-to-all-done.in_ref = f32[8,136,256]{2,1,0:T(8,128)S(1)} async-done(((f32[8,136,256]{2,1,0:T(8,128)}), f32[8,136,256]{2,1,0:T(8,128)S(1)}, u32[]{:S(2)}, u32[]{:S(2)}) %all-to-all-start) | async-done | bytes 1114144 | tf_op jit(solution)/shard_map/all_to_all | solution.py:514
  39.1 0.7 prefix_stage.1
  39.8 2.9 %collective-permute-start = (f32[136,128]{1,0:T(8,128)S(1)}, f32[136,128]{1,0:T(8,128)S(1)}, u32[]{:S(2)}, u32[]{:S(2)}) collective-permute-start(f32[136,128]{1,0:T(8,128)S(1)} %get-tuple-element.39), channel_id=1, source_target_pairs={{0,32},{4,36},{8,40},{12,44},{16,48},{20,52},{24,56},{28,60},{32,6... | collective-permute-start | bytes 208904 | tf_op jit(solution)/shard_map/ppermute | solution.py:525
  42.8 4.5 %collective-permute-done.end_ref = f32[136,128]{1,0:T(8,128)S(1)} collective-permute-done((f32[136,128]{1,0:T(8,128)S(1)}, f32[136,128]{1,0:T(8,128)S(1)}, u32[]{:S(2)}, u32[]{:S(2)}) %collective-permute-start) | collective-permute-done | bytes 69664 | tf_op jit(solution)/shard_map/ppermute | solution.py:525
  47.2 1.1 %incoming_stage.1 = f32[8,128,128]{2,1,0:T(8,128)} custom-call(f32[8,128]{1,0:T(8,128)S(1)} %get-tuple-element.37.ends_ref, f32[8,128,256]{2,1,0:T(8,128)S(1)} %get-tuple-element.38.ex_ref, f32[136,128]{1,0:T(8,128)S(1)} %collective-permute-done.end_ref), custom_call_target="tpu_custom_call" | custom-call | tf_op jit(solution)/shard_map/incoming_stage/pallas_call | solution.py:526
  48.4 3.5 %all-to-all-start.1 = ((f32[8,128,128]{2,1,0:T(8,128)}), f32[8,128,128]{2,1,0:T(8,128)S(1)}, u32[]{:S(2)}, u32[]{:S(2)}) async-start(f32[8,128,128]{2,1,0:T(8,128)} %incoming_stage.1), calls=%async_computation.1 | async-start | bytes 1048576 | tf_op jit(solution)/shard_map/all_to_all | solution.py:534
  51.9 10.2 %all-to-all-done.1.state_ref = f32[8,128,128]{2,1,0:T(8,128)S(1)} async-done(((f32[8,128,128]{2,1,0:T(8,128)}), f32[8,128,128]{2,1,0:T(8,128)S(1)}, u32[]{:S(2)}, u32[]{:S(2)}) %all-to-all-start.1) | async-done | bytes 524320 | tf_op jit(solution)/shard_map/all_to_all | solution.py:534
  62.1 3.4 %far_tile.1 = (bf16[256,1024]{1,0:T(8,128)(2,1)}, f32[128,1024]{1,0:T(8,128)S(1)}, f32[128,1024]{1,0:T(8,128)S(1)}) custom-call(s32[1]{0:T(128)} %bitcast.place_ref.pick_ref, f32[256,1024]{1,0:T(8,128)} %get-tuple-element.34.local_ref, f32[256,1024]{1,0:T(8,128)S(1)} %get-tuple-element.35.map_ref, f32[8,128,128]{2,1,0:T(8,128)S(1)} %all-to-all-done.1.state_ref, ...), custom_call_target="tpu_custom_call" | custom-call | tf_op jit(solution)/shard_map/far_tile/pallas_call | solution.py:376
  65.5 1.8 %collective-permute-start.2 = (f32[128,1024]{1,0:T(8,128)S(1)}, f32[128,1024]{1,0:T(8,128)S(1)}, u32[]{:S(2)}, u32[]{:S(2)}) collective-permute-start(f32[128,1024]{1,0:T(8,128)S(1)} %get-tuple-element.44), channel_id=1, source_target_pairs={{0,1},{1,2},{2,3},{3,0},{4,5},{5,6},{6,7},{7,4},{8,9},{9,10},{10,1... | collective-permute-start | bytes 1572872 | tf_op jit(solution)/shard_map/ppermute | solution.py:484
  67.4 1.7 %collective-permute-start.3 = (f32[128,1024]{1,0:T(8,128)S(1)}, f32[128,1024]{1,0:T(8,128)S(1)}, u32[]{:S(2)}, u32[]{:S(2)}) collective-permute-start(f32[128,1024]{1,0:T(8,128)S(1)} %get-tuple-element.46), channel_id=1, source_target_pairs={{0,3},{1,0},{2,1},{3,2},{4,7},{5,4},{6,5},{7,6},{8,11},{9,8},{10,9... | collective-permute-start | bytes 1572872 | tf_op jit(solution)/shard_map/ppermute | solution.py:485
  69.0 5.0 %side_tiles.1 = (f32[128,1024]{1,0:T(8,128)}, f32[128,1024]{1,0:T(8,128)}, f32[128,1024]{1,0:T(8,128)S(1)}, f32[128,1024]{1,0:T(8,128)S(1)}) custom-call(s32[1]{0:T(128)} %bitcast.place_ref.pick_ref, bf16[256,1024]{1,0:T(8,128)(2,1)} %get-tuple-element.40.normed_ref, bf16[1024,4096]{1,0:T(8,128)(2,1)} %last_w_ref.1, bf16[1024,4096]{1,0:T(8,128)(2,1)} %last_w_ref.1), custom_call_target="tpu_custom_call" | custom-call | tf_op jit(solution)/shard_map/side_tiles/pallas_call | solution.py:452
  74.0 1.8 %collective-permute-start.1 = (f32[128,1024]{1,0:T(8,128)}, f32[128,1024]{1,0:T(8,128)S(1)}, u32[]{:S(2)}, u32[]{:S(2)}) collective-permute-start(f32[128,1024]{1,0:T(8,128)} %get-tuple-element.42), channel_id=1, source_target_pairs={{0,3},{1,0},{2,1},{3,2},{4,7},{5,4},{6,5},{7,6},{8,11},{9,8},{10,9... | collective-permute-start | bytes 1572872 | tf_op jit(solution)/shard_map/ppermute | solution.py:485
  75.8 0.2 collective-permute-start.5
  76.0 5.7 %collective-permute-done.2.gt_ref = f32[128,1024]{1,0:T(8,128)S(1)} collective-permute-done((f32[128,1024]{1,0:T(8,128)S(1)}, f32[128,1024]{1,0:T(8,128)S(1)}, u32[]{:S(2)}, u32[]{:S(2)}) %collective-permute-start.2) | collective-permute-done | bytes 524320 | tf_op jit(solution)/shard_map/ppermute | solution.py:484
  81.8 0.4 collective-permute-done.3.gb_ref
  82.2 0.1 join_tiles.1
  82.3 1.7 %collective-permute-start.4 = (f32[128,1024]{1,0:T(8,128)S(1)}, f32[128,1024]{1,0:T(8,128)S(1)}, u32[]{:S(2)}, u32[]{:S(2)}) collective-permute-start(f32[128,1024]{1,0:T(8,128)S(1)} %get-tuple-element.47), channel_id=1, source_target_pairs={{0,1},{1,2},{2,3},{3,0},{4,5},{5,6},{6,7},{7,4},{8,9},{9,10},{10,1... | collective-permute-start | bytes 1572872 | tf_op jit(solution)/shard_map/ppermute | solution.py:484
  83.9 1.7 %collective-permute-start.6 = (f32[128,1024]{1,0:T(8,128)S(1)}, f32[128,1024]{1,0:T(8,128)S(1)}, u32[]{:S(2)}, u32[]{:S(2)}) collective-permute-start(f32[128,1024]{1,0:T(8,128)S(1)} %get-tuple-element.50), channel_id=1, source_target_pairs={{0,3},{1,0},{2,1},{3,2},{4,7},{5,4},{6,5},{7,6},{8,11},{9,8},{10,9... | collective-permute-start | bytes 1572872 | tf_op jit(solution)/shard_map/ppermute | solution.py:485
  85.6 2.3 %shard_map.82 = (f32[128,1024]{1,0:T(8,128)S(1)}, f32[128,1024]{1,0:T(8,128)S(1)}) custom-call(s32[1]{0:T(128)} %bitcast.place_ref.pick_ref, bf16[256,1024]{1,0:T(8,128)(2,1)} %get-tuple-element.40.normed_ref, bf16[1024,4096]{1,0:T(8,128)(2,1)} %last_w_ref.1), custom_call_target="tpu_custom_call" | custom-call | tf_op jit(solution)/shard_map/pallas_call | solution.py:425
  87.9 5.5 %collective-permute-done.1.st_ref = f32[128,1024]{1,0:T(8,128)S(1)} collective-permute-done((f32[128,1024]{1,0:T(8,128)}, f32[128,1024]{1,0:T(8,128)S(1)}, u32[]{:S(2)}, u32[]{:S(2)}) %collective-permute-start.1) | collective-permute-done | bytes 524320 | tf_op jit(solution)/shard_map/ppermute | solution.py:485
  93.4 0.0 collective-permute-done.5.sb_ref
  93.4 9.5 %collective-permute-done.4.gt_ref = f32[128,1024]{1,0:T(8,128)S(1)} collective-permute-done((f32[128,1024]{1,0:T(8,128)S(1)}, f32[128,1024]{1,0:T(8,128)S(1)}, u32[]{:S(2)}, u32[]{:S(2)}) %collective-permute-start.4) | collective-permute-done | bytes 524320 | tf_op jit(solution)/shard_map/ppermute | solution.py:484
  102.9 0.0 collective-permute-done.6.gb_ref
  102.9 0.9 finish.1
Async XLA Ops:
  18.1 20.9 %all-to-all-start = ((f32[8,136,256]{2,1,0:T(8,128)}), f32[8,136,256]{2,1,0:T(8,128)S(1)}, u32[]{:S(2)}, u32[]{:S(2)}) async-start(f32[8,136,256]{2,1,0:T(8,128)} %get-tuple-element.28), calls=%async_computation | async-start | bytes 2228224 | tf_op jit(solution)/shard_map/all_to_all | solution.py:514
  39.8 7.4 %collective-permute-start = (f32[136,128]{1,0:T(8,128)S(1)}, f32[136,128]{1,0:T(8,128)S(1)}, u32[]{:S(2)}, u32[]{:S(2)}) collective-permute-start(f32[136,128]{1,0:T(8,128)S(1)} %get-tuple-element.39), channel_id=1, source_target_pairs={{0,32},{4,36},{8,40},{12,44},{16,48},{20,52},{24,56},{28,60},{32,6... | collective-permute-start | bytes 208904 | tf_op jit(solution)/shard_map/ppermute | solution.py:525
  48.4 13.7 %all-to-all-start.1 = ((f32[8,128,128]{2,1,0:T(8,128)}), f32[8,128,128]{2,1,0:T(8,128)S(1)}, u32[]{:S(2)}, u32[]{:S(2)}) async-start(f32[8,128,128]{2,1,0:T(8,128)} %incoming_stage.1), calls=%async_computation.1 | async-start | bytes 1048576 | tf_op jit(solution)/shard_map/all_to_all | solution.py:534
  65.5 16.3 %collective-permute-start.2 = (f32[128,1024]{1,0:T(8,128)S(1)}, f32[128,1024]{1,0:T(8,128)S(1)}, u32[]{:S(2)}, u32[]{:S(2)}) collective-permute-start(f32[128,1024]{1,0:T(8,128)S(1)} %get-tuple-element.44), channel_id=1, source_target_pairs={{0,1},{1,2},{2,3},{3,0},{4,5},{5,6},{6,7},{7,4},{8,9},{9,10},{10,1... | collective-permute-start | bytes 1572872 | tf_op jit(solution)/shard_map/ppermute | solution.py:484
  67.4 14.8 %collective-permute-start.3 = (f32[128,1024]{1,0:T(8,128)S(1)}, f32[128,1024]{1,0:T(8,128)S(1)}, u32[]{:S(2)}, u32[]{:S(2)}) collective-permute-start(f32[128,1024]{1,0:T(8,128)S(1)} %get-tuple-element.46), channel_id=1, source_target_pairs={{0,3},{1,0},{2,1},{3,2},{4,7},{5,4},{6,5},{7,6},{8,11},{9,8},{10,9... | collective-permute-start | bytes 1572872 | tf_op jit(solution)/shard_map/ppermute | solution.py:485
  74.0 19.4 %collective-permute-start.1 = (f32[128,1024]{1,0:T(8,128)}, f32[128,1024]{1,0:T(8,128)S(1)}, u32[]{:S(2)}, u32[]{:S(2)}) collective-permute-start(f32[128,1024]{1,0:T(8,128)} %get-tuple-element.42), channel_id=1, source_target_pairs={{0,3},{1,0},{2,1},{3,2},{4,7},{5,4},{6,5},{7,6},{8,11},{9,8},{10,9... | collective-permute-start | bytes 1572872 | tf_op jit(solution)/shard_map/ppermute | solution.py:485
  75.8 17.6 %collective-permute-start.5 = (f32[128,1024]{1,0:T(8,128)}, f32[128,1024]{1,0:T(8,128)S(1)}, u32[]{:S(2)}, u32[]{:S(2)}) collective-permute-start(f32[128,1024]{1,0:T(8,128)} %get-tuple-element.49), channel_id=1, source_target_pairs={{0,1},{1,2},{2,3},{3,0},{4,5},{5,6},{6,7},{7,4},{8,9},{9,10},{10,1... | collective-permute-start | bytes 1572872 | tf_op jit(solution)/shard_map/ppermute | solution.py:484
  82.3 20.6 %collective-permute-start.4 = (f32[128,1024]{1,0:T(8,128)S(1)}, f32[128,1024]{1,0:T(8,128)S(1)}, u32[]{:S(2)}, u32[]{:S(2)}) collective-permute-start(f32[128,1024]{1,0:T(8,128)S(1)} %get-tuple-element.47), channel_id=1, source_target_pairs={{0,1},{1,2},{2,3},{3,0},{4,5},{5,6},{6,7},{7,4},{8,9},{9,10},{10,1... | collective-permute-start | bytes 1572872 | tf_op jit(solution)/shard_map/ppermute | solution.py:484
  83.9 19.0 %collective-permute-start.6 = (f32[128,1024]{1,0:T(8,128)S(1)}, f32[128,1024]{1,0:T(8,128)S(1)}, u32[]{:S(2)}, u32[]{:S(2)}) collective-permute-start(f32[128,1024]{1,0:T(8,128)S(1)} %get-tuple-element.50), channel_id=1, source_target_pairs={{0,3},{1,0},{2,1},{3,2},{4,7},{5,4},{6,5},{7,6},{8,11},{9,8},{10,9... | collective-permute-start | bytes 1572872 | tf_op jit(solution)/shard_map/ppermute | solution.py:485
